TPU v7x, 32 devices: a whole 2x2x4 slice. The times are simulated.
32 devices in a mesh: batch: 16 (over z, y, core), head: 2 (over x).
Axes of the slice: x: 2, y: 2, z: 4, core: 2. Of those that a mesh axis runs over, the one named last changes fastest.
Arguments:
- atoms: bfloat16 [16384, 512], P(('batch', 'head')), may hold values from -6 to 6
- pair: bfloat16 [64, 64, 256, 256], P('batch', 'head'), may hold values from -6 to 6
- counts: int32 [64], P('batch'), may hold values from 64 to 256, as said below
- qkv_weight: bfloat16 [3, 512, 512], P(None, 'batch', 'head'), may hold values from -0.25 to 0.25
- out_weight: bfloat16 [512, 512], P('batch', 'head'), may hold values from -2 to 2
- ln1_gain: float32 [512], P(('batch', 'head')), may hold values from 0.5 to 1.5
- ln2_gain: float32 [512], P(('batch', 'head')), may hold values from 0.5 to 1.5
- w_in: bfloat16 [512, 2048], P(('batch', 'head')), may hold values from -0.25 to 0.25
- w_out: bfloat16 [2048, 512], P(('batch', 'head')), may hold values from -0.125 to 0.125
- out_cot: bfloat16 [16384, 512], P(('batch', 'head')), may hold values from -6 to 6
- pair_cot: bfloat16 [64, 64, 256, 256], P('batch', 'head'), may hold values from -6 to 6
Outputs:
- output: bfloat16 [16384, 512], P(('batch', 'head'))
- new_pair: bfloat16 [64, 64, 256, 256], P('batch', 'head')
- atoms_grad: bfloat16 [16384, 512], P(('batch', 'head'))
- pair_grad: bfloat16 [64, 64, 256, 256], P('batch', 'head')
- qkv_weight_grad: float32 [3, 512, 512], P(None, 'batch', 'head')
- out_weight_grad: float32 [512, 512], P('batch', 'head')
- ln1_gain_grad: float32 [512], P(('batch', 'head'))
- ln2_gain_grad: float32 [512], P(('batch', 'head'))
- w_in_grad: float32 [512, 2048], P(('batch', 'head'))
- w_out_grad: float32 [2048, 512], P(('batch', 'head'))
Inputs may be any that keep to these rules, and one draw needn't show every extreme that they name: `counts`: atoms of each molecule; the first molecule has exactly 256.
All inputs are finite; a program needn't handle non-finite values.
Results may differ from a plain program's by a relative error of at most 0.03.
Values may be sent and summed in bfloat16 or wider, within the bound.
No kernel may reach another device: no remote copies, remote signals or barrier semaphores. Data moves between devices by JAX's collectives and lax.ppermute only.
A program may use at most 256 MiB of HBM per device.

v0:
```python
from functools import partial

import jax
import jax.numpy as jnp
from jax import lax
from jax.sharding import PartitionSpec as P


def layer_stats(values):
    center = values - jnp.mean(values, -1, keepdims=True)
    inverse = lax.rsqrt(jnp.mean(center * center, -1, keepdims=True) + 1e-05)
    return (center * inverse, inverse)


def norm_back(grad_norm, normed, inverse):
    return inverse * (
        grad_norm
        - jnp.mean(grad_norm, -1, keepdims=True)
        - normed * jnp.mean(grad_norm * normed, -1, keepdims=True)
    )


def times_transposed(left, right):
    return lax.dot_general(
        left, right, (((1,), (1,)), ((), ())), preferred_element_type=jnp.float32
    )


def transposed_times(left, right):
    return lax.dot_general(
        left, right, (((0,), (0,)), ((), ())), preferred_element_type=jnp.float32
    )


def block_masks(count_part, length):
    positions = jnp.arange(length, dtype=jnp.int32)
    valid_rows = positions[None, :] < count_part[:, None]
    both_valid = valid_rows[:, None, :, None] & valid_rows[:, None, None, :]
    return (valid_rows, both_valid)


def scores_of(query_part, key_part, pair_part, score_scale):
    raw = jnp.einsum("mqhd,mkhd->mhqk", query_part, key_part, preferred_element_type=jnp.float32)
    return raw * score_scale + pair_part.astype(jnp.float32)


def attend_forward(inputs, score_scale):
    query_part, key_part, value_part, pair_part, count_part = inputs
    valid_rows, both_valid = block_masks(count_part, query_part.shape[1])
    logits = scores_of(query_part, key_part, pair_part, score_scale)
    new_pair = jnp.where(both_valid, logits, 0.0).astype(jnp.bfloat16)
    masked = jnp.where(valid_rows[:, None, None, :], logits, -1e30)
    row_max = jnp.max(masked, -1, keepdims=True)
    exponent = jnp.exp(masked - row_max)
    row_total = jnp.sum(exponent, -1, keepdims=True)
    soft_weights = (exponent / row_total).astype(jnp.bfloat16)
    mixed = jnp.einsum(
        "mhqk,mkhd->mqhd", soft_weights, value_part, preferred_element_type=jnp.float32
    )
    mixed = jnp.where(valid_rows[:, :, None, None], mixed, 0.0).astype(jnp.bfloat16)
    return (new_pair, mixed, row_max[..., 0] + jnp.log(row_total[..., 0]))


def attend_backward(inputs, score_scale):
    query_part, key_part, value_part, pair_part, count_part, grad_mixed, log_total, cot_part = (
        inputs
    )
    valid_rows, both_valid = block_masks(count_part, query_part.shape[1])
    logits = scores_of(query_part, key_part, pair_part, score_scale)
    masked = jnp.where(valid_rows[:, None, None, :], logits, -1e30)
    soft = jnp.exp(masked - log_total[..., None])
    grad_masked = jnp.where(valid_rows[:, :, None, None], grad_mixed, jnp.zeros_like(grad_mixed))
    grad_soft = jnp.einsum(
        "mqhd,mkhd->mhqk", grad_masked, value_part, preferred_element_type=jnp.float32
    )
    grad_scores = soft * (grad_soft - jnp.sum(grad_soft * soft, -1, keepdims=True))
    grad_scores = (grad_scores + jnp.where(both_valid, cot_part.astype(jnp.float32), 0.0)).astype(
        jnp.bfloat16
    )
    grad_query = (
        jnp.einsum("mhqk,mkhd->mqhd", grad_scores, key_part, preferred_element_type=jnp.float32)
        * score_scale
    ).astype(jnp.bfloat16)
    grad_key = (
        jnp.einsum("mhqk,mqhd->mkhd", grad_scores, query_part, preferred_element_type=jnp.float32)
        * score_scale
    ).astype(jnp.bfloat16)
    grad_value = jnp.einsum(
        "mhqk,mqhd->mkhd",
        soft.astype(jnp.bfloat16),
        grad_masked,
        preferred_element_type=jnp.float32,
    ).astype(jnp.bfloat16)
    return (grad_scores, grad_query, grad_key, grad_value)


def body(
    atoms, pair, counts, qkv_weight, out_weight, ln1_gain, ln2_gain, w_in, w_out, out_cot, pair_cot
):
    mols_here, heads_here, length = (pair.shape[0], pair.shape[1], pair.shape[2])
    qkv_full, out_full = (
        lax.all_gather(qkv_weight, "batch", axis=1, tiled=True),
        lax.all_gather(out_weight, "batch", axis=0, tiled=True),
    )
    gain_one, gain_two, inner_weight, outer_weight = (
        lax.all_gather(ln1_gain.astype(jnp.bfloat16), ("batch", "head"), axis=0, tiled=True).astype(
            ln1_gain.dtype
        ),
        lax.all_gather(ln2_gain.astype(jnp.bfloat16), ("batch", "head"), axis=0, tiled=True).astype(
            ln2_gain.dtype
        ),
        lax.all_gather(w_in, ("batch", "head"), axis=0, tiled=True),
        lax.all_gather(w_out, ("batch", "head"), axis=0, tiled=True),
    )
    width_here = qkv_full.shape[2]
    head_size = width_here // heads_here
    score_scale = head_size ** (-0.5)
    blocks = mols_here // 2
    group_total = mols_here * length
    atoms_f = atoms.astype(jnp.float32)
    normed_one, inverse_one = layer_stats(atoms_f)
    hidden_one = (normed_one * gain_one).astype(jnp.bfloat16)
    group_rows = lax.all_gather(hidden_one, "head", axis=0, tiled=True)
    projected = jnp.einsum(
        "rd,sde->sre", group_rows, qkv_full, preferred_element_type=jnp.float32
    ).astype(jnp.bfloat16)

    def to_blocks(values):
        return values.reshape(blocks, 2, length, heads_here, head_size)

    query_all, key_all, value_all = (
        to_blocks(projected[0]),
        to_blocks(projected[1]),
        to_blocks(projected[2]),
    )
    pair_blocks = pair.reshape(blocks, 2, heads_here, length, length)
    count_blocks = counts.reshape(blocks, 2)
    new_pair, mixed, log_total = lax.map(
        partial(attend_forward, score_scale=score_scale),
        (query_all, key_all, value_all, pair_blocks, count_blocks),
    )
    mixed_flat = mixed.reshape(group_total, width_here)
    slab_rows = mixed_flat
    attention = lax.psum_scatter(
        times_transposed(slab_rows, out_full).astype(jnp.bfloat16),
        "head",
        scatter_dimension=0,
        tiled=True,
    ).astype(jnp.float32)
    first_sum = atoms_f + attention
    normed_two, inverse_two = layer_stats(first_sum)
    hidden_two = (normed_two * gain_two).astype(jnp.bfloat16)
    inner = jnp.dot(hidden_two, inner_weight, preferred_element_type=jnp.float32)
    gelu_value, gelu_pull = jax.vjp(jax.nn.gelu, inner)
    activated = gelu_value.astype(jnp.bfloat16)
    output = first_sum + jnp.dot(activated, outer_weight, preferred_element_type=jnp.float32)
    grad_outer_w = transposed_times(activated, out_cot)
    grad_act = times_transposed(out_cot, outer_weight)
    grad_inner = gelu_pull(grad_act)[0].astype(jnp.bfloat16)
    grad_inner_w = transposed_times(hidden_two, grad_inner)
    grad_hidden_two = times_transposed(grad_inner, inner_weight)
    grad_gain_two = jnp.sum(grad_hidden_two * normed_two, 0)
    grad_first = out_cot.astype(jnp.float32) + norm_back(
        grad_hidden_two * gain_two, normed_two, inverse_two
    )
    grad_attention = grad_first.astype(jnp.bfloat16)
    group_grad = lax.all_gather(grad_attention, "head", axis=0, tiled=True)
    grad_out_full = transposed_times(group_grad, mixed_flat)
    grad_mixed = jnp.dot(group_grad, out_full, preferred_element_type=jnp.float32).astype(
        jnp.bfloat16
    )
    cot_blocks = pair_cot.reshape(blocks, 2, heads_here, length, length)
    grad_scores, grad_query, grad_key, grad_value = lax.map(
        partial(attend_backward, score_scale=score_scale),
        (
            query_all,
            key_all,
            value_all,
            pair_blocks,
            count_blocks,
            to_blocks(grad_mixed),
            log_total,
            cot_blocks,
        ),
    )
    grad_projected = jnp.stack(
        [
            grad_query.reshape(group_total, width_here),
            grad_key.reshape(group_total, width_here),
            grad_value.reshape(group_total, width_here),
        ]
    )
    grad_qkv_full = jnp.einsum(
        "rd,sre->sde", group_rows, grad_projected, preferred_element_type=jnp.float32
    )
    slab_rows = grad_projected
    grad_hidden_one = lax.psum_scatter(
        jnp.einsum("sre,sde->rd", slab_rows, qkv_full, preferred_element_type=jnp.float32).astype(
            jnp.bfloat16
        ),
        "head",
        scatter_dimension=0,
        tiled=True,
    ).astype(jnp.float32)
    grad_gain_one = jnp.sum(grad_hidden_one * normed_one, 0)
    atoms_grad = grad_first + norm_back(grad_hidden_one * gain_one, normed_one, inverse_one)
    qkv_grad, out_grad = (
        lax.psum_scatter(
            grad_qkv_full.astype(jnp.bfloat16), "batch", scatter_dimension=1, tiled=True
        ).astype(jnp.float32),
        lax.psum_scatter(
            grad_out_full.astype(jnp.bfloat16), "batch", scatter_dimension=0, tiled=True
        ).astype(jnp.float32),
    )
    gain_one_grad, gain_two_grad, inner_grad, outer_grad = (
        lax.psum_scatter(grad_gain_one, ("batch", "head"), scatter_dimension=0, tiled=True),
        lax.psum_scatter(grad_gain_two, ("batch", "head"), scatter_dimension=0, tiled=True),
        lax.psum_scatter(grad_inner_w, ("batch", "head"), scatter_dimension=0, tiled=True),
        lax.psum_scatter(grad_outer_w, ("batch", "head"), scatter_dimension=0, tiled=True),
    )
    return (
        output.astype(jnp.bfloat16),
        new_pair.reshape(mols_here, heads_here, length, length),
        atoms_grad.astype(jnp.bfloat16),
        grad_scores.reshape(mols_here, heads_here, length, length),
        qkv_grad,
        out_grad,
        gain_one_grad,
        gain_two_grad,
        inner_grad,
        outer_grad,
    )


def solution(mesh):
    placed = (
        P(("batch", "head"), None),
        P("batch", "head", None, None),
        P("batch"),
        P(None, "batch", "head"),
        P("batch", "head"),
        P(("batch", "head")),
        P(("batch", "head")),
        P(("batch", "head"), None),
        P(("batch", "head"), None),
        P(("batch", "head"), None),
        P("batch", "head", None, None),
    )
    return jax.shard_map(
        body,
        mesh=mesh,
        in_specs=placed,
        out_specs=(
            P(("batch", "head"), None),
            P("batch", "head", None, None),
            P(("batch", "head"), None),
            P("batch", "head", None, None),
            P(None, "batch", "head"),
            P("batch", "head"),
            P(("batch", "head")),
            P(("batch", "head")),
            P(("batch", "head"), None),
            P(("batch", "head"), None),
        ),
        check_vma=False,
    )
```

profile of v0, /device:TPU:0, one launch (start us, length us, event | category | flops | bytes accessed | tf_op | source)
XLA Modules:
  0.0 1020.0 jit_solution(7663926731512702210)
XLA Ops:
  9.8 42.0 %all-reduce.6 = (bf16[512]{0:T(512)(128)(2,1)S(1)}, bf16[512]{0:T(512)(128)(2,1)}) all-reduce(bf16[512]{0:T(512)(128)(2,1)S(1)} %dynamic-update-slice, bf16[512]{0:T(512)(128)(2,1)S(1)} %dynamic-update-slice.1), channel_id=1, replica_groups=mesh['batch'=16,'head'=2] {'batch','head'}, use_global_device_ids=true, to_apply=%add | all-reduce | flops 1024 | bytes 4096
  57.9 21.3 %copy.79 = bf16[4,32,256,256]{2,3,1,0:T(8,128)(2,1)} copy(bf16[4,32,256,256]{3,2,1,0:T(8,128)(2,1)} %param.16) | data formatting | bytes 33554432 | tf_op args[1]
  79.1 23.4 %all_gather.27 = bf16[512,256]{1,0:T(8,128)(2,1)} all-gather(bf16[32,256]{1,0:T(8,128)(2,1)S(1)} %copy-done.37), channel_id=1, replica_groups=mesh['batch'=16,'head'=2] {'batch'}, dimensions={0}, use_global_device_ids=true | all-gather | bytes 278528 | tf_op jit(solution)/shard_map/all_gather | solution.py:103
  102.5 19.6 %all_gather.26 = bf16[3,512,256]{2,1,0:T(8,128)(2,1)S(1)} all-gather(bf16[3,32,256]{2,1,0:T(8,128)(2,1)S(1)} %copy-done.30), channel_id=1, replica_groups=mesh['batch'=16,'head'=2] {'batch'}, dimensions={1}, use_global_device_ids=true | all-gather | bytes 835584 | tf_op jit(solution)/shard_map/all_gather | solution.py:102
  130.2 6.5 broadcast.189.clone2
  136.7 111.9 %while.30 = (s32[]{:T(128)}, bf16[2,2,32,256,256]{4,3,2,1,0:T(8,128)(2,1)}, bf16[2,2,256,32,8]{2,1,0,4,3:T(2,128)(2,1)}, f32[2,2,32,256]{3,2,1,0:T(8,128)S(1)}, ...) while((s32[]{:T(128)}, ...), condition=%wide.region_5.6_spmd, body=%wide.region_2.5_spmd.sunk | while | flops 189121024 | bytes 175380800 | solution.py:138
  137.0 10.8 %select_reduce_fusion.2 = (f32[2,32,256]{2,1,0:T(8,128)S(1)}, f32[2,32,256,256]{2,3,1,0:T(8,128)}) fusion(pred[2,256]{1,0:T(4,128)(4,1)S(1)} %iota_compare_fusion.4, bf16[2,2,32,256,256]{3,4,2,1,0:T(8,128)(2,1)} %get-tuple-element.469, s32[]{:T(128)S(6)} %copy.164, bf16[2,2,256,32,8]{2,4,3,1,0:T(8,128)(2,1)S(1)} %get-tuple-element.468, ...), kind=kOutput, calls=%fused_computation.4.clone.1 | convolution fusion | flops 88064000 | bytes 25758208 | tf_op jit(solution)/shard_map/while/body/eval_jaxpr/mqhd,mkhd->mhqk/dot_general | solution.py:43
  147.8 9.8 fusion.164
  157.7 10.1 fusion.165
  167.7 4.4 fusion.163
  172.2 12.1 %copy.144 = bf16[1,2,32,256,256]{4,3,2,1,0:T(8,128)(2,1)} copy(bf16[1,2,32,256,256]{3,4,2,1,0:T(8,128)(2,1)} %fusion.163) | data formatting | bytes 16777216 | tf_op jit(solution)/shard_map/while/body/jit(dynamic_update_index_in_dim)/dynamic_update_slice | solution.py:138
  184.6 8.0 constant_dynamic-update-slice_fusion.4
  192.8 10.8 %select_reduce_fusion.2 = (f32[2,32,256]{2,1,0:T(8,128)S(1)}, f32[2,32,256,256]{2,3,1,0:T(8,128)}) fusion(pred[2,256]{1,0:T(4,128)(4,1)S(1)} %iota_compare_fusion.4, bf16[2,2,32,256,256]{3,4,2,1,0:T(8,128)(2,1)} %get-tuple-element.469, s32[]{:T(128)S(6)} %copy.164, bf16[2,2,256,32,8]{2,4,3,1,0:T(8,128)(2,1)S(1)} %get-tuple-element.468, ...), kind=kOutput, calls=%fused_computation.4.clone.1 | convolution fusion | flops 88064000 | bytes 25758208 | tf_op jit(solution)/shard_map/while/body/eval_jaxpr/mqhd,mkhd->mhqk/dot_general | solution.py:43
  203.6 9.8 fusion.164
  213.5 10.1 fusion.165
  223.6 4.4 fusion.163
  228.0 12.1 %copy.144 = bf16[1,2,32,256,256]{4,3,2,1,0:T(8,128)(2,1)} copy(bf16[1,2,32,256,256]{3,4,2,1,0:T(8,128)(2,1)} %fusion.163) | data formatting | bytes 16777216 | tf_op jit(solution)/shard_map/while/body/jit(dynamic_update_index_in_dim)/dynamic_update_slice | solution.py:138
  240.5 8.0 constant_dynamic-update-slice_fusion.4
  254.0 17.1 %reduce-scatter.6.cloned.1.call-done = bf16[512,512]{1,0:T(8,128)(2,1)} async-done(((bf16[1024,512]{1,0:T(8,128)(2,1)}), bf16[512,512]{1,0:T(8,128)(2,1)}) %reduce-scatter.6.cloned.1.call-update) | async-done | bytes 524304 | tf_op jit(solution)/shard_map/reduce_scatter | solution.py:144
  273.7 41.1 %all-gather.9.cloned.1.call-done = bf16[2048,512]{1,0:T(8,128)(2,1)} async-done(((bf16[64,512]{1,0:T(8,128)(2,1)}), bf16[2048,512]{1,0:T(8,128)(2,1)}) %all-gather.9.cloned.1.call-update) | async-done | bytes 2097168 | tf_op jit(solution)/shard_map/all_gather | solution.py:113
  314.8 4.9 fusion.117
  319.7 54.0 %all-gather.7.cloned.1.call-done = bf16[512,2048]{1,0:T(8,128)(2,1)} async-done(((bf16[16,2048]{1,0:T(8,128)(2,1)}), bf16[512,2048]{1,0:T(8,128)(2,1)}) %all-gather.7.cloned.1.call-update) | async-done | bytes 2097168 | tf_op jit(solution)/shard_map/all_gather | solution.py:112
  373.7 7.7 fusion.88
  385.3 21.3 %copy.88 = bf16[4,32,256,256]{2,3,1,0:T(8,128)(2,1)} copy(bf16[4,32,256,256]{3,2,1,0:T(8,128)(2,1)} %param.25) | data formatting | bytes 33554432 | tf_op args[10]
  411.1 6.1 broadcast.189.clone
  417.1 127.7 %while.31 = (s32[]{:T(128)}, bf16[2,2,32,256,256]{4,3,2,1,0:T(8,128)(2,1)}, bf16[2,2,256,32,8]{2,1,0,4,3:T(2,128)(2,1)}, bf16[2,2,256,32,8]{2,1,0,4,3:T(2,128)(2...) while((s32[]{:T(128)}, ...), condition=%wide.region_13.14_spmd, body=%wide.region_11.13_spmd.sunk | while | flops 458375936 | bytes 253173536 | solution.py:173
  417.8 7.9 fusion.181
  425.7 5.7 copy-done.1
  433.7 19.2 %fusion.182 = bf16[2,32,256,256]{2,3,1,0:T(8,128)(2,1)} fusion(f32[2,32,256,256]{2,3,1,0:T(8,128)} %copy-done.1, bf16[2,2,32,256,256]{3,4,2,1,0:T(8,128)(2,1)} %get-tuple-element.512, s32[]{:T(128)S(6)} %copy.177, pred[2,256,256]{1,2,0:T(8,128)(4,1)S(1)} %broadcast_and_fusion.5, bf16[2,2,256,32,8]{2,4,3,1,0:T(8,128)(2,1)} %get-tuple-element.511, ...), kind=kOutput, calls=%fused_computation.30.clone.1 | convolution fusion | flops 163856640 | bytes 51514880 | tf_op jit(solution)/shard_map/while/body/eval_jaxpr/sub | solution.py:76
  452.9 5.9 fusion.185
  461.2 12.0 %copy.150 = bf16[1,2,32,256,256]{4,3,2,1,0:T(8,128)(2,1)} copy(bf16[1,2,32,256,256]{3,4,2,1,0:T(8,128)(2,1)} %bitcast.181) | data formatting | bytes 16777216 | tf_op jit(solution)/shard_map/while/body/jit(dynamic_update_index_in_dim)/dynamic_update_slice | solution.py:138
  473.2 7.8 constant_dynamic-update-slice_fusion.5
  481.4 7.9 fusion.181
  489.3 5.7 copy-done.1
  497.3 19.2 %fusion.182 = bf16[2,32,256,256]{2,3,1,0:T(8,128)(2,1)} fusion(f32[2,32,256,256]{2,3,1,0:T(8,128)} %copy-done.1, bf16[2,2,32,256,256]{3,4,2,1,0:T(8,128)(2,1)} %get-tuple-element.512, s32[]{:T(128)S(6)} %copy.177, pred[2,256,256]{1,2,0:T(8,128)(4,1)S(1)} %broadcast_and_fusion.5, bf16[2,2,256,32,8]{2,4,3,1,0:T(8,128)(2,1)} %get-tuple-element.511, ...), kind=kOutput, calls=%fused_computation.30.clone.1 | convolution fusion | flops 163856640 | bytes 51514880 | tf_op jit(solution)/shard_map/while/body/eval_jaxpr/sub | solution.py:76
  516.6 5.9 fusion.185
  524.8 12.0 %copy.150 = bf16[1,2,32,256,256]{4,3,2,1,0:T(8,128)(2,1)} copy(bf16[1,2,32,256,256]{3,4,2,1,0:T(8,128)(2,1)} %bitcast.181) | data formatting | bytes 16777216 | tf_op jit(solution)/shard_map/while/body/jit(dynamic_update_index_in_dim)/dynamic_update_slice | solution.py:138
  536.8 7.8 constant_dynamic-update-slice_fusion.5
  553.9 3.4 bitcast_convert_fusion
  557.4 6.0 fusion.114
  565.3 3.4 fusion.110
  570.1 5.3 fusion.94
  575.4 69.7 %all-reduce.9.cloned.1.call-done = bf16[3,512,256]{2,0,1:T(4,128)(2,1)} async-done(((bf16[3,512,256]{2,0,1:T(4,128)(2,1)}), bf16[3,512,256]{2,0,1:T(4,128)(2,1)}) %all-reduce.9.cloned.1.call-update) | async-done | bytes 786448
  646.6 56.9 %reduce-scatter.10.cloned.1.call-done = bf16[32,256]{1,0:T(8,128)(2,1)} async-done(((bf16[512,256]{1,0:T(8,128)(2,1)}), bf16[32,256]{1,0:T(8,128)(2,1)}) %reduce-scatter.10.cloned.1.call-update) | async-done | bytes 16400 | tf_op jit(solution)/shard_map/reduce_scatter | solution.py:211
  704.8 20.2 %reduce-scatter.8.cloned.1.call-done = bf16[512,512]{1,0:T(8,128)(2,1)} async-done(((bf16[1024,512]{1,0:T(8,128)(2,1)}), bf16[512,512]{1,0:T(8,128)(2,1)}) %reduce-scatter.8.cloned.1.call-update) | async-done | bytes 524304 | tf_op jit(solution)/shard_map/reduce_scatter | solution.py:197
  726.7 40.3 %all-reduce.5 = (f32[512]{0:T(512)S(1)}, f32[512]{0:T(512)S(1)}) all-reduce(f32[512]{0:T(512)S(1)} %get-tuple-element.234, f32[512]{0:T(512)S(1)} %copy-done.38), channel_id=6, replica_groups=mesh['batch'=16,'head'=2] {'batch','head'}, use_global_device_ids=true, to_apply=%region_20.21.clone | all-reduce | flops 1024 | bytes 8192
  770.4 99.6 %reduce-scatter.14.cloned.1.call-done = f32[64,512]{1,0:T(8,128)} async-done(((f32[2048,512]{1,0:T(8,128)}), f32[64,512]{1,0:T(8,128)}) %reduce-scatter.14.cloned.1.call-update) | async-done | bytes 131088 | tf_op jit(solution)/shard_map/reduce_scatter | solution.py:219
  870.1 142.1 %reduce-scatter.12.cloned.1.call-done = f32[16,2048]{1,0:T(8,128)} async-done(((f32[512,2048]{1,0:T(8,128)}), f32[16,2048]{1,0:T(8,128)}) %reduce-scatter.12.cloned.1.call-update) | async-done | bytes 131088 | tf_op jit(solution)/shard_map/reduce_scatter | solution.py:218
  (225 shorter events, 62.9 us)
Async XLA Ops:
  8.0 114.1 %all-gather.5.cloned.1.call-start = ((), (), s32[]{:S(2)}) async-start(), calls=%async_computation.5 | async-start | bytes 1572864 | tf_op jit(solution)/shard_map/all_gather | solution.py:123
  57.1 214.0 %reduce-scatter.6.cloned.1.call-start = ((), (), s32[]{:S(2)}) async-start(), calls=%async_computation.6 | async-start | bytes 1572864 | tf_op jit(solution)/shard_map/reduce_scatter | solution.py:144
  57.9 21.3 %copy-start.37 = (bf16[32,256]{1,0:T(8,128)(2,1)S(1)}, bf16[32,256]{1,0:T(8,128)(2,1)}, u32[]{:S(2)}) copy-start(bf16[32,256]{1,0:T(8,128)(2,1)} %param.19) | copy-start | bytes 49156
  57.9 44.7 %copy-start.30 = (bf16[3,32,256]{2,1,0:T(8,128)(2,1)S(1)}, bf16[3,32,256]{2,1,0:T(8,128)(2,1)}, u32[]{:S(2)}) copy-start(bf16[3,32,256]{2,1,0:T(8,128)(2,1)} %param.18) | copy-start | bytes 147460
  136.7 117.2 %copy-start.39 = (bf16[512]{0:T(512)(128)(2,1)S(1)}, bf16[512]{0:T(512)(128)(2,1)}, u32[]{:S(2)}) copy-start(bf16[512]{0:T(512)(128)(2,1)} %get-tuple-element.285) | copy-start | bytes 3076
  147.8 19.9 %slice-start = ((s8[16777216]{0:T(1024)(128)(4,1)}), s8[4194304]{0:T(1024)(128)(4,1)S(1)}, s32[]{:S(2)}) async-start(s8[16777216]{0:T(1024)(128)(4,1)} %bitcast.179), calls=%async_computation.15 | async-start | bytes 8388608 | tf_op jit(solution)/shard_map/while
  157.6 10.1 slice-start.1
  157.6 10.1 slice-start.2
  157.6 10.1 slice-start.3
  172.2 12.1 %copy-start.6 = (bf16[1,2,256,32,8]{2,4,3,1,0:T(8,128)(2,1)S(1)}, bf16[1,2,256,32,8]{2,4,3,1,0:T(8,128)(2,1)}, u32[]{:S(2)}) copy-start(bf16[1,2,256,32,8]{2,4,3,1,0:T(8,128)(2,1)} %fusion.165) | copy-start | bytes 786436 | tf_op jit(solution)/shard_map/while
  172.2 12.1 %copy-start.17 = (bf16[2,2,256,32,8]{2,1,0,4,3:T(2,128)(2,1)S(1)}, bf16[2,2,256,32,8]{2,1,0,4,3:T(2,128)(2,1)}, u32[]{:S(2)}) copy-start(bf16[2,2,256,32,8]{2,1,0,4,3:T(2,128)(2,1)} %get-tuple-element.454) | copy-start | bytes 1572868 | tf_op jit(solution)/shard_map/while
  184.6 8.0 copy-start.18
  203.6 19.9 %slice-start = ((s8[16777216]{0:T(1024)(128)(4,1)}), s8[4194304]{0:T(1024)(128)(4,1)S(1)}, s32[]{:S(2)}) async-start(s8[16777216]{0:T(1024)(128)(4,1)} %bitcast.179), calls=%async_computation.15 | async-start | bytes 8388608 | tf_op jit(solution)/shard_map/while
  213.5 10.1 slice-start.1
  213.5 10.1 slice-start.2
  213.5 10.1 slice-start.3
  228.0 12.1 %copy-start.6 = (bf16[1,2,256,32,8]{2,4,3,1,0:T(8,128)(2,1)S(1)}, bf16[1,2,256,32,8]{2,4,3,1,0:T(8,128)(2,1)}, u32[]{:S(2)}) copy-start(bf16[1,2,256,32,8]{2,4,3,1,0:T(8,128)(2,1)} %fusion.165) | copy-start | bytes 786436 | tf_op jit(solution)/shard_map/while
  228.0 12.1 %copy-start.17 = (bf16[2,2,256,32,8]{2,1,0,4,3:T(2,128)(2,1)S(1)}, bf16[2,2,256,32,8]{2,1,0,4,3:T(2,128)(2,1)}, u32[]{:S(2)}) copy-start(bf16[2,2,256,32,8]{2,1,0,4,3:T(2,128)(2,1)} %get-tuple-element.454) | copy-start | bytes 1572868 | tf_op jit(solution)/shard_map/while
  240.5 8.0 copy-start.18
  248.6 22.5 %copy-start.2 = (bf16[512,512]{1,0:T(8,128)(2,1)S(1)}, bf16[512,512]{1,0:T(8,128)(2,1)}, u32[]{:S(2)}) copy-start(bf16[512,512]{1,0:T(8,128)(2,1)} %param.15) | copy-start | bytes 1572868
  248.6 66.2 %copy-start.8 = (bf16[512,512]{1,0:T(8,128)(2,1)S(1)}, bf16[512,512]{1,0:T(8,128)(2,1)}, u32[]{:S(2)}) copy-start(bf16[512,512]{1,0:T(8,128)(2,1)} %param.24) | copy-start | bytes 1572868
  250.1 23.6 %copy-start.13 = (bf16[1024,256]{0,1:T(8,128)(2,1)}, bf16[1024,256]{0,1:T(8,128)(2,1)S(1)}, u32[]{:S(2)}) copy-start(bf16[1024,256]{0,1:T(8,128)(2,1)S(1)} %reshape.239) | copy-start | bytes 1572868
  252.8 62.1 %all-gather.9.cloned.1.call-start = ((), (), s32[]{:S(2)}) async-start(), calls=%async_computation.8 | async-start | bytes 2162688 | tf_op jit(solution)/shard_map/all_gather | solution.py:113
  253.3 120.4 %all-gather.7.cloned.1.call-start = ((), (), s32[]{:S(2)}) async-start(), calls=%async_computation.7 | async-start | bytes 2162688 | tf_op jit(solution)/shard_map/all_gather | solution.py:112
  253.9 152.7 %all-gather.11.cloned.1.call-start = ((), (), s32[]{:S(2)}) async-start(), calls=%async_computation.9 | async-start | bytes 1572864 | tf_op jit(solution)/shard_map/all_gather | solution.py:167
  254.0 129.5 %copy-start.24 = (f32[512]{0:T(512)}, f32[512]{0:T(512)S(1)}, u32[]{:S(2)}) copy-start(f32[512]{0:T(512)S(1)} %convert_element_type.138) | copy-start | bytes 6148
  272.4 111.1 %copy-start.26 = (f32[512]{0:T(512)}, f32[512]{0:T(512)S(1)}, u32[]{:S(2)}) copy-start(f32[512]{0:T(512)S(1)} %broadcast_multiply_fusion.4) | copy-start | bytes 6148
  273.7 109.8 %copy-start.31 = (f32[512]{0:T(512)}, f32[512]{0:T(512)S(1)}, u32[]{:S(2)}) copy-start(f32[512]{0:T(512)S(1)} %add_rsqrt_fusion) | copy-start | bytes 6148
  273.7 100.0 %copy-start.4 = (bf16[512,512]{1,0:T(8,128)(2,1)S(1)}, bf16[512,512]{1,0:T(8,128)(2,1)}, u32[]{:S(2)}) copy-start(bf16[512,512]{1,0:T(8,128)(2,1)} %reduce-scatter.6.cloned.1.call-done) | copy-start | bytes 1572868
  373.7 7.7 copy-start.40
  385.2 21.4 %copy-start.10 = (bf16[512,256]{1,0:T(8,128)(2,1)S(1)}, bf16[512,256]{1,0:T(8,128)(2,1)}, u32[]{:S(2)}) copy-start(bf16[512,256]{1,0:T(8,128)(2,1)} %all_gather.27) | copy-start | bytes 786436
  385.2 259.8 %all-reduce.9.cloned.1.call-start = ((), (), s32[]{:S(2)}) async-start(), calls=%async_computation.14 | async-start | bytes 2097152
  425.7 5.7 copy-start.1
  452.9 5.9 copy-start
  489.3 5.7 copy-start.1
  516.5 5.9 copy-start
  548.6 4.0 copy-start.14
  548.6 4.0 copy-start.19
  552.5 150.9 %reduce-scatter.10.cloned.1.call-start = ((), (), s32[]{:S(2)}) async-start(), calls=%async_computation.11 | async-start | bytes 278528 | tf_op jit(solution)/shard_map/reduce_scatter | solution.py:211
  553.8 171.2 %reduce-scatter.8.cloned.1.call-start = ((), (), s32[]{:S(2)}) async-start(), calls=%async_computation.10 | async-start | bytes 1572864 | tf_op jit(solution)/shard_map/reduce_scatter | solution.py:197
  557.3 312.7 %reduce-scatter.14.cloned.1.call-start = ((), (), s32[]{:S(2)}) async-start(), calls=%async_computation.13 | async-start | bytes 4325376 | tf_op jit(solution)/shard_map/reduce_scatter | solution.py:219
  563.4 5.4 copy-start.41
  563.5 448.7 %reduce-scatter.12.cloned.1.call-start = ((), (), s32[]{:S(2)}) async-start(), calls=%async_computation.12 | async-start | bytes 4325376 | tf_op jit(solution)/shard_map/reduce_scatter | solution.py:218
  570.1 154.9 %copy-start.29 = (f32[512]{0:T(512)S(1)}, f32[512]{0:T(512)}, u32[]{:S(2)}) copy-start(f32[512]{0:T(512)} %copy-done.28) | copy-start | bytes 6148
  570.1 154.9 %copy-start.34 = (f32[512]{0:T(512)S(1)}, f32[512]{0:T(512)}, u32[]{:S(2)}) copy-start(f32[512]{0:T(512)} %copy-done.33) | copy-start | bytes 6148
  570.1 154.9 %copy-start.36 = (f32[512]{0:T(512)S(1)}, f32[512]{0:T(512)}, u32[]{:S(2)}) copy-start(f32[512]{0:T(512)} %copy-done.35) | copy-start | bytes 6148
  570.1 156.6 %copy-start.38 = (f32[512]{0:T(512)S(1)}, f32[512]{0:T(512)}, u32[]{:S(2)}) copy-start(f32[512]{0:T(512)} %get-tuple-element.232) | copy-start | bytes 6148
  570.1 198.1 %copy-start.7 = (f32[512,512]{1,0:T(8,128)S(1)}, f32[512,512]{1,0:T(8,128)}, u32[]{:S(2)}) copy-start(f32[512,512]{1,0:T(8,128)} %get-tuple-element.287) | copy-start | bytes 3145732
  (19 other events, 32.4 us)
Sparse Core Ops, SparseCore 0:
  57.2 21.3 all-gather.4
  252.9 18.1 reduce-scatter.5
  385.3 20.1 all-gather.10
  552.7 92.3 all-reduce.8
  648.8 54.5 reduce-scatter.9
  705.6 19.3 reduce-scatter.7
  727.8 142.1 reduce-scatter.13
  872.9 139.1 reduce-scatter.11
Sparse Core Ops, SparseCore 1:
  256.3 58.5 all-gather.8
  318.3 55.4 all-gather.6
where the time goes:
time: 1030 us; the launch traced here: 1020 us
  waiting for transfers between devices  502 us (49%)
  local copies, waits for them, and re-layouts  171 us (17%)
  matrix products  158 us (15%)
  blocking collectives  125 us (12%)
  other arithmetic  45.7 us (4%)
  between operations  17.2 us (2%)
    reduce_scatter x1, waiting for transfers between devices, body(): lax.psum_scatter(grad_inner_w, ('batch', 'head'), scatter_dimension=0, ti...  142 us
    reduce_scatter x1, waiting for transfers between devices, body(): lax.psum_scatter(grad_outer_w, ('batch', 'head'), scatter_dimension=0, ti...  99.6 us
    dynamic_update_slice x14, local copies, waits for them, and re-layouts, body(): lax.map(partial(attend_forward, score_scale=score_scale), (query_all, key...  82.5 us
    unnamed x2, blocking collectives  82.3 us
    unnamed x11, waiting for transfers between devices  70.9 us
    reduce_scatter x1, waiting for transfers between devices, body(): lax.psum_scatter(grad_out_full.astype(jnp.bfloat16), 'batch', scatter_dim...  56.9 us
    all_gather x1, waiting for transfers between devices, body(): lax.all_gather(w_in, ('batch', 'head'), axis=0, tiled=True)  54 us
    unnamed x80, local copies, waits for them, and re-layouts  48.8 us
  transfers between devices with their start and end apart: 10, of which 8 were waited for; matrix products, arithmetic and copies ran while one was open for 8% of the time, Pallas kernels for 0%

commit v1 on v0

--- a/solution.py
+++ b/solution.py
@@ -2,8 +2,16 @@
 
 import jax
 import jax.numpy as jnp
+import numpy as np
 from jax import lax
+from jax.experimental import pallas as pl
+from jax.experimental.pallas import tpu as pltpu
 from jax.sharding import PartitionSpec as P
+
+F32 = jnp.float32
+BF16 = jnp.bfloat16
+NEG = -1e30
+BOTH = ("batch", "head")
 
 
 def layer_stats(values):
@@ -94,7 +102,7 @@
     return (grad_scores, grad_query, grad_key, grad_value)
 
 
-def body(
+def body_native(
     atoms, pair, counts, qkv_weight, out_weight, ln1_gain, ln2_gain, w_in, w_out, out_cot, pair_cot
 ):
     mols_here, heads_here, length = (pair.shape[0], pair.shape[1], pair.shape[2])
@@ -232,35 +240,679 @@
     )
 
 
+def dot(left, right):
+    return jnp.dot(left, right, preferred_element_type=F32)
+
+
+def dot_nt(left, right):
+    return lax.dot_general(left, right, (((1,), (1,)), ((), ())), preferred_element_type=F32)
+
+
+def dot_tn(left, right):
+    return lax.dot_general(left, right, (((0,), (0,)), ((), ())), preferred_element_type=F32)
+
+
+def swap(values, axes, count, bit):
+    return lax.ppermute(values, axes, [(i, i ^ bit) for i in range(count)])
+
+
+def relative(position, bits):
+    return sum(((position >> k) & 1) * bit for k, bit in enumerate(bits))
+
+
+def whole(shape):
+    return pl.BlockSpec(shape, lambda *_: (0,) * len(shape))
+
+
+def prep_kernel(me_ref, near_ref, far_ref, w_ref, gains_ref, rows_s, *, bits, heads_bits, shard):
+    b, h = me_ref[0], me_ref[1]
+    half = near_ref.shape[0]
+    rows = w_ref.shape[1] // (2 * half)
+    dim = gains_ref.shape[1]
+    for p in range(2 * half):
+        ref, q = (near_ref, p) if p < half else (far_ref, p - half)
+        at = pl.multiple_of((b ^ relative(p, bits)) * rows, rows)
+        for s in range(3):
+            w_ref[s, pl.ds(at, rows), :] = ref[q, s * rows : (s + 1) * rows, :]
+        rows_s[p : p + 1, :] = ref[q, 3 * rows : 3 * rows + 1, :].astype(F32)
+    lanes = rows_s.shape[1]
+    count = 2 * half
+    lane = lax.broadcasted_iota(jnp.int32, (lanes, dim), 0)
+    col = lax.broadcasted_iota(jnp.int32, (lanes, dim), 1)
+    block = lax.broadcasted_iota(jnp.int32, (count, dim), 1) // rows
+    place = lax.broadcasted_iota(jnp.int32, (count, dim), 0)
+    owner = sum(((place >> k) & 1) * bit for k, bit in enumerate(bits)) ^ b
+    values = rows_s[...].astype(BF16)
+    for g in range(2):
+        start = (((col // shard) & 1) ^ h) * (4 * shard) + g * 2 * shard + lax.rem(col, shard)
+        pick = jnp.where((lane == start) | (lane == start + shard), 1.0, 0.0).astype(BF16)
+        spread = dot(values, pick)
+        gains_ref[g : g + 1, :] = jnp.sum(jnp.where(owner == block, spread, 0.0), 0, keepdims=True)
+
+
+def attend_forward_kernel(
+    mol_ref, cnt_ref, atoms_ref, w_ref, gains_ref, mask_ref, pair_ref, *rest,
+    hb, groups, scale, carried
+):
+    new_ref, exp_ref, hid_t_ref, qkv_ref, mixed_ref, inv_ref, q_s, kt_s, v_s, sum_s = rest[carried:]
+    step = pl.program_id(1)
+    length = atoms_ref.shape[0]
+    lanes = w_ref.shape[2] // groups
+    per_group = lanes // (8 * hb)
+    count = cnt_ref[mol_ref[pl.program_id(0)]]
+
+    @pl.when(step == 0)
+    def _():
+        values = atoms_ref[...].astype(F32)
+        center = values - jnp.mean(values, -1, keepdims=True)
+        inverse = lax.rsqrt(jnp.mean(center * center, -1, keepdims=True) + 1e-05)
+        hidden = (center * inverse * gains_ref[0:1, :]).astype(BF16)
+        hid_t_ref[...] = hidden.T
+        query = (dot(hidden, w_ref[0]) * scale).astype(BF16)
+        key = dot(hidden, w_ref[1]).astype(BF16)
+        value = dot(hidden, w_ref[2]).astype(BF16)
+        qkv_ref[0] = query
+        qkv_ref[1] = key
+        qkv_ref[2] = value
+        key_t = key.T
+        at = lax.broadcasted_iota(jnp.int32, (1, length), 1)
+        bias = jnp.where(at < count, 0.0, NEG)
+        first = lax.broadcasted_iota(jnp.int32, (lanes, length), 0) == 0
+        bias_rows = jnp.where(first, bias, 0.0).astype(BF16)
+        ones_lane = (lax.broadcasted_iota(jnp.int32, (length, lanes), 1) == 0).astype(F32).astype(BF16)
+        for g in range(groups):
+            part = slice(g * lanes, (g + 1) * lanes)
+            q_s[g, :, :lanes] = query[:, part]
+            q_s[g, :, lanes:] = ones_lane
+            kt_s[g, :lanes, :] = key_t[part]
+            kt_s[g, lanes:, :] = bias_rows
+            v_s[g, :, :lanes] = value[:, part]
+            v_s[g, :, lanes:] = jnp.ones((length, lanes), BF16)
+
+    g = step // per_group
+    block = lax.rem(step, per_group)
+    valid = (lax.broadcasted_iota(jnp.int32, (length, length), 0) < count) & (
+        lax.broadcasted_iota(jnp.int32, (length, length), 1) < count
+    )
+    total = jnp.zeros((length, 2 * lanes), F32)
+    for i in range(hb):
+        logits = dot(q_s[g] * mask_ref[0, block, i : i + 1, :], kt_s[g]) + pair_ref[0, i].astype(F32)
+        new_ref[0, i] = jnp.where(valid, logits, 0.0).astype(BF16)
+        exp_ref[0, i] = jnp.exp(logits - jnp.max(logits, -1, keepdims=True)).astype(BF16)
+        total = total + dot(exp_ref[0, i], v_s[g] * mask_ref[1, block, i : i + 1, :])
+
+    @pl.when(block == 0)
+    def _():
+        sum_s[...] = total
+
+    @pl.when(block > 0)
+    def _():
+        sum_s[...] = sum_s[...] + total
+
+    @pl.when(block == per_group - 1)
+    def _():
+        inverse = 1.0 / sum_s[:, lanes:]
+        rows_ok = lax.broadcasted_iota(jnp.int32, (length, lanes), 0) < count
+        at = pl.ds(pl.multiple_of(g * lanes, lanes), lanes)
+        inv_ref[:, at] = inverse
+        mixed_ref[:, at] = jnp.where(rows_ok, sum_s[:, :lanes] * inverse, 0.0).astype(BF16)
+
+
+def head_masks(groups, width, hb, backward):
+    lanes = width // groups
+    heads = lanes // 8
+    masks = np.zeros((2, heads, 2 * lanes), np.float32)
+    for h in range(heads):
+        own = slice(h * 8, (h + 1) * 8)
+        twin = slice(lanes + h * 8, lanes + (h + 1) * 8)
+        masks[0, h, own] = 1
+        masks[1, h, own] = 1
+        if backward:
+            masks[0, h, twin] = 1
+        else:
+            masks[0, h, lanes] = 1
+            masks[1, h, twin] = 1
+    return jnp.asarray(masks.reshape(2, heads // hb, hb, 2 * lanes), BF16)
+
+
+def specs_of(length, hb):
+    pair = pl.BlockSpec((1, hb, length, length), lambda i, j, mol, cnt: (mol[i], j, 0, 0))
+    rows = lambda cols: pl.BlockSpec((length, cols), lambda i, j, mol, cnt: (i, 0))
+    three = lambda cols: pl.BlockSpec((3, length, cols), lambda i, j, mol, cnt: (0, i, 0))
+    return pair, rows, three
+
+
+ANY = pl.BlockSpec(memory_space=pl.ANY)
+
+
+def attend_forward_call(mols, counts, atoms, weights, gains, pair, carried, hb=16):
+    n, (_, heads, length, _) = mols.shape[0], pair.shape
+    dim, width = atoms.shape[1], weights.shape[2]
+    groups = max(1, width // 128)
+    lanes = width // groups
+    masks = head_masks(groups, width, hb, False)
+    pair_spec, rows, three = specs_of(length, hb)
+    args = [atoms, weights, gains, masks, pair, *carried]
+    spec = pltpu.PrefetchScalarGridSpec(
+        num_scalar_prefetch=2,
+        grid=(n, heads // hb),
+        in_specs=[rows(dim), whole(weights.shape), whole(gains.shape), whole(masks.shape), pair_spec]
+        + [ANY] * len(carried),
+        out_specs=[
+            pair_spec,
+            pair_spec,
+            pl.BlockSpec((dim, length), lambda i, j, mol, cnt: (0, i)),
+            three(width),
+            rows(width),
+            rows(width),
+        ],
+        scratch_shapes=[
+            pltpu.VMEM((groups, length, 2 * lanes), BF16),
+            pltpu.VMEM((groups, 2 * lanes, length), BF16),
+            pltpu.VMEM((groups, length, 2 * lanes), BF16),
+            pltpu.VMEM((length, 2 * lanes), F32),
+        ],
+    )
+    shape = jax.ShapeDtypeStruct
+    return pl.pallas_call(
+        partial(
+            attend_forward_kernel,
+            hb=hb,
+            groups=groups,
+            scale=8**-0.5,
+            carried=len(carried),
+        ),
+        grid_spec=spec,
+        out_shape=[
+            shape(pair.shape, BF16),
+            shape(pair.shape, BF16),
+            shape((dim, n * length), BF16),
+            shape((3, n * length, width), BF16),
+            shape((n * length, width), BF16),
+            shape((n * length, width), F32),
+        ],
+        input_output_aliases={7: 0, 8: 1} if carried else {},
+        compiler_params=pltpu.CompilerParams(
+            dimension_semantics=("arbitrary", "arbitrary"), vmem_limit_bytes=48 << 20
+        ),
+        cost_estimate=pl.CostEstimate(
+            flops=n * heads * 4 * length**3,
+            transcendentals=n * heads * length**2,
+            bytes_accessed=6 * n * heads * length**2,
+        ),
+        name="attend_forward",
+    )(mols, counts, *args)
+
+
+def attend_backward_kernel(
+    mol_ref, cnt_ref, gm_ref, mixed_ref, inv_ref, qkv_ref, w_ref, mask_ref, exp_ref, cot_ref, *rest,
+    hb, groups, scale, carried
+):
+    pg_ref, gp_ref, gh_ref, l_s, r_s, k_s, qt_s, gt_s, gq_s, gk_s, gv_s = rest[carried:]
+    step, steps = pl.program_id(1), pl.num_programs(1)
+    length, width = gm_ref.shape
+    lanes = width // groups
+    per_group = lanes // (8 * hb)
+    count = cnt_ref[mol_ref[pl.program_id(0)]]
+
+    @pl.when(step == 0)
+    def _():
+        rows_ok = lax.broadcasted_iota(jnp.int32, (length, width), 0) < count
+        scaled = jnp.where(rows_ok, gm_ref[...].astype(F32) * inv_ref[...], 0.0).astype(BF16)
+        wide = scaled.astype(F32)
+        delta = (-(wide * mixed_ref[...].astype(F32))).astype(BF16)
+        value_t = qkv_ref[2].T
+        for g in range(groups):
+            part = slice(g * lanes, (g + 1) * lanes)
+            l_s[g, :, :lanes] = scaled[:, part]
+            l_s[g, :, lanes:] = delta[:, part]
+            r_s[g, :lanes, :] = value_t[part]
+            r_s[g, lanes:, :] = jnp.ones((lanes, length), BF16)
+            k_s[g] = qkv_ref[1, :, part]
+        qt_s[...] = qkv_ref[0].astype(F32).T.reshape(qt_s.shape).astype(BF16)
+        gt_s[...] = wide.T.reshape(gt_s.shape).astype(BF16)
+
+    g = step // per_group
+    block = lax.rem(step, per_group)
+    valid = (lax.broadcasted_iota(jnp.int32, (length, length), 0) < count) & (
+        lax.broadcasted_iota(jnp.int32, (length, length), 1) < count
+    )
+    total = jnp.zeros((length, lanes), F32)
+    for i in range(hb):
+        soft = dot(l_s[g] * mask_ref[0, block, i : i + 1, :], r_s[g])
+        scores = exp_ref[0, i].astype(F32) * soft + jnp.where(valid, cot_ref[0, i].astype(F32), 0.0)
+        pg_ref[0, i] = scores.astype(BF16)
+        total = total + dot(pg_ref[0, i], k_s[g] * mask_ref[1, block, i : i + 1, :lanes])
+        head = step * hb + i
+        gk_s[head] = dot(qt_s[head], pg_ref[0, i])
+        gv_s[head] = dot(gt_s[head], exp_ref[0, i])
+
+    @pl.when(block == 0)
+    def _():
+        gq_s[g] = total
+
+    @pl.when(block > 0)
+    def _():
+        gq_s[g] = gq_s[g] + total
+
+    @pl.when(step == steps - 1)
+    def _():
+        for k in range(groups):
+            gp_ref[0, :, k * lanes : (k + 1) * lanes] = (gq_s[k] * scale).astype(BF16)
+        gp_ref[1] = gk_s[...].reshape(width, length).T.astype(BF16)
+        gp_ref[2] = gv_s[...].reshape(width, length).T.astype(BF16)
+        gh_ref[...] = (
+            dot_nt(gp_ref[0], w_ref[0]) + dot_nt(gp_ref[1], w_ref[1]) + dot_nt(gp_ref[2], w_ref[2])
+        ).astype(BF16)
+
+
+def attend_backward_call(mols, counts, gm, mixed, inverse, qkv, weights, exps, cot, carried, hb=16):
+    n, (_, heads, length, _) = mols.shape[0], exps.shape
+    dim, width = weights.shape[1], weights.shape[2]
+    groups = max(1, width // 128)
+    lanes = width // groups
+    masks = head_masks(groups, width, hb, True)
+    pair_spec, rows, three = specs_of(length, hb)
+    args = [gm, mixed, inverse, qkv, weights, masks, exps, cot, *carried]
+    spec = pltpu.PrefetchScalarGridSpec(
+        num_scalar_prefetch=2,
+        grid=(n, heads // hb),
+        in_specs=[
+            rows(width), rows(width), rows(width), three(width),
+            whole(weights.shape), whole(masks.shape), pair_spec, pair_spec,
+        ] + [ANY] * len(carried),
+        out_specs=[pair_spec, three(width), rows(dim)],
+        scratch_shapes=[
+            pltpu.VMEM((groups, length, 2 * lanes), BF16),
+            pltpu.VMEM((groups, 2 * lanes, length), BF16),
+            pltpu.VMEM((groups, length, lanes), BF16),
+            pltpu.VMEM((heads, 8, length), BF16),
+            pltpu.VMEM((heads, 8, length), BF16),
+            pltpu.VMEM((groups, length, lanes), F32),
+            pltpu.VMEM((heads, 8, length), F32),
+            pltpu.VMEM((heads, 8, length), F32),
+        ],
+    )
+    shape = jax.ShapeDtypeStruct
+    return pl.pallas_call(
+        partial(
+            attend_backward_kernel,
+            hb=hb,
+            groups=groups,
+            scale=8**-0.5,
+            carried=len(carried),
+        ),
+        grid_spec=spec,
+        out_shape=[
+            shape(exps.shape, BF16),
+            shape((3, n * length, width), BF16),
+            shape((n * length, dim), BF16),
+        ],
+        input_output_aliases={10: 0} if carried else {},
+        compiler_params=pltpu.CompilerParams(
+            dimension_semantics=("arbitrary", "arbitrary"), vmem_limit_bytes=48 << 20
+        ),
+        cost_estimate=pl.CostEstimate(
+            flops=n * heads * 6 * length**3,
+            transcendentals=0,
+            bytes_accessed=6 * n * heads * length**2,
+        ),
+        name="attend_backward",
+    )(mols, counts, *args)
+
+
+ROOT = (2 / np.pi) ** 0.5
+
+
+def layer_kernel(
+    me_ref, atoms_ref, mine_ref, other_ref, cot_ref, gains_ref, a0_ref, a1_ref, b0_ref, b1_ref,
+    out_ref, first_ref, gm_mine_ref, gm_other_ref, ga0_ref, ga1_ref, gb0_ref, gb1_ref,
+    win_s, wout_s, ow_s, sum_s, acc_s, gh_s, normed_s, inv_s, hid_s, hid_t_s, *, bits_a, bits_b
+):
+    me = me_ref[0]
+    c, steps = pl.program_id(0), pl.num_programs(0)
+    half = a0_ref.shape[0]
+    dim = atoms_ref.shape[1]
+    width = mine_ref.shape[1]
+    rows = dim // (2 * half)
+    ff_rows = b0_ref.shape[1]
+    e_rows = dim // half
+
+    def shards(bits, near, far):
+        for p in range(2 * half):
+            yield p, me ^ relative(p, bits), (near, p) if p < half else (far, p - half)
+
+    @pl.when(c == 0)
+    def _():
+        for p, owner, (ref, q) in shards(bits_a, a0_ref, a1_ref):
+            for k in range(4):
+                win_s[k, pl.ds(pl.multiple_of(owner * rows, rows), rows), :] = ref[q, k * rows : (k + 1) * rows, :]
+            at = pl.multiple_of((owner // 2) * e_rows, e_rows)
+            ow_s[relative(p, bits_a) & 1, pl.ds(at, e_rows), :] = ref[q, 4 * rows : 4 * rows + e_rows, :width]
+        for p, owner, (ref, q) in shards(bits_b, b0_ref, b1_ref):
+            wout_s[pl.ds(pl.multiple_of(owner * ff_rows, ff_rows), ff_rows), :] = ref[q]
+        first_sum = (
+            atoms_ref[...].astype(F32) + dot_nt(mine_ref[...], ow_s[0]) + dot_nt(other_ref[...], ow_s[1])
+        )
+        sum_s[...] = first_sum
+        center = first_sum - jnp.mean(first_sum, -1, keepdims=True)
+        inverse = lax.rsqrt(jnp.mean(center * center, -1, keepdims=True) + 1e-05)
+        normed = center * inverse
+        normed_s[...] = normed
+        inv_s[...] = inverse
+        hidden = (normed * gains_ref[1:2, :]).astype(BF16)
+        hid_s[...] = hidden
+        hid_t_s[...] = hidden.T
+        acc_s[...] = jnp.zeros_like(acc_s)
+        gh_s[...] = jnp.zeros_like(gh_s)
+
+    win = win_s[c]
+    wout = wout_s[pl.ds(pl.multiple_of(c * dim, dim), dim), :]
+    inner = dot(hid_s[...], win)
+    square = inner * inner
+    tanh = jnp.tanh(ROOT * inner * (1.0 + 0.044715 * square))
+    activated = (0.5 * inner * (1.0 + tanh)).astype(BF16)
+    slope = 0.5 * (1.0 + tanh) + (0.5 * ROOT) * inner * (1.0 - tanh * tanh) * (1.0 + (3 * 0.044715) * square)
+    acc_s[...] += dot(activated, wout)
+    grad_inner = (dot_nt(cot_ref[...], wout) * slope).astype(BF16)
+    gh_s[...] += dot_nt(grad_inner, win)
+    grad_in = dot(hid_t_s[...], grad_inner).astype(BF16)
+    win_s[c] = grad_in
+    grad_out = dot_tn(activated, cot_ref[...]).astype(BF16)
+    wout_s[pl.ds(pl.multiple_of(c * dim, dim), dim), :] = grad_out
+
+    @pl.when(c == steps - 1)
+    def _():
+        out_ref[...] = (sum_s[...] + acc_s[...]).astype(BF16)
+        normed = normed_s[...]
+        grad_norm = gh_s[...] * gains_ref[1:2, :]
+        grad_first = cot_ref[...].astype(F32) + inv_s[...] * (
+            grad_norm
+            - jnp.mean(grad_norm, -1, keepdims=True)
+            - normed * jnp.mean(grad_norm * normed, -1, keepdims=True)
+        )
+        first_ref[...] = grad_first
+        grad_attention = grad_first.astype(BF16)
+        gm_mine_ref[...] = dot(grad_attention, ow_s[0]).astype(BF16)
+        gm_other_ref[...] = dot(grad_attention, ow_s[1]).astype(BF16)
+        ow_s[0] = dot_tn(grad_attention, mine_ref[...]).astype(BF16)
+        ow_s[1] = dot_tn(grad_attention, other_ref[...]).astype(BF16)
+        for p, owner, (ref, q) in shards(bits_a, ga0_ref, ga1_ref):
+            for k in range(4):
+                ref[q, k * rows : (k + 1) * rows, :] = win_s[k, pl.ds(pl.multiple_of(owner * rows, rows), rows), :]
+            at = pl.multiple_of((owner // 2) * e_rows, e_rows)
+            ref[q, 4 * rows : 4 * rows + e_rows, :width] = ow_s[relative(p, bits_a) & 1, pl.ds(at, e_rows), :]
+            ref[q, 4 * rows : 4 * rows + e_rows, width:] = jnp.zeros((e_rows, dim - width), BF16)
+        for p, owner, (ref, q) in shards(bits_b, gb0_ref, gb1_ref):
+            ref[q] = wout_s[pl.ds(pl.multiple_of(owner * ff_rows, ff_rows), ff_rows), :]
+
+
+def layer_call(me, atoms, mine, other, cot, gains, a_pair, b_pair, bits_a, bits_b):
+    own, dim = atoms.shape
+    width = mine.shape[1]
+    ff = 2 * b_pair[0].shape[0] * b_pair[0].shape[1]
+    args = [atoms, mine, other, cot, gains, *a_pair, *b_pair]
+    shape = jax.ShapeDtypeStruct
+    outs = [
+        shape((own, dim), BF16),
+        shape((own, dim), F32),
+        shape((own, width), BF16),
+        shape((own, width), BF16),
+        *[shape(x.shape, BF16) for x in (*a_pair, *b_pair)],
+    ]
+    spec = pltpu.PrefetchScalarGridSpec(
+        num_scalar_prefetch=1,
+        grid=(ff // dim,),
+        in_specs=[whole(x.shape) for x in args],
+        out_specs=[whole(x.shape) for x in outs],
+        scratch_shapes=[
+            pltpu.VMEM((ff // dim, dim, dim), BF16),
+            pltpu.VMEM((ff, dim), BF16),
+            pltpu.VMEM((2, dim, width), BF16),
+            pltpu.VMEM((own, dim), F32),
+            pltpu.VMEM((own, dim), F32),
+            pltpu.VMEM((own, dim), F32),
+            pltpu.VMEM((own, dim), F32),
+            pltpu.VMEM((own, 1), F32),
+            pltpu.VMEM((own, dim), BF16),
+            pltpu.VMEM((dim, own), BF16),
+        ],
+    )
+    return pl.pallas_call(
+        partial(layer_kernel, bits_a=bits_a, bits_b=bits_b),
+        grid_spec=spec,
+        out_shape=outs,
+        compiler_params=pltpu.CompilerParams(
+            dimension_semantics=("arbitrary",), vmem_limit_bytes=60 << 20
+        ),
+        cost_estimate=pl.CostEstimate(
+            flops=12 * own * dim * ff, transcendentals=own * ff, bytes_accessed=8 * dim * ff
+        ),
+        name="layer",
+    )(me, *args)
+
+
+def project_grad_kernel(me_ref, *refs, bits, parts):
+    b = me_ref[0]
+    near_ref, far_ref, full_s = refs[2 * parts :]
+    half = near_ref.shape[0]
+    rows = full_s.shape[1] // (2 * half)
+    for s in range(3):
+        full_s[s] = sum(dot(refs[k][...], refs[parts + k][s]) for k in range(parts)).astype(BF16)
+    for p in range(2 * half):
+        ref, q = (near_ref, p) if p < half else (far_ref, p - half)
+        at = pl.multiple_of((b ^ relative(p, bits)) * rows, rows)
+        for s in range(3):
+            ref[q, s * rows : (s + 1) * rows, :] = full_s[s, pl.ds(at, rows), :]
+
+
+def project_grad_call(me, hid_ts, gps, bits):
+    dim, width = hid_ts[0].shape[0], gps[0].shape[2]
+    half = 2 ** (len(bits) - 1)
+    rows = dim // (2 * half)
+    args = [*hid_ts, *gps]
+    outs = [jax.ShapeDtypeStruct((half, 3 * rows, width), BF16)] * 2
+    return pl.pallas_call(
+        partial(project_grad_kernel, bits=bits, parts=len(hid_ts)),
+        grid_spec=pltpu.PrefetchScalarGridSpec(
+            num_scalar_prefetch=1,
+            grid=(1,),
+            in_specs=[whole(x.shape) for x in args],
+            out_specs=[whole(x.shape) for x in outs],
+            scratch_shapes=[pltpu.VMEM((3, dim, width), BF16)],
+        ),
+        out_shape=outs,
+        compiler_params=pltpu.CompilerParams(vmem_limit_bytes=32 << 20),
+        name="project_grad",
+    )(me, *args)
+
+
+def last_kernel(atoms_ref, gains_ref, first_ref, ga_ref, gb_ref, recv_ref, out_ref):
+    values = atoms_ref[...].astype(F32)
+    center = values - jnp.mean(values, -1, keepdims=True)
+    inverse = lax.rsqrt(jnp.mean(center * center, -1, keepdims=True) + 1e-05)
+    normed = center * inverse
+    part = ga_ref.shape[0]
+    grads = jnp.concatenate([ga_ref[...], gb_ref[...]], 0).astype(F32) + recv_ref[...].astype(F32)
+    grad_norm = grads * gains_ref[0:1, :]
+    out_ref[...] = (
+        first_ref[...]
+        + inverse
+        * (
+            grad_norm
+            - jnp.mean(grad_norm, -1, keepdims=True)
+            - normed * jnp.mean(grad_norm * normed, -1, keepdims=True)
+        )
+    ).astype(BF16)
+
+
+def last_call(atoms, gains, first, gh_a, gh_b, recv):
+    args = [atoms, gains, first, gh_a, gh_b, recv]
+    return pl.pallas_call(
+        last_kernel,
+        grid=(1,),
+        in_specs=[whole(x.shape) for x in args],
+        out_specs=whole(atoms.shape),
+        out_shape=jax.ShapeDtypeStruct(atoms.shape, BF16),
+        compiler_params=pltpu.CompilerParams(vmem_limit_bytes=32 << 20),
+        name="last_norm",
+    )(*args)
+
+
+def join(values, received):
+    return jnp.concatenate([values, received], 0)
+
+
+def add(kept, received):
+    return (kept.astype(F32) + received.astype(F32)).astype(BF16)
+
+
+def halves(values):
+    half = values.shape[0] // 2
+    return values[:half], values[half:]
+
+
+def body_pairs(
+    atoms, pair, counts, qkv_weight, out_weight, ln1_gain, ln2_gain, w_in, w_out, out_cot, pair_cot,
+    batch
+):
+    b = lax.axis_index("batch")
+    h = lax.axis_index("head")
+    own, dim = atoms.shape
+    length = pair.shape[2]
+    width = qkv_weight.shape[2]
+    shard = ln1_gain.shape[0]
+    top = batch.bit_length() - 1
+    far_bits = [1 << k for k in range(top - 1, 1, -1)]
+    batch_bits = [*far_bits, 2, 1]
+    bits_a = [2 * bit for bit in far_bits] + [4, 1, 2]
+    bits_b = [2 * bit for bit in far_bits] + [1, 4, 2]
+    nz = len(far_bits)
+    over_batch = lambda x, bit: swap(x, "batch", batch, bit)
+    over_head = lambda x: swap(x, "head", 2, 1)
+    over_both = lambda x, bit: swap(x, BOTH, 2 * batch, bit)
+
+    def split_gain(gain):
+        high = gain.astype(BF16)
+        return [high, (gain - high.astype(F32)).astype(BF16)]
+
+    gain_row = jnp.concatenate(split_gain(ln1_gain) + split_gain(ln2_gain))[None]
+    gain_row = jnp.concatenate([gain_row, over_head(gain_row)], 1)
+    atoms_other = over_head(atoms)
+    tail = jnp.pad(gain_row, ((0, 15), (0, width - gain_row.shape[1])))
+    gathered = jnp.concatenate([qkv_weight.reshape(-1, width), tail], 0)[None]
+    for bit in batch_bits[:-1]:
+        gathered = join(gathered, over_batch(gathered, bit))
+    far = over_batch(gathered, batch_bits[-1])
+    me_batch = jnp.stack([b, h])
+    weights, gains = pl.pallas_call(
+        partial(prep_kernel, bits=batch_bits, heads_bits=1, shard=shard),
+        grid_spec=pltpu.PrefetchScalarGridSpec(
+            num_scalar_prefetch=1,
+            grid=(1,),
+            in_specs=[whole(gathered.shape)] * 2,
+            out_specs=[whole((3, dim, width)), whole((2, dim))],
+            scratch_shapes=[pltpu.VMEM((batch, width), F32)],
+        ),
+        out_shape=[jax.ShapeDtypeStruct((3, dim, width), BF16), jax.ShapeDtypeStruct((2, dim), F32)],
+        name="prepare",
+    )(me_batch, gathered, far)
+
+    e_rows = out_weight.shape[0]
+    blocks = w_in.shape[1] // dim
+    in_rows = [w_in[:, k * dim : (k + 1) * dim] for k in range(blocks)]
+    out_rows = jnp.pad(out_weight, ((0, 0), (0, dim - width)))
+    bulk = jnp.concatenate([*in_rows, out_rows, w_out], 0)[None]
+    cut = bulk.shape[1] - w_out.shape[0]
+    for bit in bits_a[:nz]:
+        bulk = join(bulk, over_both(bulk, bit))
+    part_a, part_b = bulk[:, :cut], bulk[:, cut:]
+    for bit_a, bit_b in zip(bits_a[nz:-1], bits_b[nz:-1]):
+        part_a, part_b = join(part_a, over_both(part_a, bit_a)), join(part_b, over_both(part_b, bit_b))
+    a_pair = (part_a, over_both(part_a, bits_a[-1]))
+    b_pair = (part_b, over_both(part_b, bits_b[-1]))
+
+    per = own // length
+    mine, theirs = h * per, (1 - h) * per
+    plan = [
+        (mine[None], atoms[:length]),
+        (theirs + jnp.arange(per, dtype=jnp.int32), atoms_other),
+        (mine + jnp.arange(1, per, dtype=jnp.int32), atoms[length:]),
+    ]
+    carried = ()
+    saved = []
+    for mols, rows in plan:
+        new_pair, exps, *rest = attend_forward_call(mols, counts, rows, weights, gains, pair, carried)
+        carried = (new_pair, exps)
+        saved.append(rest)
+    mixed_other = over_head(saved[1][2])
+    mixed_mine = jnp.concatenate([saved[0][2], saved[2][2]], 0)
+
+    me = (2 * b + h)[None]
+    output, first, gm_mine, gm_other, ga0, ga1, gb0, gb1 = layer_call(
+        me, atoms, mixed_mine, mixed_other, out_cot, gains, a_pair, b_pair, bits_a, bits_b
+    )
+    gm_received = over_head(gm_other)
+    part_a = add(ga0, over_both(ga1, bits_a[-1]))
+    part_b = add(gb0, over_both(gb1, bits_b[-1]))
+    for bit_a, bit_b in zip(bits_a[-2:nz - 1:-1], bits_b[-2:nz - 1:-1]):
+        (keep_a, send_a), (keep_b, send_b) = halves(part_a), halves(part_b)
+        part_a, part_b = add(keep_a, over_both(send_a, bit_a)), add(keep_b, over_both(send_b, bit_b))
+    bulk = jnp.concatenate([part_a, part_b], 1)
+    for bit in bits_a[nz - 1 :: -1]:
+        keep, send = halves(bulk)
+        bulk = add(keep, over_both(send, bit))
+    bulk = bulk[0].astype(F32)
+    shard_rows = w_in.shape[0]
+    in_grad = jnp.concatenate([bulk[k * shard_rows : (k + 1) * shard_rows] for k in range(blocks)], 1)
+    out_grad = bulk[blocks * shard_rows : cut, :width]
+    outer_grad = bulk[cut:]
+    gain_two_grad = jnp.sum(in_grad * w_in.astype(F32), 1) / ln2_gain
+
+    gm_parts = [gm_mine[:length], gm_received, gm_mine[length:]]
+    carried = ()
+    grads = []
+    for (mols, _), gm, (hid_t, qkv, mixed, inverse) in zip(plan, gm_parts, saved):
+        pair_grad, *rest = attend_backward_call(
+            mols, counts, gm, mixed, inverse, qkv, weights, exps, pair_cot, carried
+        )
+        carried = (pair_grad,)
+        grads.append(rest)
+    hidden_received = over_head(grads[1][1])
+    near, far = project_grad_call(
+        me_batch, [s[0] for s in saved], [g[0] for g in grads], batch_bits
+    )
+    near = add(near, over_batch(far, batch_bits[-1]))
+    for bit in batch_bits[-2::-1]:
+        keep, send = halves(near)
+        near = add(keep, over_batch(send, bit))
+    qkv_grad = near[0].reshape(qkv_weight.shape).astype(F32)
+    gain_part = jnp.sum(qkv_grad * qkv_weight.astype(F32), (0, 2)).reshape(2, shard)
+    gain_mine = lax.dynamic_index_in_dim(gain_part, h, 0, False)
+    gain_other = over_head(lax.dynamic_index_in_dim(gain_part, 1 - h, 0, False))
+    gain_one_grad = (gain_mine + gain_other) / ln1_gain
+    atoms_grad = last_call(atoms, gains, first, grads[0][1], grads[2][1], hidden_received)
+    return (
+        output, new_pair, atoms_grad, pair_grad, qkv_grad, out_grad,
+        gain_one_grad, gain_two_grad, in_grad, outer_grad,
+    )
+
+
 def solution(mesh):
-    placed = (
-        P(("batch", "head"), None),
-        P("batch", "head", None, None),
-        P("batch"),
-        P(None, "batch", "head"),
-        P("batch", "head"),
-        P(("batch", "head")),
-        P(("batch", "head")),
-        P(("batch", "head"), None),
-        P(("batch", "head"), None),
-        P(("batch", "head"), None),
-        P("batch", "head", None, None),
-    )
+    rows = P(BOTH, None)
+    heads = P("batch", "head", None, None)
+    batch, head = mesh.shape["batch"], mesh.shape["head"]
+    body = partial(body_pairs, batch=batch) if (batch, head) == (16, 2) else body_native
     return jax.shard_map(
         body,
         mesh=mesh,
-        in_specs=placed,
+        in_specs=(
+            rows, heads, P("batch"), P(None, "batch", "head"), P("batch", "head"),
+            P(BOTH), P(BOTH), rows, rows, rows, heads,
+        ),
         out_specs=(
-            P(("batch", "head"), None),
-            P("batch", "head", None, None),
-            P(("batch", "head"), None),
-            P("batch", "head", None, None),
-            P(None, "batch", "head"),
-            P("batch", "head"),
-            P(("batch", "head")),
-            P(("batch", "head")),
-            P(("batch", "head"), None),
-            P(("batch", "head"), None),
+            rows, heads, rows, heads, P(None, "batch", "head"), P("batch", "head"),
+            P(BOTH), P(BOTH), rows, rows,
         ),
         check_vma=False,
     )

time: 1030 us -> 248 us (0.24)
  waiting for transfers between devices: 502 us -> 64.1 us
  matrix products: 158 us -> 0 us
  local copies, waits for them, and re-layouts: 171 us -> 15.6 us
  blocking collectives: 125 us -> 0 us
  Pallas kernels: 0 us -> 101 us
  starting transfers between devices: 0.41 us -> 53.8 us
  other arithmetic: 45.7 us -> 11.8 us
  between operations: 17.2 us -> 1.08 us
    reduce_scatter x5 -> x0, waiting for transfers between devices: 336 us -> none  [the longest x1 142 us: body(): lax.psum_scatter(grad_inner_w, ('batch', 'head'), scatter_dimension=0, ti...]
    dot_general x24 -> x0, matrix products: 119 us -> none  [the longest x4 37.5 us: scores_of(): jnp.einsum('mqhd,mkhd->mhqk', query_part, key_part, preferred_element_typ...]
    pallas_call x0 -> x10, Pallas kernels: none -> 101 us  [the longest x3 45.2 us: attend_backward_call(): pl.pallas_call(partial(attend_backward_kernel, hb=hb, groups=groups, scal...]
    all_gather x4 -> x0, waiting for transfers between devices: 95.1 us -> none  [the longest x1 54 us: body(): lax.all_gather(w_in, ('batch', 'head'), axis=0, tiled=True)]
    dynamic_update_slice x14 -> x0, local copies, waits for them, and re-layouts: 82.5 us -> none  [body(): lax.map(partial(attend_forward, score_scale=score_scale), (query_all, key...]
    unnamed x2 -> x0, blocking collectives: 82.3 us -> none
    unnamed x11 -> x0, waiting for transfers between devices: 70.9 us -> none
    ppermute x0 -> x30, waiting for transfers between devices: none -> 64.1 us  [swap(): return lax.ppermute(values, axes, [(i, i ^ bit) for i in range(count)])]
  transfers between devices with their start and end apart: 10 -> 30, of which waited for: 8 -> 14; matrix products, arithmetic and copies ran while one was open for 8% -> 5% of each run, Pallas kernels for 0% -> 34%
where the time goes in v1:
time: 248 us; the launch traced here: 247 us
  Pallas kernels  101 us (41%)
  waiting for transfers between devices  64.1 us (26%)
  starting transfers between devices  53.8 us (22%)
  local copies, waits for them, and re-layouts  15.6 us (6%)
  other arithmetic  11.8 us (5%)
    ppermute x30, waiting for transfers between devices, swap(): return lax.ppermute(values, axes, [(i, i ^ bit) for i in range(count)])  64.1 us
    ppermute x30, starting transfers between devices, swap(): return lax.ppermute(values, axes, [(i, i ^ bit) for i in range(count)])  53.8 us
    pallas_call x3, Pallas kernels, attend_backward_call(): pl.pallas_call(partial(attend_backward_kernel, hb=hb, groups=groups, scal...  45.2 us
    pallas_call x3, Pallas kernels, attend_forward_call(): pl.pallas_call(partial(attend_forward_kernel, hb=hb, groups=groups, scale...  32 us
    pallas_call x1, Pallas kernels, layer_call(): pl.pallas_call(partial(layer_kernel, bits_a=bits_a, bits_b=bits_b), grid_...  17.4 us
    unnamed x75, local copies, waits for them, and re-layouts  10.4 us
  transfers between devices with their start and end apart: 30, of which 14 were waited for; matrix products, arithmetic and copies ran while one was open for 5% of the time, Pallas kernels for 34%

profile of v1, /device:TPU:0, one launch (start us, length us, event | category | flops | bytes accessed | tf_op | source)
XLA Modules:
  0.0 246.9 jit_solution(3909591943554407034)
XLA Ops:
  5.1 4.0 %collective-permute-start.7 = (bf16[1,160,512]{2,1,0:T(8,128)(2,1)S(1)}, bf16[1,160,512]{2,1,0:T(8,128)(2,1)S(1)}, u32[]{:S(2)}, u32[]{:S(2)}) collective-permute-start(bf16[1,160,512]{2,1,0:T(8,128)(2,1)S(1)} %bitcast.30), channel_id=1, source_target_pairs={{0,16},{1,17},{2,18},{3,19},{4,20},{5,21},{6,22},{7,23},{8,24},{9,... | collective-permute-start | bytes 491528 | tf_op jit(solution)/shard_map/ppermute | solution.py:256
  9.2 7.7 %collective-permute-done.7 = bf16[1,160,512]{2,1,0:T(8,128)(2,1)S(1)} collective-permute-done((bf16[1,160,512]{2,1,0:T(8,128)(2,1)S(1)}, bf16[1,160,512]{2,1,0:T(8,128)(2,1)S(1)}, u32[]{:S(2)}, u32[]{:S(2)}) %collective-permute-start.7) | collective-permute-done | bytes 163872 | tf_op jit(solution)/shard_map/ppermute | solution.py:256
  17.7 8.2 %collective-permute-done.8 = bf16[2,160,512]{2,1,0:T(8,128)(2,1)S(1)} collective-permute-done((bf16[2,160,512]{2,1,0:T(8,128)(2,1)S(1)}, bf16[2,160,512]{2,1,0:T(8,128)(2,1)S(1)}, u32[]{:S(2)}, u32[]{:S(2)}) %collective-permute-start.8) | collective-permute-done | bytes 327712 | tf_op jit(solution)/shard_map/ppermute | solution.py:256
  26.0 1.3 collective-permute-start.9
  27.4 1.5 collective-permute-start
  28.9 6.5 %collective-permute-done.9 = bf16[4,96,512]{2,1,0:T(8,128)(2,1)S(1)} collective-permute-done((bf16[4,96,512]{2,1,0:T(8,128)(2,1)S(1)}, bf16[4,96,512]{2,1,0:T(8,128)(2,1)S(1)}, u32[]{:S(2)}, u32[]{:S(2)}) %collective-permute-start.9) | collective-permute-done | bytes 393248 | tf_op jit(solution)/shard_map/ppermute | solution.py:256
  35.5 1.3 collective-permute-start.10
  36.9 4.5 %collective-permute-start.1 = (bf16[1,112,256]{2,1,0:T(8,128)(2,1)S(1)}, bf16[1,112,256]{2,1,0:T(8,128)(2,1)S(1)}, u32[]{:S(2)}, u32[]{:S(2)}) collective-permute-start(bf16[1,112,256]{2,1,0:T(8,128)(2,1)S(1)} %maximum_bitcast_fusion), channel_id=1, source_target_pairs={{0,16},{2,18},{4,20},{6,22},{8,24},{10,26},{12,28},{14,30},{16,0},... | collective-permute-start | bytes 172040 | tf_op jit(solution)/shard_map/ppermute | solution.py:256
  42.1 1.7 collective-permute-done.1
  43.8 1.3 collective-permute-start.2
  45.1 3.5 %collective-permute-done.2 = bf16[2,112,256]{2,1,0:T(8,128)(2,1)S(1)} collective-permute-done((bf16[2,112,256]{2,1,0:T(8,128)(2,1)S(1)}, bf16[2,112,256]{2,1,0:T(8,128)(2,1)S(1)}, u32[]{:S(2)}, u32[]{:S(2)}) %collective-permute-start.2) | collective-permute-done | bytes 114720 | tf_op jit(solution)/shard_map/ppermute | solution.py:256
  48.7 1.6 collective-permute-start.3
  50.2 7.8 %collective-permute-done.12 = bf16[4,64,512]{2,1,0:T(8,128)(2,1)S(1)} collective-permute-done((bf16[4,64,512]{2,1,0:T(8,128)(2,1)S(1)}, bf16[4,64,512]{2,1,0:T(8,128)(2,1)S(1)}, u32[]{:S(2)}, u32[]{:S(2)}) %collective-permute-start.12) | collective-permute-done | bytes 262176 | tf_op jit(solution)/shard_map/ppermute | solution.py:256
  58.1 1.7 collective-permute-start.13
  59.8 1.6 collective-permute-start.5
  61.5 1.3 pad_maximum_fusion.a0_ref
  63.5 5.2 %collective-permute-done.13 = bf16[8,64,512]{2,1,0:T(8,128)(2,1)} collective-permute-done((bf16[8,64,512]{2,1,0:T(8,128)(2,1)S(1)}, bf16[8,64,512]{2,1,0:T(8,128)(2,1)}, u32[]{:S(2)}, u32[]{:S(2)}) %collective-permute-start.13) | collective-permute-done | bytes 524320 | tf_op jit(solution)/shard_map/ppermute | solution.py:256
  68.6 2.1 pad_maximum_fusion.1.b0_ref
  71.4 2.9 %prepare.1 = (bf16[3,512,256]{2,1,0:T(8,128)(2,1)}, f32[2,512]{1,0:T(2,128)}) custom-call(s32[2]{0:T(128)} %pad_add_fusion.me_ref, bf16[8,112,256]{2,1,0:T(8,128)(2,1)} %copy-done.27, bf16[8,112,256]{2,1,0:T(8,128)(2,1)} %collective-permute-done.4.far_ref), custom_call_target="tpu_custom_call" | custom-call | tf_op jit(solution)/shard_map/prepare/pallas_call | solution.py:808
  76.1 8.9 %attend_forward.3 = (bf16[4,32,256,256]{3,2,1,0:T(8,128)(2,1)}, bf16[4,32,256,256]{3,2,1,0:T(8,128)(2,1)}, bf16[512,256]{1,0:T(8,128)(2,1)S(1)}, bf16[3,256,256]...) custom-call(s32[1]{0:T(128)} %bitcast.1.mol_ref, s32[4]{0:T(128)S(1)} %copy-done.21, ...), custom_call_target="tpu_custom_call" | custom-call | flops 2147483648 | bytes 12582912 | tf_op jit(solution)/shard_map/attend_forward/pallas_call | solution.py:417
  86.5 14.2 %attend_forward.4 = (bf16[4,32,256,256]{3,2,1,0:T(8,128)(2,1)}, bf16[4,32,256,256]{3,2,1,0:T(8,128)(2,1)}, bf16[512,512]{1,0:T(8,128)(2,1)S(1)}, bf16[3,512,256]...) custom-call(s32[2]{0:T(128)S(1)} %iota_add_fusion.mol_ref, ...), custom_call_target="tpu_custom_call", output_to_operand_aliasing={{0}: (7, {}), {1}: (8, {})} | custom-call | flops 4294967296 | bytes 25165824 | tf_op jit(solution)/shard_map/attend_forward/pallas_call | solution.py:417
  100.7 1.5 collective-permute-start.6
  102.2 8.8 %attend_forward.5 = (bf16[4,32,256,256]{3,2,1,0:T(8,128)(2,1)}, bf16[4,32,256,256]{3,2,1,0:T(8,128)(2,1)}, bf16[512,256]{1,0:T(8,128)(2,1)S(1)}, bf16[3,256,256]...) custom-call(s32[1]{0:T(128)S(6)} %add.65.mol_ref, ...), custom_call_target="tpu_custom_call", output_to_operand_aliasing={{0}: (7, {}), {1}: (8, {})} | custom-call | flops 2147483648 | bytes 12582912 | tf_op jit(solution)/shard_map/attend_forward/pallas_call | solution.py:417
  112.5 17.4 %layer.1 = (bf16[512,512]{1,0:T(8,128)(2,1)}, f32[512,512]{1,0:T(8,128)}, bf16[512,256]{1,0:T(8,128)(2,1)}, bf16[512,256]{1,0:T(8,128)(2,1)}, bf16[16,96,512]{2,...) custom-call(s32[1]{0:T(128)} %bitcast.me_ref, ...), custom_call_target="tpu_custom_call" | custom-call | flops 6442450944 | bytes 8388608 | tf_op jit(solution)/shard_map/layer/pallas_call | solution.py:681
  132.9 12.4 %attend_backward.3 = (bf16[4,32,256,256]{3,2,1,0:T(8,128)(2,1)}, bf16[3,256,256]{2,1,0:T(8,128)(2,1)S(1)}, bf16[256,512]{1,0:T(8,128)(2,1)S(1)}) custom-call(s32[1]{0:T(128)} %bitcast.1.mol_ref, s32[4]{0:T(128)S(1)} %copy-done.21, bf16[256,256]{1,0:T(8,128)(2,1)S(1)} %get-tuple-element.101.gm_ref, bf16[256,256]{1,0:T(8,128)(2,1)S(1)} %get-tuple-element.51.mixed_ref, ...), custom_call_target="tpu_custom_call" | custom-call | flops 3221225472 | bytes 12582912 | tf_op jit(solution)/shard_map/attend_backward/pallas_call | solution.py:537
  146.0 20.6 %attend_backward.4 = (bf16[4,32,256,256]{3,2,1,0:T(8,128)(2,1)}, bf16[3,512,256]{2,1,0:T(8,128)(2,1)S(1)}, bf16[512,512]{1,0:T(8,128)(2,1)}) custom-call(s32[2]{0:T(128)S(1)} %iota_add_fusion.mol_ref, s32[4]{0:T(128)S(1)} %copy-done.21, bf16[512,256]{1,0:T(8,128)(2,1)S(1)} %collective-permute-done.15.gm_ref, ...), custom_call_target="tpu_custom_call", output_to_operand_aliasing={{0}: (10, {})} | custom-call | flops 6442450944 | bytes 25165824 | tf_op jit(solution)/shard_map/attend_backward/pallas_call | solution.py:537
  166.6 12.2 %attend_backward.5 = (bf16[4,32,256,256]{3,2,1,0:T(8,128)(2,1)}, bf16[3,256,256]{2,1,0:T(8,128)(2,1)S(1)}, bf16[256,512]{1,0:T(8,128)(2,1)S(1)}) custom-call(s32[1]{0:T(128)S(6)} %add.65.mol_ref, s32[4]{0:T(128)S(1)} %copy-done.21, bf16[256,256]{1,0:T(8,128)(2,1)S(1)} %get-tuple-element.100.gm_ref, ...), custom_call_target="tpu_custom_call", output_to_operand_aliasing={{0}: (10, {})} | custom-call | flops 3221225472 | bytes 12582912 | tf_op jit(solution)/shard_map/attend_backward/pallas_call | solution.py:537
  178.8 1.6 project_grad.1
  180.5 1.7 collective-permute-start.16
  182.3 1.6 collective-permute-start.18
  186.1 1.2 copy-done.23
  188.3 1.6 collective-permute-start.22
  190.2 4.1 %collective-permute-start.19 = (bf16[2,96,256]{2,1,0:T(8,128)(2,1)S(1)}, bf16[2,96,256]{2,1,0:T(8,128)(2,1)S(1)}, u32[]{:S(2)}, u32[]{:S(2)}) collective-permute-start(bf16[2,96,256]{2,1,0:T(8,128)(2,1)S(1)} %slice.160), channel_id=1, source_target_pairs={{0,8},{2,10},{4,12},{6,14},{8,0},{10,2},{12,4},{14,6},{16,24},{18,... | collective-permute-start | bytes 294920 | tf_op jit(solution)/shard_map/ppermute | solution.py:256
  194.3 1.2 collective-permute-done.16.recv_ref
  195.5 1.6 last_norm.1
  197.1 6.6 %collective-permute-start.20 = (bf16[1,96,256]{2,1,0:T(8,128)(2,1)S(1)}, bf16[1,96,256]{2,1,0:T(8,128)(2,1)S(1)}, u32[]{:S(2)}, u32[]{:S(2)}) collective-permute-start(bf16[1,96,256]{2,1,0:T(8,128)(2,1)S(1)} %slice.162), channel_id=1, source_target_pairs={{0,16},{2,18},{4,20},{6,22},{8,24},{10,26},{12,28},{14,30},{16,0},... | collective-permute-start | bytes 147464 | tf_op jit(solution)/shard_map/ppermute | solution.py:256
  203.7 1.2 add_convert_fusion.3
  204.9 1.8 collective-permute-start.26
  206.8 5.7 %collective-permute-done.22 = bf16[8,96,512]{2,1,0:T(8,128)(2,1)} collective-permute-done((bf16[8,96,512]{2,1,0:T(8,128)(2,1)}, bf16[8,96,512]{2,1,0:T(8,128)(2,1)}, u32[]{:S(2)}, u32[]{:S(2)}) %collective-permute-start.22) | collective-permute-done | bytes 786464 | tf_op jit(solution)/shard_map/ppermute | solution.py:256
  212.4 1.3 add_convert_fusion.2
  213.8 1.4 collective-permute-start.23
  215.3 2.2 collective-permute-done.26
  217.6 6.5 %collective-permute-done.23 = bf16[4,96,512]{2,1,0:T(8,128)(2,1)S(1)} collective-permute-done((bf16[4,96,512]{2,1,0:T(8,128)(2,1)S(1)}, bf16[4,96,512]{2,1,0:T(8,128)(2,1)S(1)}, u32[]{:S(2)}, u32[]{:S(2)}) %collective-permute-start.23) | collective-permute-done | bytes 393248 | tf_op jit(solution)/shard_map/ppermute | solution.py:256
  224.3 4.0 %collective-permute-start.27 = (bf16[2,160,512]{2,1,0:T(8,128)(2,1)S(1)}, bf16[2,160,512]{2,1,0:T(8,128)(2,1)S(1)}, u32[]{:S(2)}, u32[]{:S(2)}) collective-permute-start(bf16[2,160,512]{2,1,0:T(8,128)(2,1)S(1)} %pad_maximum_fusion.6), channel_id=1, source_target_pairs={{0,8},{1,9},{2,10},{3,11},{4,12},{5,13},{6,14},{7,15},{8,0},{9,1},... | collective-permute-start | bytes 983048 | tf_op jit(solution)/shard_map/ppermute | solution.py:256
  229.1 1.8 collective-permute-start.29
  230.9 3.6 %collective-permute-done.27 = bf16[2,160,512]{2,1,0:T(8,128)(2,1)S(1)} collective-permute-done((bf16[2,160,512]{2,1,0:T(8,128)(2,1)S(1)}, bf16[2,160,512]{2,1,0:T(8,128)(2,1)S(1)}, u32[]{:S(2)}, u32[]{:S(2)}) %collective-permute-start.27) | collective-permute-done | bytes 327712 | tf_op jit(solution)/shard_map/ppermute | solution.py:256
  234.6 5.1 %collective-permute-start.28 = (bf16[1,160,512]{2,1,0:T(8,128)(2,1)S(1)}, bf16[1,160,512]{2,1,0:T(8,128)(2,1)S(1)}, u32[]{:S(2)}, u32[]{:S(2)}) collective-permute-start(bf16[1,160,512]{2,1,0:T(8,128)(2,1)S(1)} %slice.174), channel_id=1, source_target_pairs={{0,16},{1,17},{2,18},{3,19},{4,20},{5,21},{6,22},{7,23},{8,24},{9,... | collective-permute-start | bytes 491528 | tf_op jit(solution)/shard_map/ppermute | solution.py:256
  240.2 4.0 %collective-permute-done.28 = bf16[1,160,512]{2,1,0:T(8,128)(2,1)S(1)} collective-permute-done((bf16[1,160,512]{2,1,0:T(8,128)(2,1)S(1)}, bf16[1,160,512]{2,1,0:T(8,128)(2,1)S(1)}, u32[]{:S(2)}, u32[]{:S(2)}) %collective-permute-start.28) | collective-permute-done | bytes 163872 | tf_op jit(solution)/shard_map/ppermute | solution.py:256
  (148 shorter events, 24.0 us)
Async XLA Ops:
  0.6 26.7 %copy-start.32 = (f32[16]{0:T(128)S(1)}, f32[16]{0:T(128)}, u32[]{:S(2)}) copy-start(f32[16]{0:T(128)} %param.22) | copy-start | bytes 196
  0.7 26.7 %copy-start.33 = (f32[16]{0:T(128)S(1)}, f32[16]{0:T(128)}, u32[]{:S(2)}) copy-start(f32[16]{0:T(128)} %param.23) | copy-start | bytes 196
  5.1 11.7 %collective-permute-start.7 = (bf16[1,160,512]{2,1,0:T(8,128)(2,1)S(1)}, bf16[1,160,512]{2,1,0:T(8,128)(2,1)S(1)}, u32[]{:S(2)}, u32[]{:S(2)}) collective-permute-start(bf16[1,160,512]{2,1,0:T(8,128)(2,1)S(1)} %bitcast.30), channel_id=1, source_target_pairs={{0,16},{1,17},{2,18},{3,19},{4,20},{5,21},{6,22},{7,23},{8,24},{9,... | collective-permute-start | bytes 491528 | tf_op jit(solution)/shard_map/ppermute | solution.py:256
  16.9 20.0 %copy-start.31 = (bf16[3,32,256]{2,1,0:T(8,128)(2,1)S(1)}, bf16[3,32,256]{2,1,0:T(8,128)(2,1)}, u32[]{:S(2)}) copy-start(bf16[3,32,256]{2,1,0:T(8,128)(2,1)} %param.20) | copy-start | bytes 147460
  16.9 9.0 %collective-permute-start.8 = (bf16[2,160,512]{2,1,0:T(8,128)(2,1)S(1)}, bf16[2,160,512]{2,1,0:T(8,128)(2,1)S(1)}, u32[]{:S(2)}, u32[]{:S(2)}) collective-permute-start(bf16[2,160,512]{2,1,0:T(8,128)(2,1)S(1)} %pad_maximum_fusion.7), channel_id=1, source_target_pairs={{0,8},{1,9},{2,10},{3,11},{4,12},{5,13},{6,14},{7,15},{8,0},{9,1},... | collective-permute-start | bytes 983048 | tf_op jit(solution)/shard_map/ppermute | solution.py:256
  26.0 9.4 %collective-permute-start.9 = (bf16[4,96,512]{2,1,0:T(8,128)(2,1)S(1)}, bf16[4,96,512]{2,1,0:T(8,128)(2,1)S(1)}, u32[]{:S(2)}, u32[]{:S(2)}) collective-permute-start(bf16[4,96,512]{2,1,0:T(8,128)(2,1)S(1)} %slice.156), channel_id=1, source_target_pairs={{0,4},{1,5},{2,6},{3,7},{4,0},{5,1},{6,2},{7,3},{8,12},{9,13},{10,... | collective-permute-start | bytes 1179656 | tf_op jit(solution)/shard_map/ppermute | solution.py:256
  27.4 9.4 %collective-permute-start = (bf16[1,64]{1,0:T(2,128)(2,1)S(1)}, bf16[1,64]{1,0:T(2,128)(2,1)S(1)}, u32[]{:S(2)}, u32[]{:S(2)}) collective-permute-start(bf16[1,64]{1,0:T(2,128)(2,1)S(1)} %maximum_bitcast_fusion.1), channel_id=1, source_target_pairs={{0,1},{1,0},{2,3},{3,2},{4,5},{5,4},{6,7},{7,6},{8,9},{9,8},{10,11... | collective-permute-start | bytes 392 | tf_op jit(solution)/shard_map/ppermute | solution.py:256
  35.5 24.3 %copy-start.2 = (bf16[512,512]{1,0:T(8,128)(2,1)S(1)}, bf16[512,512]{1,0:T(8,128)(2,1)}, u32[]{:S(2)}) copy-start(bf16[512,512]{1,0:T(8,128)(2,1)} %atoms_ref.3) | copy-start | bytes 1572868
  35.5 26.0 %collective-permute-start.10 = (bf16[8,96,512]{2,1,0:T(8,128)(2,1)S(1)}, bf16[8,96,512]{2,1,0:T(8,128)(2,1)S(1)}, u32[]{:S(2)}, u32[]{:S(2)}) collective-permute-start(bf16[8,96,512]{2,1,0:T(8,128)(2,1)S(1)} %pad_maximum_fusion.2), channel_id=1, source_target_pairs={{0,1},{1,0},{2,3},{3,2},{4,5},{5,4},{6,7},{7,6},{8,9},{9,8},{10,11... | collective-permute-start | bytes 2359304 | tf_op jit(solution)/shard_map/ppermute | solution.py:256
  36.9 6.8 %collective-permute-start.1 = (bf16[1,112,256]{2,1,0:T(8,128)(2,1)S(1)}, bf16[1,112,256]{2,1,0:T(8,128)(2,1)S(1)}, u32[]{:S(2)}, u32[]{:S(2)}) collective-permute-start(bf16[1,112,256]{2,1,0:T(8,128)(2,1)S(1)} %maximum_bitcast_fusion), channel_id=1, source_target_pairs={{0,16},{2,18},{4,20},{6,22},{8,24},{10,26},{12,28},{14,30},{16,0},... | collective-permute-start | bytes 172040 | tf_op jit(solution)/shard_map/ppermute | solution.py:256
  41.5 16.6 %collective-permute-start.12 = (bf16[4,64,512]{2,1,0:T(8,128)(2,1)S(1)}, bf16[4,64,512]{2,1,0:T(8,128)(2,1)S(1)}, u32[]{:S(2)}, u32[]{:S(2)}) collective-permute-start(bf16[4,64,512]{2,1,0:T(8,128)(2,1)S(1)} %pad_maximum_fusion.8), channel_id=1, source_target_pairs={{0,1},{1,0},{2,3},{3,2},{4,5},{5,4},{6,7},{7,6},{8,9},{9,8},{10,11... | collective-permute-start | bytes 786440 | tf_op jit(solution)/shard_map/ppermute | solution.py:256
  43.8 4.9 %collective-permute-start.2 = (bf16[2,112,256]{2,1,0:T(8,128)(2,1)S(1)}, bf16[2,112,256]{2,1,0:T(8,128)(2,1)S(1)}, u32[]{:S(2)}, u32[]{:S(2)}) collective-permute-start(bf16[2,112,256]{2,1,0:T(8,128)(2,1)S(1)} %pad_maximum_fusion.12), channel_id=1, source_target_pairs={{0,8},{2,10},{4,12},{6,14},{8,0},{10,2},{12,4},{14,6},{16,24},{18,... | collective-permute-start | bytes 344072 | tf_op jit(solution)/shard_map/ppermute | solution.py:256
  48.7 14.1 %collective-permute-start.3 = (bf16[4,112,256]{2,1,0:T(8,128)(2,1)S(1)}, bf16[4,112,256]{2,1,0:T(8,128)(2,1)S(1)}, u32[]{:S(2)}, u32[]{:S(2)}) collective-permute-start(bf16[4,112,256]{2,1,0:T(8,128)(2,1)S(1)} %pad_maximum_fusion.10), channel_id=1, source_target_pairs={{0,4},{2,6},{4,0},{6,2},{8,12},{10,14},{12,8},{14,10},{16,20},{18,... | collective-permute-start | bytes 688136 | tf_op jit(solution)/shard_map/ppermute | solution.py:256
  58.1 10.5 %collective-permute-start.13 = (bf16[8,64,512]{2,1,0:T(8,128)(2,1)S(1)}, bf16[8,64,512]{2,1,0:T(8,128)(2,1)}, u32[]{:S(2)}, u32[]{:S(2)}) collective-permute-start(bf16[8,64,512]{2,1,0:T(8,128)(2,1)S(1)} %pad_maximum_fusion.4), channel_id=1, source_target_pairs={{0,4},{1,5},{2,6},{3,7},{4,0},{5,1},{6,2},{7,3},{8,12},{9,13},{10,... | collective-permute-start | bytes 1572872 | tf_op jit(solution)/shard_map/ppermute | solution.py:256
  59.8 26.6 %collective-permute-start.5 = (bf16[512,512]{1,0:T(8,128)(2,1)S(1)}, bf16[512,512]{1,0:T(8,128)(2,1)S(1)}, u32[]{:S(2)}, u32[]{:S(2)}) collective-permute-start(bf16[512,512]{1,0:T(8,128)(2,1)S(1)} %copy-done.2), channel_id=1, source_target_pairs={{0,1},{1,0},{2,3},{3,2},{4,5},{5,4},{6,7},{7,6},{8,9},{9,8},{10,11... | collective-permute-start | bytes 1572872 | tf_op jit(solution)/shard_map/ppermute | solution.py:256
  62.8 49.1 %collective-permute-start.11 = (bf16[16,96,512]{2,1,0:T(8,128)(2,1)}, bf16[16,96,512]{2,1,0:T(8,128)(2,1)}, u32[]{:S(2)}, u32[]{:S(2)}) collective-permute-start(bf16[16,96,512]{2,1,0:T(8,128)(2,1)} %pad_maximum_fusion.a0_ref), channel_id=1, source_target_pairs={{0,2},{1,3},{2,0},{3,1},{4,6},{5,7},{6,4},{7,5},{8,10},{9,11},{10,... | collective-permute-start | bytes 4718600 | tf_op jit(solution)/shard_map/ppermute | solution.py:256
  62.8 8.5 %collective-permute-start.4 = (bf16[8,112,256]{2,1,0:T(8,128)(2,1)S(1)}, bf16[8,112,256]{2,1,0:T(8,128)(2,1)}, u32[]{:S(2)}, u32[]{:S(2)}) collective-permute-start(bf16[8,112,256]{2,1,0:T(8,128)(2,1)S(1)} %pad_maximum_fusion.5.near_ref), channel_id=1, source_target_pairs={{0,2},{2,0},{4,6},{6,4},{8,10},{10,8},{12,14},{14,12},{16,18},{18,... | collective-permute-start | bytes 1376264 | tf_op jit(solution)/shard_map/ppermute | solution.py:256
  63.5 10.8 %copy-start.18 = (bf16[2,1,16,256]{3,2,1,0:T(8,128)(2,1)S(1)}, bf16[2,1,16,256]{3,2,1,0:T(8,128)(2,1)}, u32[]{:S(2)}) copy-start(bf16[2,1,16,256]{3,2,1,0:T(8,128)(2,1)} %constant.32.clone.mask_ref) | copy-start | bytes 49156
  63.5 10.8 %copy-start.21 = (s32[4]{0:T(128)S(1)}, s32[4]{0:T(128)}, u32[]{:S(2)}) copy-start(s32[4]{0:T(128)} %cnt_ref.11) | copy-start | bytes 52
  70.8 41.1 %collective-permute-start.14 = (bf16[16,64,512]{2,1,0:T(8,128)(2,1)}, bf16[16,64,512]{2,1,0:T(8,128)(2,1)}, u32[]{:S(2)}, u32[]{:S(2)}) collective-permute-start(bf16[16,64,512]{2,1,0:T(8,128)(2,1)} %pad_maximum_fusion.1.b0_ref), channel_id=1, source_target_pairs={{0,2},{1,3},{2,0},{3,1},{4,6},{5,7},{6,4},{7,5},{8,10},{9,11},{10,... | collective-permute-start | bytes 3145736 | tf_op jit(solution)/shard_map/ppermute | solution.py:256
  100.7 10.3 %copy-start.5 = (bf16[512,256]{1,0:T(8,128)(2,1)}, bf16[512,256]{1,0:T(8,128)(2,1)S(1)}, u32[]{:S(2)}) copy-start(bf16[512,256]{1,0:T(8,128)(2,1)S(1)} %get-tuple-element.57.mixed_ref) | copy-start | bytes 786436
  100.7 11.2 %collective-permute-start.6 = (bf16[512,256]{1,0:T(8,128)(2,1)S(1)}, bf16[512,256]{1,0:T(8,128)(2,1)S(1)}, u32[]{:S(2)}, u32[]{:S(2)}) collective-permute-start(bf16[512,256]{1,0:T(8,128)(2,1)S(1)} %get-tuple-element.57.mixed_ref), channel_id=1, source_target_pairs={{0,1},{1,0},{2,3},{3,2},{4,5},{5,4},{6,7},{7,6},{8,9},{9,8},{10,11... | collective-permute-start | bytes 786440 | tf_op jit(solution)/shard_map/ppermute | solution.py:256
  112.5 19.4 %copy-start.1 = (bf16[3,512,256]{2,1,0:T(8,128)(2,1)S(1)}, bf16[3,512,256]{2,1,0:T(8,128)(2,1)}, u32[]{:S(2)}) copy-start(bf16[3,512,256]{2,1,0:T(8,128)(2,1)} %get-tuple-element.49.w_ref) | copy-start | bytes 2359300
  112.5 19.4 %copy-start.17 = (bf16[2,1,16,256]{3,2,1,0:T(8,128)(2,1)S(1)}, bf16[2,1,16,256]{3,2,1,0:T(8,128)(2,1)}, u32[]{:S(2)}) copy-start(bf16[2,1,16,256]{3,2,1,0:T(8,128)(2,1)} %constant.33.clone.mask_ref) | copy-start | bytes 49156
  130.0 55.6 %collective-permute-start.21 = (bf16[16,96,512]{2,1,0:T(8,128)(2,1)}, bf16[16,96,512]{2,1,0:T(8,128)(2,1)S(1)}, u32[]{:S(2)}, u32[]{:S(2)}) collective-permute-start(bf16[16,96,512]{2,1,0:T(8,128)(2,1)} %get-tuple-element.85), channel_id=1, source_target_pairs={{0,2},{1,3},{2,0},{3,1},{4,6},{5,7},{6,4},{7,5},{8,10},{9,11},{10,... | collective-permute-start | bytes 4718600 | tf_op jit(solution)/shard_map/ppermute | solution.py:256
  130.2 53.7 %collective-permute-start.24 = (bf16[16,64,512]{2,1,0:T(8,128)(2,1)}, bf16[16,64,512]{2,1,0:T(8,128)(2,1)S(1)}, u32[]{:S(2)}, u32[]{:S(2)}) collective-permute-start(bf16[16,64,512]{2,1,0:T(8,128)(2,1)} %get-tuple-element.87), channel_id=1, source_target_pairs={{0,2},{1,3},{2,0},{3,1},{4,6},{5,7},{6,4},{7,5},{8,10},{9,11},{10,... | collective-permute-start | bytes 3145736 | tf_op jit(solution)/shard_map/ppermute | solution.py:256
  131.5 14.5 %collective-permute-start.15 = (bf16[512,256]{1,0:T(8,128)(2,1)}, bf16[512,256]{1,0:T(8,128)(2,1)S(1)}, u32[]{:S(2)}, u32[]{:S(2)}) collective-permute-start(bf16[512,256]{1,0:T(8,128)(2,1)} %get-tuple-element.68), channel_id=1, source_target_pairs={{0,1},{1,0},{2,3},{3,2},{4,5},{5,4},{6,7},{7,6},{8,9},{9,8},{10,11... | collective-permute-start | bytes 786440 | tf_op jit(solution)/shard_map/ppermute | solution.py:256
  132.9 13.1 %copy-start.6 = (bf16[512,256]{1,0:T(8,128)(2,1)S(1)}, bf16[512,256]{1,0:T(8,128)(2,1)}, u32[]{:S(2)}) copy-start(bf16[512,256]{1,0:T(8,128)(2,1)} %copy-done.5) | copy-start | bytes 786436
  146.0 20.6 %copy-start.8 = (f32[256,256]{1,0:T(8,128)S(1)}, f32[256,256]{1,0:T(8,128)}, u32[]{:S(2)}) copy-start(f32[256,256]{1,0:T(8,128)} %copy-done.7) | copy-start | bytes 786436
  166.6 12.2 %copy-start.14 = (bf16[512,256]{1,0:T(8,128)(2,1)S(1)}, bf16[512,256]{1,0:T(8,128)(2,1)}, u32[]{:S(2)}) copy-start(bf16[512,256]{1,0:T(8,128)(2,1)} %copy-done.13) | copy-start | bytes 786436
  166.6 12.2 %copy-start.16 = (bf16[512,256]{1,0:T(8,128)(2,1)S(1)}, bf16[512,256]{1,0:T(8,128)(2,1)}, u32[]{:S(2)}) copy-start(bf16[512,256]{1,0:T(8,128)(2,1)} %copy-done.15) | copy-start | bytes 786436
  166.6 12.2 %copy-start.22 = (s32[2]{0:T(128)S(1)}, s32[2]{0:T(128)}, u32[]{:S(2)}) copy-start(s32[2]{0:T(128)} %pad_add_fusion.me_ref) | copy-start | bytes 28
  180.4 1.8 collective-permute-start.17
  180.5 15.0 %collective-permute-start.16 = (bf16[512,512]{1,0:T(8,128)(2,1)}, bf16[512,512]{1,0:T(8,128)(2,1)S(1)}, u32[]{:S(2)}, u32[]{:S(2)}) collective-permute-start(bf16[512,512]{1,0:T(8,128)(2,1)} %get-tuple-element.74), channel_id=1, source_target_pairs={{0,1},{1,0},{2,3},{3,2},{4,5},{5,4},{6,7},{7,6},{8,9},{9,8},{10,11... | collective-permute-start | bytes 1572872 | tf_op jit(solution)/shard_map/ppermute | solution.py:256
  182.3 7.8 %collective-permute-start.18 = (bf16[4,96,256]{2,1,0:T(8,128)(2,1)S(1)}, bf16[4,96,256]{2,1,0:T(8,128)(2,1)S(1)}, u32[]{:S(2)}, u32[]{:S(2)}) collective-permute-start(bf16[4,96,256]{2,1,0:T(8,128)(2,1)S(1)} %slice.158), channel_id=1, source_target_pairs={{0,4},{2,6},{4,0},{6,2},{8,12},{10,14},{12,8},{14,10},{16,20},{18,... | collective-permute-start | bytes 589832 | tf_op jit(solution)/shard_map/ppermute | solution.py:256
  185.1 18.6 %collective-permute-start.25 = (bf16[8,64,512]{2,1,0:T(8,128)(2,1)}, bf16[8,64,512]{2,1,0:T(8,128)(2,1)}, u32[]{:S(2)}, u32[]{:S(2)}) collective-permute-start(bf16[8,64,512]{2,1,0:T(8,128)(2,1)} %slice.168), channel_id=1, source_target_pairs={{0,4},{1,5},{2,6},{3,7},{4,0},{5,1},{6,2},{7,3},{8,12},{9,13},{10,... | collective-permute-start | bytes 1572872 | tf_op jit(solution)/shard_map/ppermute | solution.py:256
  187.3 8.2 %copy-start.20 = (f32[2,512]{1,0:T(2,128)S(1)}, f32[2,512]{1,0:T(2,128)}, u32[]{:S(2)}) copy-start(f32[2,512]{1,0:T(2,128)} %get-tuple-element.50.gains_ref) | copy-start | bytes 12292
  188.3 24.2 %collective-permute-start.22 = (bf16[8,96,512]{2,1,0:T(8,128)(2,1)}, bf16[8,96,512]{2,1,0:T(8,128)(2,1)}, u32[]{:S(2)}, u32[]{:S(2)}) collective-permute-start(bf16[8,96,512]{2,1,0:T(8,128)(2,1)} %slice.164), channel_id=1, source_target_pairs={{0,1},{1,0},{2,3},{3,2},{4,5},{5,4},{6,7},{7,6},{8,9},{9,8},{10,11... | collective-permute-start | bytes 2359304 | tf_op jit(solution)/shard_map/ppermute | solution.py:256
  190.2 6.9 %collective-permute-start.19 = (bf16[2,96,256]{2,1,0:T(8,128)(2,1)S(1)}, bf16[2,96,256]{2,1,0:T(8,128)(2,1)S(1)}, u32[]{:S(2)}, u32[]{:S(2)}) collective-permute-start(bf16[2,96,256]{2,1,0:T(8,128)(2,1)S(1)} %slice.160), channel_id=1, source_target_pairs={{0,8},{2,10},{4,12},{6,14},{8,0},{10,2},{12,4},{14,6},{16,24},{18,... | collective-permute-start | bytes 294920 | tf_op jit(solution)/shard_map/ppermute | solution.py:256
  195.5 8.2 %copy-start.26 = (bf16[16,64,512]{2,1,0:T(8,128)(2,1)S(1)}, bf16[16,64,512]{2,1,0:T(8,128)(2,1)}, u32[]{:S(2)}) copy-start(bf16[16,64,512]{2,1,0:T(8,128)(2,1)} %copy-done.25) | copy-start | bytes 3145732
  197.1 15.3 %copy-start.24 = (bf16[16,96,512]{2,1,0:T(8,128)(2,1)S(1)}, bf16[16,96,512]{2,1,0:T(8,128)(2,1)}, u32[]{:S(2)}) copy-start(bf16[16,96,512]{2,1,0:T(8,128)(2,1)} %copy-done.23) | copy-start | bytes 4718596
  197.1 18.1 %collective-permute-start.20 = (bf16[1,96,256]{2,1,0:T(8,128)(2,1)S(1)}, bf16[1,96,256]{2,1,0:T(8,128)(2,1)S(1)}, u32[]{:S(2)}, u32[]{:S(2)}) collective-permute-start(bf16[1,96,256]{2,1,0:T(8,128)(2,1)S(1)} %slice.162), channel_id=1, source_target_pairs={{0,16},{2,18},{4,20},{6,22},{8,24},{10,26},{12,28},{14,30},{16,0},... | collective-permute-start | bytes 147464 | tf_op jit(solution)/shard_map/ppermute | solution.py:256
  204.9 12.6 %collective-permute-start.26 = (bf16[4,64,512]{2,1,0:T(8,128)(2,1)S(1)}, bf16[4,64,512]{2,1,0:T(8,128)(2,1)S(1)}, u32[]{:S(2)}, u32[]{:S(2)}) collective-permute-start(bf16[4,64,512]{2,1,0:T(8,128)(2,1)S(1)} %slice.170), channel_id=1, source_target_pairs={{0,1},{1,0},{2,3},{3,2},{4,5},{5,4},{6,7},{7,6},{8,9},{9,8},{10,11... | collective-permute-start | bytes 786440 | tf_op jit(solution)/shard_map/ppermute | solution.py:256
  213.8 10.3 %collective-permute-start.23 = (bf16[4,96,512]{2,1,0:T(8,128)(2,1)S(1)}, bf16[4,96,512]{2,1,0:T(8,128)(2,1)S(1)}, u32[]{:S(2)}, u32[]{:S(2)}) collective-permute-start(bf16[4,96,512]{2,1,0:T(8,128)(2,1)S(1)} %slice.166), channel_id=1, source_target_pairs={{0,4},{1,5},{2,6},{3,7},{4,0},{5,1},{6,2},{7,3},{8,12},{9,13},{10,... | collective-permute-start | bytes 1179656 | tf_op jit(solution)/shard_map/ppermute | solution.py:256
  224.3 10.2 %collective-permute-start.27 = (bf16[2,160,512]{2,1,0:T(8,128)(2,1)S(1)}, bf16[2,160,512]{2,1,0:T(8,128)(2,1)S(1)}, u32[]{:S(2)}, u32[]{:S(2)}) collective-permute-start(bf16[2,160,512]{2,1,0:T(8,128)(2,1)S(1)} %pad_maximum_fusion.6), channel_id=1, source_target_pairs={{0,8},{1,9},{2,10},{3,11},{4,12},{5,13},{6,14},{7,15},{8,0},{9,1},... | collective-permute-start | bytes 983048 | tf_op jit(solution)/shard_map/ppermute | solution.py:256
  229.1 15.9 %copy-start.30 = (bf16[16,2048]{1,0:T(8,128)(2,1)S(1)}, bf16[16,2048]{1,0:T(8,128)(2,1)}, u32[]{:S(2)}) copy-start(bf16[16,2048]{1,0:T(8,128)(2,1)} %param.24) | copy-start | bytes 196612
  229.1 10.6 %collective-permute-start.29 = (f32[16]{0:T(128)S(1)}, f32[16]{0:T(128)S(1)}, u32[]{:S(2)}, u32[]{:S(2)}) collective-permute-start(f32[16]{0:T(128)S(1)} %dynamic-slice_bitcast_fusion), channel_id=1, source_target_pairs={{0,1},{1,0},{2,3},{3,2},{4,5},{5,4},{6,7},{7,6},{8,9},{9,8},{10,11... | collective-permute-start | bytes 200 | tf_op jit(solution)/shard_map/ppermute | solution.py:256
  234.6 9.6 %collective-permute-start.28 = (bf16[1,160,512]{2,1,0:T(8,128)(2,1)S(1)}, bf16[1,160,512]{2,1,0:T(8,128)(2,1)S(1)}, u32[]{:S(2)}, u32[]{:S(2)}) collective-permute-start(bf16[1,160,512]{2,1,0:T(8,128)(2,1)S(1)} %slice.174), channel_id=1, source_target_pairs={{0,16},{1,17},{2,18},{3,19},{4,20},{5,21},{6,22},{7,23},{8,24},{9,... | collective-permute-start | bytes 491528 | tf_op jit(solution)/shard_map/ppermute | solution.py:256
  (17 other events, 49.1 us)

commit v2 on v1

--- a/solution.py
+++ b/solution.py
@@ -588,7 +588,8 @@
             for k in range(4):
                 win_s[k, pl.ds(pl.multiple_of(owner * rows, rows), rows), :] = ref[q, k * rows : (k + 1) * rows, :]
             at = pl.multiple_of((owner // 2) * e_rows, e_rows)
-            ow_s[relative(p, bits_a) & 1, pl.ds(at, e_rows), :] = ref[q, 4 * rows : 4 * rows + e_rows, :width]
+            for k in range(2):
+                ow_s[relative(p, bits_a) & 1, pl.ds(at + k * rows, rows), :] = ref[q, 4 * rows :, k * width : (k + 1) * width]
         for p, owner, (ref, q) in shards(bits_b, b0_ref, b1_ref):
             wout_s[pl.ds(pl.multiple_of(owner * ff_rows, ff_rows), ff_rows), :] = ref[q]
         first_sum = (
@@ -641,8 +642,8 @@
             for k in range(4):
                 ref[q, k * rows : (k + 1) * rows, :] = win_s[k, pl.ds(pl.multiple_of(owner * rows, rows), rows), :]
             at = pl.multiple_of((owner // 2) * e_rows, e_rows)
-            ref[q, 4 * rows : 4 * rows + e_rows, :width] = ow_s[relative(p, bits_a) & 1, pl.ds(at, e_rows), :]
-            ref[q, 4 * rows : 4 * rows + e_rows, width:] = jnp.zeros((e_rows, dim - width), BF16)
+            for k in range(2):
+                ref[q, 4 * rows :, k * width : (k + 1) * width] = ow_s[relative(p, bits_a) & 1, pl.ds(at + k * rows, rows), :]
         for p, owner, (ref, q) in shards(bits_b, gb0_ref, gb1_ref):
             ref[q] = wout_s[pl.ds(pl.multiple_of(owner * ff_rows, ff_rows), ff_rows), :]
 
@@ -792,18 +793,28 @@
     over_head = lambda x: swap(x, "head", 2, 1)
     over_both = lambda x, bit: swap(x, BOTH, 2 * batch, bit)
 
+    tie = lax.optimization_barrier
+
     def split_gain(gain):
         high = gain.astype(BF16)
         return [high, (gain - high.astype(F32)).astype(BF16)]
 
     gain_row = jnp.concatenate(split_gain(ln1_gain) + split_gain(ln2_gain))[None]
     gain_row = jnp.concatenate([gain_row, over_head(gain_row)], 1)
-    atoms_other = over_head(atoms)
     tail = jnp.pad(gain_row, ((0, 15), (0, width - gain_row.shape[1])))
     gathered = jnp.concatenate([qkv_weight.reshape(-1, width), tail], 0)[None]
-    for bit in batch_bits[:-1]:
+    for bit in far_bits:
         gathered = join(gathered, over_batch(gathered, bit))
-    far = over_batch(gathered, batch_bits[-1])
+    e_rows = out_weight.shape[0]
+    blocks = w_in.shape[1] // dim
+    in_rows = [w_in[:, k * dim : (k + 1) * dim] for k in range(blocks)]
+    out_rows = jnp.concatenate([out_weight[: e_rows // 2], out_weight[e_rows // 2 :]], 1)
+    bulk = jnp.concatenate([*in_rows, out_rows, w_out], 0)[None]
+    cut = bulk.shape[1] - w_out.shape[0]
+    gathered, bulk = tie((gathered, bulk))
+    atoms_other = over_head(atoms)
+    gathered = join(gathered, over_batch(gathered, 2))
+    far = over_batch(gathered, 1)
     me_batch = jnp.stack([b, h])
     weights, gains = pl.pallas_call(
         partial(prep_kernel, bits=batch_bits, heads_bits=1, shard=shard),
@@ -818,67 +829,75 @@
         name="prepare",
     )(me_batch, gathered, far)
 
-    e_rows = out_weight.shape[0]
-    blocks = w_in.shape[1] // dim
-    in_rows = [w_in[:, k * dim : (k + 1) * dim] for k in range(blocks)]
-    out_rows = jnp.pad(out_weight, ((0, 0), (0, dim - width)))
-    bulk = jnp.concatenate([*in_rows, out_rows, w_out], 0)[None]
-    cut = bulk.shape[1] - w_out.shape[0]
-    for bit in bits_a[:nz]:
-        bulk = join(bulk, over_both(bulk, bit))
-    part_a, part_b = bulk[:, :cut], bulk[:, cut:]
-    for bit_a, bit_b in zip(bits_a[nz:-1], bits_b[nz:-1]):
-        part_a, part_b = join(part_a, over_both(part_a, bit_a)), join(part_b, over_both(part_b, bit_b))
-    a_pair = (part_a, over_both(part_a, bits_a[-1]))
-    b_pair = (part_b, over_both(part_b, bits_b[-1]))
-
     per = own // length
     mine, theirs = h * per, (1 - h) * per
-    plan = [
-        (mine[None], atoms[:length]),
-        (theirs + jnp.arange(per, dtype=jnp.int32), atoms_other),
-        (mine + jnp.arange(1, per, dtype=jnp.int32), atoms[length:]),
-    ]
+    plan = [(mine, atoms[:length])]
+    plan += [(theirs + k, atoms_other[k * length : (k + 1) * length]) for k in range(per)]
+    plan += [(mine + k, atoms[k * length : (k + 1) * length]) for k in range(1, per)]
+    plan = [(mol[None], rows) for mol, rows in plan]
+    stage_bits = [(bit, bit) for bit in bits_a[:nz]] + list(zip(bits_a[nz:], bits_b[nz:]))
+    parts = (bulk,)
+
+    def send_stage(parts, k):
+        return tuple(over_both(x, bit) for x, bit in zip(parts, stage_bits[k]))
+
+    received = send_stage(parts, 0)
+    received, gains = tie((received, gains))
+    cnt = counts
     carried = ()
     saved = []
-    for mols, rows in plan:
-        new_pair, exps, *rest = attend_forward_call(mols, counts, rows, weights, gains, pair, carried)
+    for k, (mols, rows) in enumerate(plan):
+        if k < len(stage_bits) - 1:
+            parts = tuple(map(join, parts, received))
+            if k + 1 == nz:
+                parts = (parts[0][:, :cut], parts[0][:, cut:])
+            cnt, parts = tie((cnt, parts))
+        if k < len(stage_bits) - 2:
+            received = send_stage(parts, k + 1)
+        new_pair, exps, *rest = attend_forward_call(mols, cnt, rows, weights, gains, pair, carried)
+        if k < len(stage_bits) - 2:
+            received, rest = tie((received, rest))
         carried = (new_pair, exps)
         saved.append(rest)
-    mixed_other = over_head(saved[1][2])
-    mixed_mine = jnp.concatenate([saved[0][2], saved[2][2]], 0)
+    a_pair = (parts[0], over_both(parts[0], bits_a[-1]))
+    b_pair = (parts[1], over_both(parts[1], bits_b[-1]))
+    mixed_theirs = jnp.concatenate([s[2] for s in saved[1 : 1 + per]], 0)
+    mixed_other = over_head(mixed_theirs)
+    mixed_mine = jnp.concatenate([saved[0][2], *[s[2] for s in saved[1 + per :]]], 0)
 
     me = (2 * b + h)[None]
     output, first, gm_mine, gm_other, ga0, ga1, gb0, gb1 = layer_call(
         me, atoms, mixed_mine, mixed_other, out_cot, gains, a_pair, b_pair, bits_a, bits_b
     )
     gm_received = over_head(gm_other)
-    part_a = add(ga0, over_both(ga1, bits_a[-1]))
-    part_b = add(gb0, over_both(gb1, bits_b[-1]))
-    for bit_a, bit_b in zip(bits_a[-2:nz - 1:-1], bits_b[-2:nz - 1:-1]):
-        (keep_a, send_a), (keep_b, send_b) = halves(part_a), halves(part_b)
-        part_a, part_b = add(keep_a, over_both(send_a, bit_a)), add(keep_b, over_both(send_b, bit_b))
-    bulk = jnp.concatenate([part_a, part_b], 1)
-    for bit in bits_a[nz - 1 :: -1]:
-        keep, send = halves(bulk)
-        bulk = add(keep, over_both(send, bit))
-    bulk = bulk[0].astype(F32)
-    shard_rows = w_in.shape[0]
-    in_grad = jnp.concatenate([bulk[k * shard_rows : (k + 1) * shard_rows] for k in range(blocks)], 1)
-    out_grad = bulk[blocks * shard_rows : cut, :width]
-    outer_grad = bulk[cut:]
-    gain_two_grad = jnp.sum(in_grad * w_in.astype(F32), 1) / ln2_gain
-
-    gm_parts = [gm_mine[:length], gm_received, gm_mine[length:]]
+
+    def scatter_stage(parts, k):
+        if k == nz - 1:
+            parts = (jnp.concatenate(parts, 1),)
+        return tuple(
+            add(keep, over_both(send, bit))
+            for (keep, send), bit in zip(map(halves, parts), stage_bits[k])
+        )
+
+    parts = (add(ga0, over_both(ga1, bits_a[-1])), add(gb0, over_both(gb1, bits_b[-1])))
+    gm_parts = [gm_mine[:length]]
+    gm_parts += [gm_received[k * length : (k + 1) * length] for k in range(per)]
+    gm_parts += [gm_mine[k * length : (k + 1) * length] for k in range(1, per)]
     carried = ()
     grads = []
-    for (mols, _), gm, (hid_t, qkv, mixed, inverse) in zip(plan, gm_parts, saved):
+    stage = len(stage_bits) - 2
+    cnt = counts
+    for k, ((mols, _), gm, (hid_t, qkv, mixed, inverse)) in enumerate(zip(plan, gm_parts, saved)):
+        if k > 0:
+            cnt, parts = tie((cnt, parts))
+            parts = scatter_stage(parts, stage)
+            stage -= 1
         pair_grad, *rest = attend_backward_call(
-            mols, counts, gm, mixed, inverse, qkv, weights, exps, pair_cot, carried
+            mols, cnt, gm, mixed, inverse, qkv, weights, exps, pair_cot, carried
         )
         carried = (pair_grad,)
         grads.append(rest)
-    hidden_received = over_head(grads[1][1])
+    hidden_received = over_head(jnp.concatenate([g[1] for g in grads[1 : 1 + per]], 0))
     near, far = project_grad_call(
         me_batch, [s[0] for s in saved], [g[0] for g in grads], batch_bits
     )
@@ -891,7 +910,16 @@
     gain_mine = lax.dynamic_index_in_dim(gain_part, h, 0, False)
     gain_other = over_head(lax.dynamic_index_in_dim(gain_part, 1 - h, 0, False))
     gain_one_grad = (gain_mine + gain_other) / ln1_gain
-    atoms_grad = last_call(atoms, gains, first, grads[0][1], grads[2][1], hidden_received)
+    atoms_grad = last_call(atoms, gains, first, grads[0][1], grads[-1][1], hidden_received)
+    while stage >= 0:
+        parts = scatter_stage(parts, stage)
+        stage -= 1
+    bulk = parts[0][0].astype(F32)
+    shard_rows = w_in.shape[0]
+    in_grad = jnp.concatenate([bulk[k * shard_rows : (k + 1) * shard_rows] for k in range(blocks)], 1)
+    out_grad = jnp.concatenate([bulk[blocks * shard_rows : cut, k * width : (k + 1) * width] for k in range(2)], 0)
+    outer_grad = bulk[cut:]
+    gain_two_grad = jnp.sum(in_grad * w_in.astype(F32), 1) / ln2_gain
     return (
         output, new_pair, atoms_grad, pair_grad, qkv_grad, out_grad,
         gain_one_grad, gain_two_grad, in_grad, outer_grad,

time: 248 us -> 207 us (0.83)
  waiting for transfers between devices: 64.1 us -> 36.1 us
  starting transfers between devices: 53.8 us -> 32.8 us
  other arithmetic: 11.8 us -> 17.2 us
  Pallas kernels: 101 us -> 106 us
  local copies, waits for them, and re-layouts: 15.6 us -> 12.5 us
    ppermute x30, waiting for transfers between devices: 64.1 us -> 36.1 us  [swap(): return lax.ppermute(values, axes, [(i, i ^ bit) for i in range(count)])]
    ppermute x30, starting transfers between devices: 53.8 us -> 32.8 us  [swap(): return lax.ppermute(values, axes, [(i, i ^ bit) for i in range(count)])]
    pallas_call x3 -> x4, Pallas kernels: 45.2 us -> 48.7 us  [attend_backward_call(): pl.pallas_call(partial(attend_backward_kernel, hb=hb, groups=groups, scal...]
    concatenate x9 -> x7, other arithmetic: 3.72 us -> 6.58 us  [join(): return jnp.concatenate([values, received], 0)]
    unnamed x75 -> x81, local copies, waits for them, and re-layouts: 10.4 us -> 8.06 us
    pallas_call x3 -> x4, Pallas kernels: 32 us -> 33.6 us  [attend_forward_call(): pl.pallas_call(partial(attend_forward_kernel, hb=hb, groups=groups, scale...]
  transfers between devices with their start and end apart: 30 -> 30, of which waited for: 14 -> 11; matrix products, arithmetic and copies ran while one was open for 5% -> 7% of each run, Pallas kernels for 34% -> 43%
where the time goes in v2:
time: 207 us; the launch traced here: 206 us
  Pallas kernels  106 us (51%)
  waiting for transfers between devices  36.1 us (17%)
  starting transfers between devices  32.8 us (16%)
  other arithmetic  17.2 us (8%)
  local copies, waits for them, and re-layouts  12.5 us (6%)
    pallas_call x4, Pallas kernels, attend_backward_call(): pl.pallas_call(partial(attend_backward_kernel, hb=hb, groups=groups, scal...  48.7 us
    ppermute x30, waiting for transfers between devices, swap(): return lax.ppermute(values, axes, [(i, i ^ bit) for i in range(count)])  36.1 us
    pallas_call x4, Pallas kernels, attend_forward_call(): pl.pallas_call(partial(attend_forward_kernel, hb=hb, groups=groups, scale...  33.6 us
    ppermute x30, starting transfers between devices, swap(): return lax.ppermute(values, axes, [(i, i ^ bit) for i in range(count)])  32.8 us
    pallas_call x1, Pallas kernels, layer_call(): pl.pallas_call(partial(layer_kernel, bits_a=bits_a, bits_b=bits_b), grid_...  17.3 us
    unnamed x81, local copies, waits for them, and re-layouts  8.06 us
    concatenate x7, other arithmetic, join(): return jnp.concatenate([values, received], 0)  6.58 us
  transfers between devices with their start and end apart: 30, of which 11 were waited for; matrix products, arithmetic and copies ran while one was open for 7% of the time, Pallas kernels for 43%

profile of v2, /device:TPU:0, one launch (start us, length us, event | category | flops | bytes accessed | tf_op | source)
XLA Modules:
  0.0 206.2 jit_solution(441362865741261529)
XLA Ops:
  1.5 2.9 %collective-permute-start = (bf16[1,64]{1,0:T(2,128)(2,1)S(1)}, bf16[1,64]{1,0:T(2,128)(2,1)S(1)}, u32[]{:S(2)}, u32[]{:S(2)}) collective-permute-start(bf16[1,64]{1,0:T(2,128)(2,1)S(1)} %maximum_bitcast_fusion.1), channel_id=1, source_target_pairs={{0,1},{1,0},{2,3},{3,2},{4,5},{5,4},{6,7},{7,6},{8,9},{9,8},{10,11... | collective-permute-start | bytes 392 | tf_op jit(solution)/shard_map/ppermute | solution.py:256
  7.4 0.8 maximum_bitcast_fusion
  8.2 2.6 %collective-permute-start.1 = (bf16[1,112,256]{2,1,0:T(8,128)(2,1)S(1)}, bf16[1,112,256]{2,1,0:T(8,128)(2,1)S(1)}, u32[]{:S(2)}, u32[]{:S(2)}) collective-permute-start(bf16[1,112,256]{2,1,0:T(8,128)(2,1)S(1)} %maximum_bitcast_fusion), channel_id=1, source_target_pairs={{0,16},{2,18},{4,20},{6,22},{8,24},{10,26},{12,28},{14,30},{16,0},... | collective-permute-start | bytes 172040 | tf_op jit(solution)/shard_map/ppermute | solution.py:256
  11.5 2.0 collective-permute-done.1
  13.5 1.4 collective-permute-start.2
  14.9 0.8 constant_dynamic-update-slice_fusion
  15.8 2.6 %collective-permute-done.2 = bf16[2,112,256]{2,1,0:T(8,128)(2,1)S(1)} collective-permute-done((bf16[2,112,256]{2,1,0:T(8,128)(2,1)S(1)}, bf16[2,112,256]{2,1,0:T(8,128)(2,1)S(1)}, u32[]{:S(2)}, u32[]{:S(2)}) %collective-permute-start.2) | collective-permute-done | bytes 114720 | tf_op jit(solution)/shard_map/ppermute | solution.py:256
  18.4 1.6 collective-permute-start.4
  20.0 4.5 %collective-permute-done.4 = bf16[4,112,256]{2,1,0:T(8,128)(2,1)S(1)} collective-permute-done((bf16[4,112,256]{2,1,0:T(8,128)(2,1)S(1)}, bf16[4,112,256]{2,1,0:T(8,128)(2,1)S(1)}, u32[]{:S(2)}, u32[]{:S(2)}) %collective-permute-start.4) | collective-permute-done | bytes 229408 | tf_op jit(solution)/shard_map/ppermute | solution.py:256
  25.2 2.6 %collective-permute-start.3 = (bf16[1,144,512]{2,1,0:T(8,128)(2,1)S(1)}, bf16[1,144,512]{2,1,0:T(8,128)(2,1)S(1)}, u32[]{:S(2)}, u32[]{:S(2)}) collective-permute-start(bf16[1,144,512]{2,1,0:T(8,128)(2,1)S(1)} %bitcast.35), channel_id=1, source_target_pairs={{0,16},{1,17},{2,18},{3,19},{4,20},{5,21},{6,22},{7,23},{8,24},{9,... | collective-permute-start | bytes 442376 | tf_op jit(solution)/shard_map/ppermute | solution.py:256
  29.2 2.9 %prepare.1 = (bf16[3,512,256]{2,1,0:T(8,128)(2,1)}, f32[2,512]{1,0:T(2,128)}) custom-call(s32[2]{0:T(128)} %pad_add_fusion.me_ref, bf16[8,112,256]{2,1,0:T(8,128)(2,1)} %copy-done.30, bf16[8,112,256]{2,1,0:T(8,128)(2,1)} %copy-done.31), custom_call_target="tpu_custom_call" | custom-call | tf_op jit(solution)/shard_map/prepare/pallas_call | solution.py:819
  32.1 3.1 %collective-permute-done.3 = bf16[1,144,512]{2,1,0:T(8,128)(2,1)S(1)} collective-permute-done((bf16[1,144,512]{2,1,0:T(8,128)(2,1)S(1)}, bf16[1,144,512]{2,1,0:T(8,128)(2,1)S(1)}, u32[]{:S(2)}, u32[]{:S(2)}) %collective-permute-start.3) | collective-permute-done | bytes 147488 | tf_op jit(solution)/shard_map/ppermute | solution.py:256
  36.0 1.1 copy-done
  37.8 8.4 %attend_forward.4 = (bf16[4,32,256,256]{3,2,1,0:T(8,128)(2,1)}, bf16[4,32,256,256]{3,2,1,0:T(8,128)(2,1)}, bf16[512,256]{1,0:T(8,128)(2,1)S(1)}, bf16[3,256,256]...) custom-call(s32[1]{0:T(128)} %bitcast.7.mol_ref, s32[4]{0:T(128)S(1)} %copy-done.24, ...), custom_call_target="tpu_custom_call" | custom-call | flops 2147483648 | bytes 12582912 | tf_op jit(solution)/shard_map/attend_forward/pallas_call | solution.py:417
  46.3 1.5 collective-permute-start.8
  47.8 1.5 collective-permute-start.7
  49.4 8.5 %attend_forward.5 = (bf16[4,32,256,256]{3,2,1,0:T(8,128)(2,1)}, bf16[4,32,256,256]{3,2,1,0:T(8,128)(2,1)}, bf16[512,256]{1,0:T(8,128)(2,1)S(1)}, bf16[3,256,256]...) custom-call(s32[1]{0:T(128)} %bitcast.9.mol_ref, ...), custom_call_target="tpu_custom_call", output_to_operand_aliasing={{0}: (7, {}), {1}: (8, {})} | custom-call | flops 2147483648 | bytes 12582912 | tf_op jit(solution)/shard_map/attend_forward/pallas_call | solution.py:417
  58.6 0.9 pad_maximum_fusion.2
  59.5 0.8 pad_maximum_fusion.3
  61.3 8.3 %attend_forward.6 = (bf16[4,32,256,256]{3,2,1,0:T(8,128)(2,1)}, bf16[4,32,256,256]{3,2,1,0:T(8,128)(2,1)}, bf16[512,256]{1,0:T(8,128)(2,1)S(1)}, bf16[3,256,256]...) custom-call(s32[1]{0:T(128)} %bitcast.10.mol_ref, ...), custom_call_target="tpu_custom_call", output_to_operand_aliasing={{0}: (7, {}), {1}: (8, {})} | custom-call | flops 2147483648 | bytes 12582912 | tf_op jit(solution)/shard_map/attend_forward/pallas_call | solution.py:417
  69.7 4.2 %collective-permute-done.11 = bf16[8,64,512]{2,1,0:T(8,128)(2,1)} collective-permute-done((bf16[8,64,512]{2,1,0:T(8,128)(2,1)}, bf16[8,64,512]{2,1,0:T(8,128)(2,1)}, u32[]{:S(2)}, u32[]{:S(2)}) %collective-permute-start.11) | collective-permute-done | bytes 524320 | tf_op jit(solution)/shard_map/ppermute | solution.py:256
  73.9 2.6 %collective-permute-done.10 = bf16[8,80,512]{2,1,0:T(8,128)(2,1)} collective-permute-done((bf16[8,80,512]{2,1,0:T(8,128)(2,1)}, bf16[8,80,512]{2,1,0:T(8,128)(2,1)}, u32[]{:S(2)}, u32[]{:S(2)}) %collective-permute-start.10) | collective-permute-done | bytes 655392 | tf_op jit(solution)/shard_map/ppermute | solution.py:256
  76.5 2.5 %pad_maximum_fusion.a0_ref = bf16[16,80,512]{2,1,0:T(8,128)(2,1)} fusion(bf16[8,80,512]{2,1,0:T(8,128)(2,1)} %collective-permute-done.10, bf16[8,80,512]{2,1,0:T(8,128)(2,1)} %pad_maximum_fusion.2), kind=kLoop, calls=%fused_computation.2 | loop fusion | flops 655360 | bytes 2621440 | tf_op jit(solution)/shard_map/concatenate | solution.py:764
  78.9 2.3 %pad_maximum_fusion.1.b0_ref = bf16[16,64,512]{2,1,0:T(8,128)(2,1)} fusion(bf16[8,64,512]{2,1,0:T(8,128)(2,1)} %collective-permute-done.11, bf16[8,64,512]{2,1,0:T(8,128)(2,1)} %pad_maximum_fusion.3), kind=kLoop, calls=%fused_computation.4 | loop fusion | flops 524288 | bytes 2097152 | tf_op jit(solution)/shard_map/concatenate | solution.py:764
  82.3 8.4 %attend_forward.7 = (bf16[4,32,256,256]{3,2,1,0:T(8,128)(2,1)}, bf16[4,32,256,256]{3,2,1,0:T(8,128)(2,1)}, bf16[512,256]{1,0:T(8,128)(2,1)S(1)}, bf16[3,256,256]...) custom-call(s32[1]{0:T(128)} %bitcast.8.mol_ref, ...), custom_call_target="tpu_custom_call", output_to_operand_aliasing={{0}: (7, {}), {1}: (8, {})} | custom-call | flops 2147483648 | bytes 12582912 | tf_op jit(solution)/shard_map/attend_forward/pallas_call | solution.py:417
  92.2 17.3 %layer.1 = (bf16[512,512]{1,0:T(8,128)(2,1)}, f32[512,512]{1,0:T(8,128)}, bf16[512,256]{1,0:T(8,128)(2,1)}, bf16[512,256]{1,0:T(8,128)(2,1)}, bf16[16,80,512]{2,...) custom-call(s32[1]{0:T(128)} %bitcast.me_ref, ...), custom_call_target="tpu_custom_call" | custom-call | flops 6442450944 | bytes 8388608 | tf_op jit(solution)/shard_map/layer/pallas_call | solution.py:682
  110.0 1.5 collective-permute-start.21
  111.4 1.0 fusion.13
  112.5 12.1 %attend_backward.4 = (bf16[4,32,256,256]{3,2,1,0:T(8,128)(2,1)}, bf16[3,256,256]{2,1,0:T(8,128)(2,1)S(1)}, bf16[256,512]{1,0:T(8,128)(2,1)S(1)}) custom-call(s32[1]{0:T(128)} %bitcast.7.mol_ref, s32[4]{0:T(128)S(1)} %copy-done.24, bf16[256,256]{1,0:T(8,128)(2,1)S(1)} %get-tuple-element.207.gm_ref, bf16[256,256]{1,0:T(8,128)(2,1)S(1)} %get-tuple-element.111.mixed_ref, ...), custom_call_target="tpu_custom_call" | custom-call | flops 3221225472 | bytes 12582912 | tf_op jit(solution)/shard_map/attend_backward/pallas_call | solution.py:537
  127.8 12.3 %attend_backward.5 = (bf16[4,32,256,256]{3,2,1,0:T(8,128)(2,1)}, bf16[3,256,256]{2,1,0:T(8,128)(2,1)S(1)}, bf16[256,512]{1,0:T(8,128)(2,1)S(1)}) custom-call(s32[1]{0:T(128)} %bitcast.9.mol_ref, s32[4]{0:T(128)S(1)} %copy-done.24, bf16[256,256]{1,0:T(8,128)(2,1)S(1)} %get-tuple-element.204.gm_ref, ...), custom_call_target="tpu_custom_call", output_to_operand_aliasing={{0}: (10, {})} | custom-call | flops 3221225472 | bytes 12582912 | tf_op jit(solution)/shard_map/attend_backward/pallas_call | solution.py:537
  140.3 3.0 %collective-permute-done.17 = bf16[8,80,512]{2,1,0:T(8,128)(2,1)S(1)} collective-permute-done((bf16[8,80,512]{2,1,0:T(8,128)(2,1)S(1)}, bf16[8,80,512]{2,1,0:T(8,128)(2,1)S(1)}, u32[]{:S(2)}, u32[]{:S(2)}) %collective-permute-start.17) | collective-permute-done | bytes 655392 | tf_op jit(solution)/shard_map/ppermute | solution.py:256
  144.2 1.5 collective-permute-start.19
  145.7 12.1 %attend_backward.6 = (bf16[4,32,256,256]{3,2,1,0:T(8,128)(2,1)}, bf16[3,256,256]{2,1,0:T(8,128)(2,1)S(1)}, bf16[256,512]{1,0:T(8,128)(2,1)S(1)}) custom-call(s32[1]{0:T(128)} %bitcast.10.mol_ref, s32[4]{0:T(128)S(1)} %copy-done.24, bf16[256,256]{1,0:T(8,128)(2,1)S(1)} %get-tuple-element.205.gm_ref, ...), custom_call_target="tpu_custom_call", output_to_operand_aliasing={{0}: (10, {})} | custom-call | flops 3221225472 | bytes 12582912 | tf_op jit(solution)/shard_map/attend_backward/pallas_call | solution.py:537
  157.8 0.8 pad_maximum_fusion.4
  158.7 1.4 collective-permute-start.22
  161.1 0.8 collective-permute-start.27
  162.0 12.1 %attend_backward.7 = (bf16[4,32,256,256]{3,2,1,0:T(8,128)(2,1)}, bf16[3,256,256]{2,1,0:T(8,128)(2,1)S(1)}, bf16[256,512]{1,0:T(8,128)(2,1)S(1)}) custom-call(s32[1]{0:T(128)} %bitcast.8.mol_ref, s32[4]{0:T(128)S(1)} %copy-done.24, bf16[256,256]{1,0:T(8,128)(2,1)S(1)} %get-tuple-element.206.gm_ref, ...), custom_call_target="tpu_custom_call", output_to_operand_aliasing={{0}: (10, {})} | custom-call | flops 3221225472 | bytes 12582912 | tf_op jit(solution)/shard_map/attend_backward/pallas_call | solution.py:537
  174.2 2.3 %project_grad.1 = (bf16[8,96,256]{2,1,0:T(8,128)(2,1)S(1)}, bf16[8,96,256]{2,1,0:T(8,128)(2,1)}) custom-call(s32[2]{0:T(128)S(1)} %copy-done.25, bf16[512,256]{1,0:T(8,128)(2,1)S(1)} %copy-done.13, bf16[512,256]{1,0:T(8,128)(2,1)S(1)} %copy-done.15, bf16[512,256]{1,0:T(8,128)(2,1)S(1)} %copy-done.17, bf16[512,256]{1,0:T(8,128)(2,1)S(1)} %copy-done.19, ...), custom_call_target="tpu_custom_call" | custom-call | tf_op jit(solution)/shard_map/project_grad/pallas_call | solution.py:716
  176.6 1.6 last_norm.1
  178.2 1.1 add_convert_fusion.6
  179.3 2.9 %collective-permute-start.28 = (bf16[1,144,512]{2,1,0:T(8,128)(2,1)S(1)}, bf16[1,144,512]{2,1,0:T(8,128)(2,1)S(1)}, u32[]{:S(2)}, u32[]{:S(2)}) collective-permute-start(bf16[1,144,512]{2,1,0:T(8,128)(2,1)S(1)} %slice.199), channel_id=1, source_target_pairs={{0,16},{1,17},{2,18},{3,19},{4,20},{5,21},{6,22},{7,23},{8,24},{9,... | collective-permute-start | bytes 442376 | tf_op jit(solution)/shard_map/ppermute | solution.py:256
  182.2 1.1 add_convert_fusion.4
  183.9 5.9 %collective-permute-done.28 = bf16[1,144,512]{2,1,0:T(8,128)(2,1)S(1)} collective-permute-done((bf16[1,144,512]{2,1,0:T(8,128)(2,1)S(1)}, bf16[1,144,512]{2,1,0:T(8,128)(2,1)S(1)}, u32[]{:S(2)}, u32[]{:S(2)}) %collective-permute-start.28) | collective-permute-done | bytes 147488 | tf_op jit(solution)/shard_map/ppermute | solution.py:256
  191.5 0.8 collective-permute-start.25
  192.3 3.9 %collective-permute-done.25 = bf16[2,96,256]{2,1,0:T(8,128)(2,1)S(1)} collective-permute-done((bf16[2,96,256]{2,1,0:T(8,128)(2,1)S(1)}, bf16[2,96,256]{2,1,0:T(8,128)(2,1)S(1)}, u32[]{:S(2)}, u32[]{:S(2)}) %collective-permute-start.25) | collective-permute-done | bytes 98336 | tf_op jit(solution)/shard_map/ppermute | solution.py:256
  196.2 2.6 %collective-permute-start.26 = (bf16[1,96,256]{2,1,0:T(8,128)(2,1)S(1)}, bf16[1,96,256]{2,1,0:T(8,128)(2,1)S(1)}, u32[]{:S(2)}, u32[]{:S(2)}) collective-permute-start(bf16[1,96,256]{2,1,0:T(8,128)(2,1)S(1)} %slice.195), channel_id=1, source_target_pairs={{0,16},{2,18},{4,20},{6,22},{8,24},{10,26},{12,28},{14,30},{16,0},... | collective-permute-start | bytes 147464 | tf_op jit(solution)/shard_map/ppermute | solution.py:256
  199.4 1.9 collective-permute-done.26
  203.3 2.4 %collective-permute-done.29 = f32[16]{0:T(128)S(1)} collective-permute-done((f32[16]{0:T(128)S(1)}, f32[16]{0:T(128)S(1)}, u32[]{:S(2)}, u32[]{:S(2)}) %collective-permute-start.29) | collective-permute-done | bytes 96 | tf_op jit(solution)/shard_map/ppermute | solution.py:256
  (163 shorter events, 23.6 us)
Async XLA Ops:
  0.6 27.1 %copy-start.2 = (bf16[512,512]{1,0:T(8,128)(2,1)S(1)}, bf16[512,512]{1,0:T(8,128)(2,1)}, u32[]{:S(2)}) copy-start(bf16[512,512]{1,0:T(8,128)(2,1)} %atoms_ref.3) | copy-start | bytes 1572868
  1.5 5.8 %collective-permute-start = (bf16[1,64]{1,0:T(2,128)(2,1)S(1)}, bf16[1,64]{1,0:T(2,128)(2,1)S(1)}, u32[]{:S(2)}, u32[]{:S(2)}) collective-permute-start(bf16[1,64]{1,0:T(2,128)(2,1)S(1)} %maximum_bitcast_fusion.1), channel_id=1, source_target_pairs={{0,1},{1,0},{2,3},{3,2},{4,5},{5,4},{6,7},{7,6},{8,9},{9,8},{10,11... | collective-permute-start | bytes 392 | tf_op jit(solution)/shard_map/ppermute | solution.py:256
  8.2 5.3 %collective-permute-start.1 = (bf16[1,112,256]{2,1,0:T(8,128)(2,1)S(1)}, bf16[1,112,256]{2,1,0:T(8,128)(2,1)S(1)}, u32[]{:S(2)}, u32[]{:S(2)}) collective-permute-start(bf16[1,112,256]{2,1,0:T(8,128)(2,1)S(1)} %maximum_bitcast_fusion), channel_id=1, source_target_pairs={{0,16},{2,18},{4,20},{6,22},{8,24},{10,26},{12,28},{14,30},{16,0},... | collective-permute-start | bytes 172040 | tf_op jit(solution)/shard_map/ppermute | solution.py:256
  13.5 4.9 %collective-permute-start.2 = (bf16[2,112,256]{2,1,0:T(8,128)(2,1)S(1)}, bf16[2,112,256]{2,1,0:T(8,128)(2,1)S(1)}, u32[]{:S(2)}, u32[]{:S(2)}) collective-permute-start(bf16[2,112,256]{2,1,0:T(8,128)(2,1)S(1)} %pad_maximum_fusion.10), channel_id=1, source_target_pairs={{0,8},{2,10},{4,12},{6,14},{8,0},{10,2},{12,4},{14,6},{16,24},{18,... | collective-permute-start | bytes 344072 | tf_op jit(solution)/shard_map/ppermute | solution.py:256
  18.4 17.6 %copy-start.20 = (bf16[2,1,16,256]{3,2,1,0:T(8,128)(2,1)S(1)}, bf16[2,1,16,256]{3,2,1,0:T(8,128)(2,1)}, u32[]{:S(2)}) copy-start(bf16[2,1,16,256]{3,2,1,0:T(8,128)(2,1)} %constant.30.clone.mask_ref) | copy-start | bytes 49156
  18.4 17.6 %copy-start.24 = (s32[4]{0:T(128)S(1)}, s32[4]{0:T(128)}, u32[]{:S(2)}) copy-start(s32[4]{0:T(128)} %cnt_ref.8) | copy-start | bytes 52
  18.4 6.1 %collective-permute-start.4 = (bf16[4,112,256]{2,1,0:T(8,128)(2,1)S(1)}, bf16[4,112,256]{2,1,0:T(8,128)(2,1)S(1)}, u32[]{:S(2)}, u32[]{:S(2)}) collective-permute-start(bf16[4,112,256]{2,1,0:T(8,128)(2,1)S(1)} %pad_maximum_fusion.8), channel_id=1, source_target_pairs={{0,4},{2,6},{4,0},{6,2},{8,12},{10,14},{12,8},{14,10},{16,20},{18,... | collective-permute-start | bytes 688136 | tf_op jit(solution)/shard_map/ppermute | solution.py:256
  24.5 3.9 %copy-start.30 = (bf16[8,112,256]{2,1,0:T(8,128)(2,1)}, bf16[8,112,256]{2,1,0:T(8,128)(2,1)S(1)}, u32[]{:S(2)}) copy-start(bf16[8,112,256]{2,1,0:T(8,128)(2,1)S(1)} %constant_dynamic-update-slice_fusion.6.near_ref) | copy-start | bytes 1376260
  24.5 3.9 %collective-permute-start.5 = (bf16[8,112,256]{2,1,0:T(8,128)(2,1)S(1)}, bf16[8,112,256]{2,1,0:T(8,128)(2,1)S(1)}, u32[]{:S(2)}, u32[]{:S(2)}) collective-permute-start(bf16[8,112,256]{2,1,0:T(8,128)(2,1)S(1)} %constant_dynamic-update-slice_fusion.6.near_ref), channel_id=1, source_target_pairs={{0,2},{2,0},{4,6},{6,4},{8,10},{10,8},{12,14},{14,12},{16,18},{18,... | collective-permute-start | bytes 1376264 | tf_op jit(solution)/shard_map/ppermute | solution.py:256
  24.6 24.7 %collective-permute-start.9 = (bf16[512,512]{1,0:T(8,128)(2,1)}, bf16[512,512]{1,0:T(8,128)(2,1)S(1)}, u32[]{:S(2)}, u32[]{:S(2)}) collective-permute-start(bf16[512,512]{1,0:T(8,128)(2,1)} %atoms_ref.3), channel_id=1, source_target_pairs={{0,1},{1,0},{2,3},{3,2},{4,5},{5,4},{6,7},{7,6},{8,9},{9,8},{10,11... | collective-permute-start | bytes 1572872 | tf_op jit(solution)/shard_map/ppermute | solution.py:256
  25.2 10.0 %collective-permute-start.3 = (bf16[1,144,512]{2,1,0:T(8,128)(2,1)S(1)}, bf16[1,144,512]{2,1,0:T(8,128)(2,1)S(1)}, u32[]{:S(2)}, u32[]{:S(2)}) collective-permute-start(bf16[1,144,512]{2,1,0:T(8,128)(2,1)S(1)} %bitcast.35), channel_id=1, source_target_pairs={{0,16},{1,17},{2,18},{3,19},{4,20},{5,21},{6,22},{7,23},{8,24},{9,... | collective-permute-start | bytes 442376 | tf_op jit(solution)/shard_map/ppermute | solution.py:256
  35.2 11.0 %collective-permute-start.6 = (bf16[2,144,512]{2,1,0:T(8,128)(2,1)S(1)}, bf16[2,144,512]{2,1,0:T(8,128)(2,1)S(1)}, u32[]{:S(2)}, u32[]{:S(2)}) collective-permute-start(bf16[2,144,512]{2,1,0:T(8,128)(2,1)S(1)} %pad_maximum_fusion.5), channel_id=1, source_target_pairs={{0,8},{1,9},{2,10},{3,11},{4,12},{5,13},{6,14},{7,15},{8,0},{9,1},... | collective-permute-start | bytes 884744 | tf_op jit(solution)/shard_map/ppermute | solution.py:256
  46.2 3.2 %copy-start.12 = (bf16[512,256]{1,0:T(8,128)(2,1)}, bf16[512,256]{1,0:T(8,128)(2,1)S(1)}, u32[]{:S(2)}) copy-start(bf16[512,256]{1,0:T(8,128)(2,1)S(1)} %get-tuple-element.176.refs_0_) | copy-start | bytes 786436
  46.3 12.3 %collective-permute-start.8 = (bf16[4,64,512]{2,1,0:T(8,128)(2,1)S(1)}, bf16[4,64,512]{2,1,0:T(8,128)(2,1)S(1)}, u32[]{:S(2)}, u32[]{:S(2)}) collective-permute-start(bf16[4,64,512]{2,1,0:T(8,128)(2,1)S(1)} %slice.185), channel_id=1, source_target_pairs={{0,1},{1,0},{2,3},{3,2},{4,5},{5,4},{6,7},{7,6},{8,9},{9,8},{10,11... | collective-permute-start | bytes 786440 | tf_op jit(solution)/shard_map/ppermute | solution.py:256
  47.8 10.8 %collective-permute-start.7 = (bf16[4,80,512]{2,1,0:T(8,128)(2,1)S(1)}, bf16[4,80,512]{2,1,0:T(8,128)(2,1)S(1)}, u32[]{:S(2)}, u32[]{:S(2)}) collective-permute-start(bf16[4,80,512]{2,1,0:T(8,128)(2,1)S(1)} %slice.184), channel_id=1, source_target_pairs={{0,4},{1,5},{2,6},{3,7},{4,0},{5,1},{6,2},{7,3},{8,12},{9,13},{10,... | collective-permute-start | bytes 983048 | tf_op jit(solution)/shard_map/ppermute | solution.py:256
  60.3 16.1 %collective-permute-start.10 = (bf16[8,80,512]{2,1,0:T(8,128)(2,1)}, bf16[8,80,512]{2,1,0:T(8,128)(2,1)}, u32[]{:S(2)}, u32[]{:S(2)}) collective-permute-start(bf16[8,80,512]{2,1,0:T(8,128)(2,1)} %pad_maximum_fusion.2), channel_id=1, source_target_pairs={{0,1},{1,0},{2,3},{3,2},{4,5},{5,4},{6,7},{7,6},{8,9},{9,8},{10,11... | collective-permute-start | bytes 1966088 | tf_op jit(solution)/shard_map/ppermute | solution.py:256
  60.8 13.0 %collective-permute-start.11 = (bf16[8,64,512]{2,1,0:T(8,128)(2,1)}, bf16[8,64,512]{2,1,0:T(8,128)(2,1)}, u32[]{:S(2)}, u32[]{:S(2)}) collective-permute-start(bf16[8,64,512]{2,1,0:T(8,128)(2,1)} %pad_maximum_fusion.3), channel_id=1, source_target_pairs={{0,4},{1,5},{2,6},{3,7},{4,0},{5,1},{6,2},{7,3},{8,12},{9,13},{10,... | collective-permute-start | bytes 1572872 | tf_op jit(solution)/shard_map/ppermute | solution.py:256
  69.7 11.6 %copy-start.16 = (bf16[512,256]{1,0:T(8,128)(2,1)}, bf16[512,256]{1,0:T(8,128)(2,1)S(1)}, u32[]{:S(2)}) copy-start(bf16[512,256]{1,0:T(8,128)(2,1)S(1)} %get-tuple-element.178.refs_2_) | copy-start | bytes 786436
  81.2 10.3 %collective-permute-start.13 = (bf16[16,80,512]{2,1,0:T(8,128)(2,1)}, bf16[16,80,512]{2,1,0:T(8,128)(2,1)}, u32[]{:S(2)}, u32[]{:S(2)}) collective-permute-start(bf16[16,80,512]{2,1,0:T(8,128)(2,1)} %pad_maximum_fusion.a0_ref), channel_id=1, source_target_pairs={{0,2},{1,3},{2,0},{3,1},{4,6},{5,7},{6,4},{7,5},{8,10},{9,11},{10,... | collective-permute-start | bytes 3932168 | tf_op jit(solution)/shard_map/ppermute | solution.py:256
  81.2 10.3 %collective-permute-start.14 = (bf16[16,64,512]{2,1,0:T(8,128)(2,1)}, bf16[16,64,512]{2,1,0:T(8,128)(2,1)}, u32[]{:S(2)}, u32[]{:S(2)}) collective-permute-start(bf16[16,64,512]{2,1,0:T(8,128)(2,1)} %pad_maximum_fusion.1.b0_ref), channel_id=1, source_target_pairs={{0,2},{1,3},{2,0},{3,1},{4,6},{5,7},{6,4},{7,5},{8,10},{9,11},{10,... | collective-permute-start | bytes 3145736 | tf_op jit(solution)/shard_map/ppermute | solution.py:256
  81.7 9.7 %collective-permute-start.12 = (bf16[512,256]{1,0:T(8,128)(2,1)S(1)}, bf16[512,256]{1,0:T(8,128)(2,1)S(1)}, u32[]{:S(2)}, u32[]{:S(2)}) collective-permute-start(bf16[512,256]{1,0:T(8,128)(2,1)S(1)} %pad_maximum_fusion.7), channel_id=1, source_target_pairs={{0,1},{1,0},{2,3},{3,2},{4,5},{5,4},{6,7},{7,6},{8,9},{9,8},{10,11... | collective-permute-start | bytes 786440 | tf_op jit(solution)/shard_map/ppermute | solution.py:256
  92.2 20.2 %copy-start.8 = (f32[256,256]{1,0:T(8,128)S(1)}, f32[256,256]{1,0:T(8,128)}, u32[]{:S(2)}) copy-start(f32[256,256]{1,0:T(8,128)} %copy-done.7) | copy-start | bytes 786436
  92.2 20.3 %copy-start.9 = (bf16[2,1,16,256]{3,2,1,0:T(8,128)(2,1)S(1)}, bf16[2,1,16,256]{3,2,1,0:T(8,128)(2,1)}, u32[]{:S(2)}) copy-start(bf16[2,1,16,256]{3,2,1,0:T(8,128)(2,1)} %constant.31.clone.mask_ref) | copy-start | bytes 49156
  109.5 15.1 %collective-permute-start.16 = (bf16[16,64,512]{2,1,0:T(8,128)(2,1)}, bf16[16,64,512]{2,1,0:T(8,128)(2,1)S(1)}, u32[]{:S(2)}, u32[]{:S(2)}) collective-permute-start(bf16[16,64,512]{2,1,0:T(8,128)(2,1)} %get-tuple-element.154), channel_id=1, source_target_pairs={{0,2},{1,3},{2,0},{3,1},{4,6},{5,7},{6,4},{7,5},{8,10},{9,11},{10,... | collective-permute-start | bytes 3145736 | tf_op jit(solution)/shard_map/ppermute | solution.py:256
  109.5 15.5 %collective-permute-start.15 = (bf16[16,80,512]{2,1,0:T(8,128)(2,1)}, bf16[16,80,512]{2,1,0:T(8,128)(2,1)S(1)}, u32[]{:S(2)}, u32[]{:S(2)}) collective-permute-start(bf16[16,80,512]{2,1,0:T(8,128)(2,1)} %get-tuple-element.152), channel_id=1, source_target_pairs={{0,2},{1,3},{2,0},{3,1},{4,6},{5,7},{6,4},{7,5},{8,10},{9,11},{10,... | collective-permute-start | bytes 3932168 | tf_op jit(solution)/shard_map/ppermute | solution.py:256
  110.0 17.8 %collective-permute-start.21 = (bf16[512,256]{1,0:T(8,128)(2,1)}, bf16[512,256]{1,0:T(8,128)(2,1)S(1)}, u32[]{:S(2)}, u32[]{:S(2)}) collective-permute-start(bf16[512,256]{1,0:T(8,128)(2,1)} %get-tuple-element.164), channel_id=1, source_target_pairs={{0,1},{1,0},{2,3},{3,2},{4,5},{5,4},{6,7},{7,6},{8,9},{9,8},{10,11... | collective-permute-start | bytes 786440 | tf_op jit(solution)/shard_map/ppermute | solution.py:256
  112.4 12.1 %copy-start.29 = (bf16[16,64,512]{2,1,0:T(8,128)(2,1)S(1)}, bf16[16,64,512]{2,1,0:T(8,128)(2,1)}, u32[]{:S(2)}) copy-start(bf16[16,64,512]{2,1,0:T(8,128)(2,1)} %get-tuple-element.153) | copy-start | bytes 3145732
  126.4 13.7 %collective-permute-start.18 = (bf16[8,64,512]{2,1,0:T(8,128)(2,1)S(1)}, bf16[8,64,512]{2,1,0:T(8,128)(2,1)S(1)}, u32[]{:S(2)}, u32[]{:S(2)}) collective-permute-start(bf16[8,64,512]{2,1,0:T(8,128)(2,1)S(1)} %slice.154), channel_id=1, source_target_pairs={{0,4},{1,5},{2,6},{3,7},{4,0},{5,1},{6,2},{7,3},{8,12},{9,13},{10,... | collective-permute-start | bytes 1572872 | tf_op jit(solution)/shard_map/ppermute | solution.py:256
  127.1 16.2 %collective-permute-start.17 = (bf16[8,80,512]{2,1,0:T(8,128)(2,1)S(1)}, bf16[8,80,512]{2,1,0:T(8,128)(2,1)S(1)}, u32[]{:S(2)}, u32[]{:S(2)}) collective-permute-start(bf16[8,80,512]{2,1,0:T(8,128)(2,1)S(1)} %slice.152), channel_id=1, source_target_pairs={{0,1},{1,0},{2,3},{3,2},{4,5},{5,4},{6,7},{7,6},{8,9},{9,8},{10,11... | collective-permute-start | bytes 1966088 | tf_op jit(solution)/shard_map/ppermute | solution.py:256
  143.5 16.6 %collective-permute-start.20 = (bf16[4,64,512]{2,1,0:T(8,128)(2,1)S(1)}, bf16[4,64,512]{2,1,0:T(8,128)(2,1)S(1)}, u32[]{:S(2)}, u32[]{:S(2)}) collective-permute-start(bf16[4,64,512]{2,1,0:T(8,128)(2,1)S(1)} %slice.158), channel_id=1, source_target_pairs={{0,1},{1,0},{2,3},{3,2},{4,5},{5,4},{6,7},{7,6},{8,9},{9,8},{10,11... | collective-permute-start | bytes 786440 | tf_op jit(solution)/shard_map/ppermute | solution.py:256
  144.2 16.0 %collective-permute-start.19 = (bf16[4,80,512]{2,1,0:T(8,128)(2,1)S(1)}, bf16[4,80,512]{2,1,0:T(8,128)(2,1)S(1)}, u32[]{:S(2)}, u32[]{:S(2)}) collective-permute-start(bf16[4,80,512]{2,1,0:T(8,128)(2,1)S(1)} %slice.156), channel_id=1, source_target_pairs={{0,4},{1,5},{2,6},{3,7},{4,0},{5,1},{6,2},{7,3},{8,12},{9,13},{10,... | collective-permute-start | bytes 983048 | tf_op jit(solution)/shard_map/ppermute | solution.py:256
  158.7 17.9 %collective-permute-start.22 = (bf16[512,512]{1,0:T(8,128)(2,1)}, bf16[512,512]{1,0:T(8,128)(2,1)S(1)}, u32[]{:S(2)}, u32[]{:S(2)}) collective-permute-start(bf16[512,512]{1,0:T(8,128)(2,1)} %pad_maximum_fusion.4), channel_id=1, source_target_pairs={{0,1},{1,0},{2,3},{3,2},{4,5},{5,4},{6,7},{7,6},{8,9},{9,8},{10,11... | collective-permute-start | bytes 1572872 | tf_op jit(solution)/shard_map/ppermute | solution.py:256
  161.1 17.0 %collective-permute-start.27 = (bf16[2,144,512]{2,1,0:T(8,128)(2,1)}, bf16[2,144,512]{2,1,0:T(8,128)(2,1)}, u32[]{:S(2)}, u32[]{:S(2)}) collective-permute-start(bf16[2,144,512]{2,1,0:T(8,128)(2,1)} %slice.197), channel_id=1, source_target_pairs={{0,8},{1,9},{2,10},{3,11},{4,12},{5,13},{6,14},{7,15},{8,0},{9,1},... | collective-permute-start | bytes 884744 | tf_op jit(solution)/shard_map/ppermute | solution.py:256
  162.0 12.2 %copy-start.13 = (bf16[512,256]{1,0:T(8,128)(2,1)S(1)}, bf16[512,256]{1,0:T(8,128)(2,1)}, u32[]{:S(2)}) copy-start(bf16[512,256]{1,0:T(8,128)(2,1)} %copy-done.12) | copy-start | bytes 786436
  162.0 12.2 %copy-start.15 = (bf16[512,256]{1,0:T(8,128)(2,1)S(1)}, bf16[512,256]{1,0:T(8,128)(2,1)}, u32[]{:S(2)}) copy-start(bf16[512,256]{1,0:T(8,128)(2,1)} %copy-done.14) | copy-start | bytes 786436
  162.0 12.2 %copy-start.17 = (bf16[512,256]{1,0:T(8,128)(2,1)S(1)}, bf16[512,256]{1,0:T(8,128)(2,1)}, u32[]{:S(2)}) copy-start(bf16[512,256]{1,0:T(8,128)(2,1)} %copy-done.16) | copy-start | bytes 786436
  162.0 12.2 %copy-start.19 = (bf16[512,256]{1,0:T(8,128)(2,1)S(1)}, bf16[512,256]{1,0:T(8,128)(2,1)}, u32[]{:S(2)}) copy-start(bf16[512,256]{1,0:T(8,128)(2,1)} %copy-done.18) | copy-start | bytes 786436
  162.0 12.2 %copy-start.25 = (s32[2]{0:T(128)S(1)}, s32[2]{0:T(128)}, u32[]{:S(2)}) copy-start(s32[2]{0:T(128)} %pad_add_fusion.me_ref) | copy-start | bytes 28
  176.5 5.7 %collective-permute-start.23 = (bf16[8,96,256]{2,1,0:T(8,128)(2,1)}, bf16[8,96,256]{2,1,0:T(8,128)(2,1)}, u32[]{:S(2)}, u32[]{:S(2)}) collective-permute-start(bf16[8,96,256]{2,1,0:T(8,128)(2,1)} %get-tuple-element.185), channel_id=1, source_target_pairs={{0,2},{2,0},{4,6},{6,4},{8,10},{10,8},{12,14},{14,12},{16,18},{18,... | collective-permute-start | bytes 1179656 | tf_op jit(solution)/shard_map/ppermute | solution.py:256
  178.2 12.5 %copy-start.32 = (bf16[16,2048]{1,0:T(8,128)(2,1)S(1)}, bf16[16,2048]{1,0:T(8,128)(2,1)}, u32[]{:S(2)}) copy-start(bf16[16,2048]{1,0:T(8,128)(2,1)} %param.26) | copy-start | bytes 196612
  179.3 10.6 %collective-permute-start.28 = (bf16[1,144,512]{2,1,0:T(8,128)(2,1)S(1)}, bf16[1,144,512]{2,1,0:T(8,128)(2,1)S(1)}, u32[]{:S(2)}, u32[]{:S(2)}) collective-permute-start(bf16[1,144,512]{2,1,0:T(8,128)(2,1)S(1)} %slice.199), channel_id=1, source_target_pairs={{0,16},{1,17},{2,18},{3,19},{4,20},{5,21},{6,22},{7,23},{8,24},{9,... | collective-permute-start | bytes 442376 | tf_op jit(solution)/shard_map/ppermute | solution.py:256
  183.3 18.0 %copy-start.33 = (bf16[3,32,256]{2,1,0:T(8,128)(2,1)S(1)}, bf16[3,32,256]{2,1,0:T(8,128)(2,1)}, u32[]{:S(2)}) copy-start(bf16[3,32,256]{2,1,0:T(8,128)(2,1)} %param.22) | copy-start | bytes 147460
  183.3 19.4 %copy-start.35 = (f32[16]{0:T(128)S(1)}, f32[16]{0:T(128)}, u32[]{:S(2)}) copy-start(f32[16]{0:T(128)} %param.25) | copy-start | bytes 196
  183.3 22.4 %copy-start.34 = (f32[16]{0:T(128)S(1)}, f32[16]{0:T(128)}, u32[]{:S(2)}) copy-start(f32[16]{0:T(128)} %param.24) | copy-start | bytes 196
  183.4 8.1 %collective-permute-start.24 = (bf16[4,96,256]{2,1,0:T(8,128)(2,1)S(1)}, bf16[4,96,256]{2,1,0:T(8,128)(2,1)S(1)}, u32[]{:S(2)}, u32[]{:S(2)}) collective-permute-start(bf16[4,96,256]{2,1,0:T(8,128)(2,1)S(1)} %slice.191), channel_id=1, source_target_pairs={{0,4},{2,6},{4,0},{6,2},{8,12},{10,14},{12,8},{14,10},{16,20},{18,... | collective-permute-start | bytes 589832 | tf_op jit(solution)/shard_map/ppermute | solution.py:256
  191.5 4.7 %collective-permute-start.25 = (bf16[2,96,256]{2,1,0:T(8,128)(2,1)S(1)}, bf16[2,96,256]{2,1,0:T(8,128)(2,1)S(1)}, u32[]{:S(2)}, u32[]{:S(2)}) collective-permute-start(bf16[2,96,256]{2,1,0:T(8,128)(2,1)S(1)} %slice.193), channel_id=1, source_target_pairs={{0,8},{2,10},{4,12},{6,14},{8,0},{10,2},{12,4},{14,6},{16,24},{18,... | collective-permute-start | bytes 294920 | tf_op jit(solution)/shard_map/ppermute | solution.py:256
  196.2 5.1 %collective-permute-start.26 = (bf16[1,96,256]{2,1,0:T(8,128)(2,1)S(1)}, bf16[1,96,256]{2,1,0:T(8,128)(2,1)S(1)}, u32[]{:S(2)}, u32[]{:S(2)}) collective-permute-start(bf16[1,96,256]{2,1,0:T(8,128)(2,1)S(1)} %slice.195), channel_id=1, source_target_pairs={{0,16},{2,18},{4,20},{6,22},{8,24},{10,26},{12,28},{14,30},{16,0},... | collective-permute-start | bytes 147464 | tf_op jit(solution)/shard_map/ppermute | solution.py:256
  202.1 3.5 %collective-permute-start.29 = (f32[16]{0:T(128)S(1)}, f32[16]{0:T(128)S(1)}, u32[]{:S(2)}, u32[]{:S(2)}) collective-permute-start(f32[16]{0:T(128)S(1)} %dynamic-slice_bitcast_fusion), channel_id=1, source_target_pairs={{0,1},{1,0},{2,3},{3,2},{4,5},{5,4},{6,7},{7,6},{8,9},{9,8},{10,11... | collective-permute-start | bytes 200 | tf_op jit(solution)/shard_map/ppermute | solution.py:256
  (19 other events, 32.8 us)

commit v3 on v2

--- a/solution.py
+++ b/solution.py
@@ -11,6 +11,7 @@
 F32 = jnp.float32
 BF16 = jnp.bfloat16
 NEG = -1e30
+VMEM_LIMIT = 48 << 20
 BOTH = ("batch", "head")
 
 
@@ -264,8 +265,8 @@
     return pl.BlockSpec(shape, lambda *_: (0,) * len(shape))
 
 
-def prep_kernel(me_ref, near_ref, far_ref, w_ref, gains_ref, rows_s, *, bits, heads_bits, shard):
-    b, h = me_ref[0], me_ref[1]
+def unpack_shards(info_ref, near_ref, far_ref, w_ref, gains_ref, rows_s, bits, shard):
+    b, h = info_ref[0], info_ref[1]
     half = near_ref.shape[0]
     rows = w_ref.shape[1] // (2 * half)
     dim = gains_ref.shape[1]
@@ -291,15 +292,27 @@
 
 
 def attend_forward_kernel(
-    mol_ref, cnt_ref, atoms_ref, w_ref, gains_ref, mask_ref, pair_ref, *rest,
-    hb, groups, scale, carried
+    info_ref, cnt_ref, atoms_ref, w_ref, gains_ref, pair_ref, *rest, hb, scale, carried, mol, bits, shard
 ):
-    new_ref, exp_ref, hid_t_ref, qkv_ref, mixed_ref, inv_ref, q_s, kt_s, v_s, sum_s = rest[carried:]
-    step = pl.program_id(1)
+    rest = rest[carried:]
+    new_ref, exp_ref, mixed_ref, hid_t_ref, qkv_t_ref, inv_ref = rest[:6]
+    if bits:
+        near_ref, far_ref, (w_ref, gains_ref) = w_ref, gains_ref, rest[6:8]
+        rest = (*rest[:6], *rest[8:-1], rest[-1])
+        rows_s = rest[-1]
+        rest = rest[:-1]
+    q_s, kz_s, va_s, valid_s, sum_s = rest[6:]
+    step = pl.program_id(0)
     length = atoms_ref.shape[0]
-    lanes = w_ref.shape[2] // groups
-    per_group = lanes // (8 * hb)
-    count = cnt_ref[mol_ref[pl.program_id(0)]]
+    heads = qkv_t_ref.shape[1]
+    lanes = 8 * hb
+    count = cnt_ref[mol(info_ref)]
+
+    @pl.when(step == 0)
+    def _():
+        kz_s[...] = jnp.zeros_like(kz_s)
+        if bits:
+            unpack_shards(info_ref, near_ref, far_ref, w_ref, gains_ref, rows_s, bits, shard)
 
     @pl.when(step == 0)
     def _():
@@ -311,289 +324,253 @@
         query = (dot(hidden, w_ref[0]) * scale).astype(BF16)
         key = dot(hidden, w_ref[1]).astype(BF16)
         value = dot(hidden, w_ref[2]).astype(BF16)
-        qkv_ref[0] = query
-        qkv_ref[1] = key
-        qkv_ref[2] = value
-        key_t = key.T
-        at = lax.broadcasted_iota(jnp.int32, (1, length), 1)
-        bias = jnp.where(at < count, 0.0, NEG)
-        first = lax.broadcasted_iota(jnp.int32, (lanes, length), 0) == 0
-        bias_rows = jnp.where(first, bias, 0.0).astype(BF16)
-        ones_lane = (lax.broadcasted_iota(jnp.int32, (length, lanes), 1) == 0).astype(F32).astype(BF16)
-        for g in range(groups):
-            part = slice(g * lanes, (g + 1) * lanes)
-            q_s[g, :, :lanes] = query[:, part]
-            q_s[g, :, lanes:] = ones_lane
-            kt_s[g, :lanes, :] = key_t[part]
-            kt_s[g, lanes:, :] = bias_rows
-            v_s[g, :, :lanes] = value[:, part]
-            v_s[g, :, lanes:] = jnp.ones((length, lanes), BF16)
-
-    g = step // per_group
-    block = lax.rem(step, per_group)
-    valid = (lax.broadcasted_iota(jnp.int32, (length, length), 0) < count) & (
-        lax.broadcasted_iota(jnp.int32, (length, length), 1) < count
-    )
-    total = jnp.zeros((length, 2 * lanes), F32)
+        qkv_t_ref[0] = query.T.reshape(heads, 8, length)
+        qkv_t_ref[1] = key.T.reshape(heads, 8, length)
+        value_t = value.T.reshape(heads, 8, length)
+        qkv_t_ref[2] = value_t
+        va_s[:, :8, :] = value_t
+        top = lax.broadcasted_iota(jnp.int32, (8, length), 0) == 0
+        first = jnp.where(top, 1.0, 0.0).astype(BF16)
+        va_s[:, 8:, :] = jnp.broadcast_to(first[None], (heads, 8, length))
+        at = lax.broadcasted_iota(jnp.int32, (8, length), 1)
+        bias = jnp.where(top & (at >= count), NEG, 0.0).astype(BF16)
+        kz_s[:, lanes : lanes + 8, :] = jnp.broadcast_to(bias[None], (hb, 8, length))
+        first_lane = jnp.where(lax.broadcasted_iota(jnp.int32, (length, lanes), 1) == 0, 1.0, 0.0).astype(BF16)
+        for g in range(heads // hb):
+            q_s[g, :, :lanes] = query[:, g * lanes : (g + 1) * lanes]
+            q_s[g, :, lanes:] = first_lane
+        valid = (lax.broadcasted_iota(jnp.int32, (length, length), 0) < count) & (
+            lax.broadcasted_iota(jnp.int32, (length, length), 1) < count
+        )
+        valid_s[...] = jnp.where(valid, 1.0, 0.0).astype(BF16)
+
     for i in range(hb):
-        logits = dot(q_s[g] * mask_ref[0, block, i : i + 1, :], kt_s[g]) + pair_ref[0, i].astype(F32)
-        new_ref[0, i] = jnp.where(valid, logits, 0.0).astype(BF16)
-        exp_ref[0, i] = jnp.exp(logits - jnp.max(logits, -1, keepdims=True)).astype(BF16)
-        total = total + dot(exp_ref[0, i], v_s[g] * mask_ref[1, block, i : i + 1, :])
-
-    @pl.when(block == 0)
-    def _():
-        sum_s[...] = total
-
-    @pl.when(block > 0)
-    def _():
-        sum_s[...] = sum_s[...] + total
-
-    @pl.when(block == per_group - 1)
-    def _():
-        inverse = 1.0 / sum_s[:, lanes:]
-        rows_ok = lax.broadcasted_iota(jnp.int32, (length, lanes), 0) < count
-        at = pl.ds(pl.multiple_of(g * lanes, lanes), lanes)
-        inv_ref[:, at] = inverse
-        mixed_ref[:, at] = jnp.where(rows_ok, sum_s[:, :lanes] * inverse, 0.0).astype(BF16)
-
-
-def head_masks(groups, width, hb, backward):
-    lanes = width // groups
-    heads = lanes // 8
-    masks = np.zeros((2, heads, 2 * lanes), np.float32)
-    for h in range(heads):
-        own = slice(h * 8, (h + 1) * 8)
-        twin = slice(lanes + h * 8, lanes + (h + 1) * 8)
-        masks[0, h, own] = 1
-        masks[1, h, own] = 1
-        if backward:
-            masks[0, h, twin] = 1
-        else:
-            masks[0, h, lanes] = 1
-            masks[1, h, twin] = 1
-    return jnp.asarray(masks.reshape(2, heads // hb, hb, 2 * lanes), BF16)
-
-
-def specs_of(length, hb):
-    pair = pl.BlockSpec((1, hb, length, length), lambda i, j, mol, cnt: (mol[i], j, 0, 0))
-    rows = lambda cols: pl.BlockSpec((length, cols), lambda i, j, mol, cnt: (i, 0))
-    three = lambda cols: pl.BlockSpec((3, length, cols), lambda i, j, mol, cnt: (0, i, 0))
-    return pair, rows, three
+        kz_s[i, i * 8 : (i + 1) * 8, :] = qkv_t_ref[1, step * hb + i]
+    for i in range(hb):
+        logits = dot(q_s[step], kz_s[i]) + pair_ref[0, i].astype(F32)
+        new_ref[0, i] = logits.astype(BF16) * valid_s[...]
+        soft = jnp.exp(logits - jnp.max(logits, -1, keepdims=True)).astype(BF16)
+        exp_ref[0, i] = soft
+        sum_s[i] = dot_nt(va_s[step * hb + i], exp_ref[0, i])
+    inverse = 1.0 / sum_s[:, 8:9, :]
+    rows_ok = lax.broadcasted_iota(jnp.int32, (1, 1, length), 2) < count
+    mixed = jnp.where(rows_ok, sum_s[:, :8, :] * inverse, 0.0)
+    at = pl.ds(pl.multiple_of(step * lanes, lanes), lanes)
+    mixed_ref[:, at] = mixed.reshape(lanes, length).T.astype(BF16)
+    inv_ref[:, at] = jnp.broadcast_to(inverse, (hb, 8, length)).reshape(lanes, length).T
 
 
 ANY = pl.BlockSpec(memory_space=pl.ANY)
 
 
-def attend_forward_call(mols, counts, atoms, weights, gains, pair, carried, hb=16):
-    n, (_, heads, length, _) = mols.shape[0], pair.shape
-    dim, width = atoms.shape[1], weights.shape[2]
-    groups = max(1, width // 128)
-    lanes = width // groups
-    masks = head_masks(groups, width, hb, False)
-    pair_spec, rows, three = specs_of(length, hb)
-    args = [atoms, weights, gains, masks, pair, *carried]
+def pair_spec_of(mol, hb, length):
+    return pl.BlockSpec((1, hb, length, length), lambda j, info, cnt: (mol(info), j, 0, 0))
+
+
+def rows_spec(length, cols, at=0):
+    return pl.BlockSpec((length, cols), lambda *_: (at, 0))
+
+
+def attend_forward_call(info, mol, counts, atoms, at, weights, pair, carried, theirs, bits=(), shard=0, hb=16):
+    _, heads, length, _ = pair.shape
+    dim = atoms.shape[1]
+    width = 8 * heads
+    lanes = 8 * hb
+    pair_spec = pair_spec_of(mol, hb, length)
+    place, blocks = theirs
+    args = [atoms, *weights, pair, *carried]
+    shape = jax.ShapeDtypeStruct
+    outs = [
+        (shape(pair.shape, BF16), pair_spec),
+        (shape(pair.shape, BF16), pair_spec),
+        (shape((blocks * length, width), BF16), rows_spec(length, width, place)),
+        (shape((dim, length), BF16), whole((dim, length))),
+        (shape((3, heads, 8, length), BF16), whole((3, heads, 8, length))),
+        (shape((length, width), F32), whole((length, width))),
+    ]
+    scratch = [
+        pltpu.VMEM((heads // hb, length, 2 * lanes), BF16),
+        pltpu.VMEM((hb, 2 * lanes, length), BF16),
+        pltpu.VMEM((heads, 16, length), BF16),
+        pltpu.VMEM((length, length), BF16),
+        pltpu.VMEM((hb, 16, length), F32),
+    ]
+    if bits:
+        outs += [
+            (shape((3, dim, width), BF16), whole((3, dim, width))),
+            (shape((2, dim), F32), whole((2, dim))),
+        ]
+        scratch.append(pltpu.VMEM((2 ** len(bits), width), F32))
     spec = pltpu.PrefetchScalarGridSpec(
         num_scalar_prefetch=2,
-        grid=(n, heads // hb),
-        in_specs=[rows(dim), whole(weights.shape), whole(gains.shape), whole(masks.shape), pair_spec]
+        grid=(heads // hb,),
+        in_specs=[rows_spec(length, dim, at), *[whole(x.shape) for x in weights], pair_spec]
         + [ANY] * len(carried),
-        out_specs=[
-            pair_spec,
-            pair_spec,
-            pl.BlockSpec((dim, length), lambda i, j, mol, cnt: (0, i)),
-            three(width),
-            rows(width),
-            rows(width),
-        ],
-        scratch_shapes=[
-            pltpu.VMEM((groups, length, 2 * lanes), BF16),
-            pltpu.VMEM((groups, 2 * lanes, length), BF16),
-            pltpu.VMEM((groups, length, 2 * lanes), BF16),
-            pltpu.VMEM((length, 2 * lanes), F32),
-        ],
-    )
-    shape = jax.ShapeDtypeStruct
+        out_specs=[x[1] for x in outs],
+        scratch_shapes=scratch,
+    )
     return pl.pallas_call(
         partial(
             attend_forward_kernel,
             hb=hb,
-            groups=groups,
             scale=8**-0.5,
             carried=len(carried),
+            mol=mol,
+            bits=bits,
+            shard=shard,
         ),
         grid_spec=spec,
-        out_shape=[
-            shape(pair.shape, BF16),
-            shape(pair.shape, BF16),
-            shape((dim, n * length), BF16),
-            shape((3, n * length, width), BF16),
-            shape((n * length, width), BF16),
-            shape((n * length, width), F32),
-        ],
-        input_output_aliases={7: 0, 8: 1} if carried else {},
+        out_shape=[x[0] for x in outs],
+        input_output_aliases={6 + k: k for k in range(len(carried))},
         compiler_params=pltpu.CompilerParams(
-            dimension_semantics=("arbitrary", "arbitrary"), vmem_limit_bytes=48 << 20
+            dimension_semantics=("arbitrary",), vmem_limit_bytes=VMEM_LIMIT
         ),
         cost_estimate=pl.CostEstimate(
-            flops=n * heads * 4 * length**3,
-            transcendentals=n * heads * length**2,
-            bytes_accessed=6 * n * heads * length**2,
+            flops=heads * 4 * length**3,
+            transcendentals=heads * length**2,
+            bytes_accessed=6 * heads * length**2,
         ),
         name="attend_forward",
-    )(mols, counts, *args)
+    )(info, counts, *args)
 
 
 def attend_backward_kernel(
-    mol_ref, cnt_ref, gm_ref, mixed_ref, inv_ref, qkv_ref, w_ref, mask_ref, exp_ref, cot_ref, *rest,
-    hb, groups, scale, carried
+    info_ref, cnt_ref, gm_ref, mixed_ref, inv_ref, qkv_t_ref, w_ref, mask_ref, exp_ref, cot_ref, *rest,
+    hb, scale, carried, mol
 ):
-    pg_ref, gp_ref, gh_ref, l_s, r_s, k_s, qt_s, gt_s, gq_s, gk_s, gv_s = rest[carried:]
-    step, steps = pl.program_id(1), pl.num_programs(1)
+    pg_ref, gh_ref, gp_ref, l_s, r_s, gt_s, valid_s, gq_s, gk_s, gv_s = rest[carried:]
+    step, steps = pl.program_id(0), pl.num_programs(0)
     length, width = gm_ref.shape
-    lanes = width // groups
-    per_group = lanes // (8 * hb)
-    count = cnt_ref[mol_ref[pl.program_id(0)]]
+    heads = qkv_t_ref.shape[1]
+    lanes = 8 * hb
+    count = cnt_ref[mol(info_ref)]
 
     @pl.when(step == 0)
     def _():
         rows_ok = lax.broadcasted_iota(jnp.int32, (length, width), 0) < count
         scaled = jnp.where(rows_ok, gm_ref[...].astype(F32) * inv_ref[...], 0.0).astype(BF16)
-        wide = scaled.astype(F32)
-        delta = (-(wide * mixed_ref[...].astype(F32))).astype(BF16)
-        value_t = qkv_ref[2].T
-        for g in range(groups):
+        delta = (-(scaled.astype(F32) * mixed_ref[...].astype(F32))).astype(BF16)
+        gt_s[...] = scaled.T.reshape(gt_s.shape)
+        for g in range(heads // hb):
             part = slice(g * lanes, (g + 1) * lanes)
             l_s[g, :, :lanes] = scaled[:, part]
             l_s[g, :, lanes:] = delta[:, part]
-            r_s[g, :lanes, :] = value_t[part]
+            r_s[g, :lanes, :] = qkv_t_ref[2, g * hb : (g + 1) * hb].reshape(lanes, length)
             r_s[g, lanes:, :] = jnp.ones((lanes, length), BF16)
-            k_s[g] = qkv_ref[1, :, part]
-        qt_s[...] = qkv_ref[0].astype(F32).T.reshape(qt_s.shape).astype(BF16)
-        gt_s[...] = wide.T.reshape(gt_s.shape).astype(BF16)
-
-    g = step // per_group
-    block = lax.rem(step, per_group)
-    valid = (lax.broadcasted_iota(jnp.int32, (length, length), 0) < count) & (
-        lax.broadcasted_iota(jnp.int32, (length, length), 1) < count
-    )
-    total = jnp.zeros((length, lanes), F32)
-    for i in range(hb):
-        soft = dot(l_s[g] * mask_ref[0, block, i : i + 1, :], r_s[g])
-        scores = exp_ref[0, i].astype(F32) * soft + jnp.where(valid, cot_ref[0, i].astype(F32), 0.0)
-        pg_ref[0, i] = scores.astype(BF16)
-        total = total + dot(pg_ref[0, i], k_s[g] * mask_ref[1, block, i : i + 1, :lanes])
-        head = step * hb + i
-        gk_s[head] = dot(qt_s[head], pg_ref[0, i])
-        gv_s[head] = dot(gt_s[head], exp_ref[0, i])
-
-    @pl.when(block == 0)
-    def _():
-        gq_s[g] = total
-
-    @pl.when(block > 0)
-    def _():
-        gq_s[g] = gq_s[g] + total
+        valid = (lax.broadcasted_iota(jnp.int32, (length, length), 0) < count) & (
+            lax.broadcasted_iota(jnp.int32, (length, length), 1) < count
+        )
+        valid_s[...] = jnp.where(valid, 1.0, 0.0).astype(BF16)
+
+    for i in range(0, hb, 16):
+        left = [l_s[step] * mask_ref[k : k + 1, :] for k in range(i, i + 16)]
+        soft = dot(jnp.concatenate(left, 0), r_s[step])
+        for k in range(16):
+            part = soft[k * length : (k + 1) * length]
+            cot = (cot_ref[0, i + k] * valid_s[...]).astype(F32)
+            scores = (exp_ref[0, i + k].astype(F32) * part + cot).astype(BF16)
+            pg_ref[0, i + k] = scores
+            head = step * hb + i + k
+            gq_s[head] = dot_nt(qkv_t_ref[1, head], pg_ref[0, i + k])
+            gk_s[head] = dot(qkv_t_ref[0, head], pg_ref[0, i + k])
+            gv_s[head] = dot(gt_s[head], exp_ref[0, i + k])
 
     @pl.when(step == steps - 1)
     def _():
-        for k in range(groups):
-            gp_ref[0, :, k * lanes : (k + 1) * lanes] = (gq_s[k] * scale).astype(BF16)
-        gp_ref[1] = gk_s[...].reshape(width, length).T.astype(BF16)
-        gp_ref[2] = gv_s[...].reshape(width, length).T.astype(BF16)
+        gp_ref[0] = (gq_s[...] * scale).reshape(width, length).astype(BF16).T
+        gp_ref[1] = gk_s[...].reshape(width, length).astype(BF16).T
+        gp_ref[2] = gv_s[...].reshape(width, length).astype(BF16).T
         gh_ref[...] = (
             dot_nt(gp_ref[0], w_ref[0]) + dot_nt(gp_ref[1], w_ref[1]) + dot_nt(gp_ref[2], w_ref[2])
         ).astype(BF16)
 
 
-def attend_backward_call(mols, counts, gm, mixed, inverse, qkv, weights, exps, cot, carried, hb=16):
-    n, (_, heads, length, _) = mols.shape[0], exps.shape
+def attend_backward_call(info, mol, counts, gm, at, mixed, place, saved, weights, exps, cot, carried, theirs, hb=16):
+    _, heads, length, _ = exps.shape
     dim, width = weights.shape[1], weights.shape[2]
-    groups = max(1, width // 128)
-    lanes = width // groups
-    masks = head_masks(groups, width, hb, True)
-    pair_spec, rows, three = specs_of(length, hb)
-    args = [gm, mixed, inverse, qkv, weights, masks, exps, cot, *carried]
+    lanes = 8 * hb
+    masks = jnp.asarray(np.tile(np.repeat(np.eye(hb, dtype=np.float32), 8, 1), 2), BF16)
+    pair_spec = pair_spec_of(mol, hb, length)
+    qkv_t, inverse = saved
+    args = [gm, mixed, inverse, qkv_t, weights, masks, exps, cot, *carried]
+    block, blocks = theirs
     spec = pltpu.PrefetchScalarGridSpec(
         num_scalar_prefetch=2,
-        grid=(n, heads // hb),
+        grid=(heads // hb,),
         in_specs=[
-            rows(width), rows(width), rows(width), three(width),
-            whole(weights.shape), whole(masks.shape), pair_spec, pair_spec,
+            rows_spec(length, width, at), rows_spec(length, width, place), whole(inverse.shape),
+            whole(qkv_t.shape), whole(weights.shape), whole(masks.shape), pair_spec, pair_spec,
         ] + [ANY] * len(carried),
-        out_specs=[pair_spec, three(width), rows(dim)],
+        out_specs=[pair_spec, rows_spec(length, dim, block), whole((3, length, width))],
         scratch_shapes=[
-            pltpu.VMEM((groups, length, 2 * lanes), BF16),
-            pltpu.VMEM((groups, 2 * lanes, length), BF16),
-            pltpu.VMEM((groups, length, lanes), BF16),
+            pltpu.VMEM((heads // hb, length, 2 * lanes), BF16),
+            pltpu.VMEM((heads // hb, 2 * lanes, length), BF16),
             pltpu.VMEM((heads, 8, length), BF16),
-            pltpu.VMEM((heads, 8, length), BF16),
-            pltpu.VMEM((groups, length, lanes), F32),
+            pltpu.VMEM((length, length), BF16),
+            pltpu.VMEM((heads, 8, length), F32),
             pltpu.VMEM((heads, 8, length), F32),
             pltpu.VMEM((heads, 8, length), F32),
         ],
     )
     shape = jax.ShapeDtypeStruct
     return pl.pallas_call(
-        partial(
-            attend_backward_kernel,
-            hb=hb,
-            groups=groups,
-            scale=8**-0.5,
-            carried=len(carried),
-        ),
+        partial(attend_backward_kernel, hb=hb, scale=8**-0.5, carried=len(carried), mol=mol),
         grid_spec=spec,
         out_shape=[
             shape(exps.shape, BF16),
-            shape((3, n * length, width), BF16),
-            shape((n * length, dim), BF16),
+            shape((blocks * length, dim), BF16),
+            shape((3, length, width), BF16),
         ],
-        input_output_aliases={10: 0} if carried else {},
+        input_output_aliases={10 + k: k for k in range(len(carried))},
         compiler_params=pltpu.CompilerParams(
-            dimension_semantics=("arbitrary", "arbitrary"), vmem_limit_bytes=48 << 20
+            dimension_semantics=("arbitrary",), vmem_limit_bytes=VMEM_LIMIT
         ),
         cost_estimate=pl.CostEstimate(
-            flops=n * heads * 6 * length**3,
+            flops=heads * 6 * length**3,
             transcendentals=0,
-            bytes_accessed=6 * n * heads * length**2,
+            bytes_accessed=6 * heads * length**2,
         ),
         name="attend_backward",
-    )(mols, counts, *args)
+    )(info, counts, *args)
 
 
 ROOT = (2 / np.pi) ** 0.5
 
 
 def layer_kernel(
-    me_ref, atoms_ref, mine_ref, other_ref, cot_ref, gains_ref, a0_ref, a1_ref, b0_ref, b1_ref,
-    out_ref, first_ref, gm_mine_ref, gm_other_ref, ga0_ref, ga1_ref, gb0_ref, gb1_ref,
-    win_s, wout_s, ow_s, sum_s, acc_s, gh_s, normed_s, inv_s, hid_s, hid_t_s, *, bits_a, bits_b
+    info_ref, atoms_ref, mine0_ref, mine1_ref, other_ref, cot_ref, gains_ref, *rest, bits_a, bits_b
 ):
-    me = me_ref[0]
+    a_refs, b_refs = rest[:4], rest[4:8]
+    out_ref, first_ref, gm_mine_ref, gm_other_ref = rest[8:12]
+    ga_refs, gb_refs = rest[12:16], rest[16:20]
+    win_s, wout_s, ow_s, sum_s, acc_s, gh_s, normed_s, inv_s, hid_s, hid_t_s, mixed_s = rest[20:]
+    me = 2 * info_ref[0] + info_ref[1]
     c, steps = pl.program_id(0), pl.num_programs(0)
-    half = a0_ref.shape[0]
+    part = a_refs[0].shape[0]
     dim = atoms_ref.shape[1]
-    width = mine_ref.shape[1]
-    rows = dim // (2 * half)
-    ff_rows = b0_ref.shape[1]
-    e_rows = dim // half
-
-    def shards(bits, near, far):
-        for p in range(2 * half):
-            yield p, me ^ relative(p, bits), (near, p) if p < half else (far, p - half)
+    length, width = mine0_ref.shape
+    rows = dim // (4 * part)
+    ff_rows = b_refs[0].shape[1]
+    e_rows = dim // (2 * part)
+
+    def shards(bits, refs):
+        for p in range(4 * part):
+            yield p, me ^ relative(p, bits), (refs[p // part], p % part)
 
     @pl.when(c == 0)
     def _():
-        for p, owner, (ref, q) in shards(bits_a, a0_ref, a1_ref):
+        for p, owner, (ref, q) in shards(bits_a, a_refs):
             for k in range(4):
                 win_s[k, pl.ds(pl.multiple_of(owner * rows, rows), rows), :] = ref[q, k * rows : (k + 1) * rows, :]
             at = pl.multiple_of((owner // 2) * e_rows, e_rows)
             for k in range(2):
                 ow_s[relative(p, bits_a) & 1, pl.ds(at + k * rows, rows), :] = ref[q, 4 * rows :, k * width : (k + 1) * width]
-        for p, owner, (ref, q) in shards(bits_b, b0_ref, b1_ref):
+        for p, owner, (ref, q) in shards(bits_b, b_refs):
             wout_s[pl.ds(pl.multiple_of(owner * ff_rows, ff_rows), ff_rows), :] = ref[q]
+        mixed_s[:length] = mine0_ref[...]
+        mixed_s[length:] = mine1_ref[...]
         first_sum = (
-            atoms_ref[...].astype(F32) + dot_nt(mine_ref[...], ow_s[0]) + dot_nt(other_ref[...], ow_s[1])
+            atoms_ref[...].astype(F32) + dot_nt(mixed_s[...], ow_s[0]) + dot_nt(other_ref[...], ow_s[1])
         )
         sum_s[...] = first_sum
         center = first_sum - jnp.mean(first_sum, -1, keepdims=True)
@@ -636,30 +613,30 @@
         grad_attention = grad_first.astype(BF16)
         gm_mine_ref[...] = dot(grad_attention, ow_s[0]).astype(BF16)
         gm_other_ref[...] = dot(grad_attention, ow_s[1]).astype(BF16)
-        ow_s[0] = dot_tn(grad_attention, mine_ref[...]).astype(BF16)
+        ow_s[0] = dot_tn(grad_attention, mixed_s[...]).astype(BF16)
         ow_s[1] = dot_tn(grad_attention, other_ref[...]).astype(BF16)
-        for p, owner, (ref, q) in shards(bits_a, ga0_ref, ga1_ref):
+        for p, owner, (ref, q) in shards(bits_a, ga_refs):
             for k in range(4):
                 ref[q, k * rows : (k + 1) * rows, :] = win_s[k, pl.ds(pl.multiple_of(owner * rows, rows), rows), :]
             at = pl.multiple_of((owner // 2) * e_rows, e_rows)
             for k in range(2):
                 ref[q, 4 * rows :, k * width : (k + 1) * width] = ow_s[relative(p, bits_a) & 1, pl.ds(at + k * rows, rows), :]
-        for p, owner, (ref, q) in shards(bits_b, gb0_ref, gb1_ref):
+        for p, owner, (ref, q) in shards(bits_b, gb_refs):
             ref[q] = wout_s[pl.ds(pl.multiple_of(owner * ff_rows, ff_rows), ff_rows), :]
 
 
-def layer_call(me, atoms, mine, other, cot, gains, a_pair, b_pair, bits_a, bits_b):
+def layer_call(info, atoms, mine, other, cot, gains, a_parts, b_parts, bits_a, bits_b):
     own, dim = atoms.shape
-    width = mine.shape[1]
-    ff = 2 * b_pair[0].shape[0] * b_pair[0].shape[1]
-    args = [atoms, mine, other, cot, gains, *a_pair, *b_pair]
+    width = other.shape[1]
+    ff = 4 * b_parts[0].shape[0] * b_parts[0].shape[1]
+    args = [atoms, *mine, other, cot, gains, *a_parts, *b_parts]
     shape = jax.ShapeDtypeStruct
     outs = [
         shape((own, dim), BF16),
         shape((own, dim), F32),
         shape((own, width), BF16),
         shape((own, width), BF16),
-        *[shape(x.shape, BF16) for x in (*a_pair, *b_pair)],
+        *[shape(x.shape, BF16) for x in (*a_parts, *b_parts)],
     ]
     spec = pltpu.PrefetchScalarGridSpec(
         num_scalar_prefetch=1,
@@ -677,6 +654,7 @@
             pltpu.VMEM((own, 1), F32),
             pltpu.VMEM((own, dim), BF16),
             pltpu.VMEM((dim, own), BF16),
+            pltpu.VMEM((own, width), BF16),
         ],
     )
     return pl.pallas_call(
@@ -684,13 +662,13 @@
         grid_spec=spec,
         out_shape=outs,
         compiler_params=pltpu.CompilerParams(
-            dimension_semantics=("arbitrary",), vmem_limit_bytes=60 << 20
+            dimension_semantics=("arbitrary",), vmem_limit_bytes=VMEM_LIMIT
         ),
         cost_estimate=pl.CostEstimate(
             flops=12 * own * dim * ff, transcendentals=own * ff, bytes_accessed=8 * dim * ff
         ),
         name="layer",
-    )(me, *args)
+    )(info, *args)
 
 
 def project_grad_kernel(me_ref, *refs, bits, parts):
@@ -777,22 +755,21 @@
     atoms, pair, counts, qkv_weight, out_weight, ln1_gain, ln2_gain, w_in, w_out, out_cot, pair_cot,
     batch
 ):
-    b = lax.axis_index("batch")
-    h = lax.axis_index("head")
+    info = jnp.stack([lax.axis_index("batch"), lax.axis_index("head")])
+    h = info[1]
     own, dim = atoms.shape
     length = pair.shape[2]
     width = qkv_weight.shape[2]
     shard = ln1_gain.shape[0]
     top = batch.bit_length() - 1
     far_bits = [1 << k for k in range(top - 1, 1, -1)]
-    batch_bits = [*far_bits, 2, 1]
+    batch_bits = (*far_bits, 2, 1)
     bits_a = [2 * bit for bit in far_bits] + [4, 1, 2]
     bits_b = [2 * bit for bit in far_bits] + [1, 4, 2]
     nz = len(far_bits)
     over_batch = lambda x, bit: swap(x, "batch", batch, bit)
     over_head = lambda x: swap(x, "head", 2, 1)
     over_both = lambda x, bit: swap(x, BOTH, 2 * batch, bit)
-
     tie = lax.optimization_barrier
 
     def split_gain(gain):
@@ -803,118 +780,121 @@
     gain_row = jnp.concatenate([gain_row, over_head(gain_row)], 1)
     tail = jnp.pad(gain_row, ((0, 15), (0, width - gain_row.shape[1])))
     gathered = jnp.concatenate([qkv_weight.reshape(-1, width), tail], 0)[None]
+    gathered, w_in_late, w_out_late, out_late = tie((gathered, w_in, w_out, out_weight))
     for bit in far_bits:
         gathered = join(gathered, over_batch(gathered, bit))
     e_rows = out_weight.shape[0]
     blocks = w_in.shape[1] // dim
-    in_rows = [w_in[:, k * dim : (k + 1) * dim] for k in range(blocks)]
-    out_rows = jnp.concatenate([out_weight[: e_rows // 2], out_weight[e_rows // 2 :]], 1)
-    bulk = jnp.concatenate([*in_rows, out_rows, w_out], 0)[None]
+    in_rows = [w_in_late[:, k * dim : (k + 1) * dim] for k in range(blocks)]
+    out_rows = jnp.concatenate([out_late[: e_rows // 2], out_late[e_rows // 2 :]], 1)
+    bulk = jnp.concatenate([*in_rows, out_rows, w_out_late], 0)[None]
     cut = bulk.shape[1] - w_out.shape[0]
     gathered, bulk = tie((gathered, bulk))
     atoms_other = over_head(atoms)
     gathered = join(gathered, over_batch(gathered, 2))
     far = over_batch(gathered, 1)
-    me_batch = jnp.stack([b, h])
-    weights, gains = pl.pallas_call(
-        partial(prep_kernel, bits=batch_bits, heads_bits=1, shard=shard),
-        grid_spec=pltpu.PrefetchScalarGridSpec(
-            num_scalar_prefetch=1,
-            grid=(1,),
-            in_specs=[whole(gathered.shape)] * 2,
-            out_specs=[whole((3, dim, width)), whole((2, dim))],
-            scratch_shapes=[pltpu.VMEM((batch, width), F32)],
-        ),
-        out_shape=[jax.ShapeDtypeStruct((3, dim, width), BF16), jax.ShapeDtypeStruct((2, dim), F32)],
-        name="prepare",
-    )(me_batch, gathered, far)
 
     per = own // length
-    mine, theirs = h * per, (1 - h) * per
-    plan = [(mine, atoms[:length])]
-    plan += [(theirs + k, atoms_other[k * length : (k + 1) * length]) for k in range(per)]
-    plan += [(mine + k, atoms[k * length : (k + 1) * length]) for k in range(1, per)]
-    plan = [(mol[None], rows) for mol, rows in plan]
+    mine = lambda k: lambda info: info[1] * per + k
+    theirs = lambda k: lambda info: (1 - info[1]) * per + k
+    plan = [(mine(0), atoms, 0, (0, 1))]
+    plan += [(theirs(k), atoms_other, k, (k, per)) for k in range(per)]
+    plan += [(mine(k), atoms, k, (0, 1)) for k in range(1, per)]
     stage_bits = [(bit, bit) for bit in bits_a[:nz]] + list(zip(bits_a[nz:], bits_b[nz:]))
+    last = len(stage_bits) - 1
     parts = (bulk,)
 
     def send_stage(parts, k):
         return tuple(over_both(x, bit) for x, bit in zip(parts, stage_bits[k]))
 
     received = send_stage(parts, 0)
-    received, gains = tie((received, gains))
+    received, far = tie((received, far))
     cnt = counts
     carried = ()
     saved = []
-    for k, (mols, rows) in enumerate(plan):
-        if k < len(stage_bits) - 1:
+    for k, (mol, rows, at, place) in enumerate(plan):
+        if k < last - 1:
             parts = tuple(map(join, parts, received))
             if k + 1 == nz:
                 parts = (parts[0][:, :cut], parts[0][:, cut:])
             cnt, parts = tie((cnt, parts))
-        if k < len(stage_bits) - 2:
             received = send_stage(parts, k + 1)
-        new_pair, exps, *rest = attend_forward_call(mols, cnt, rows, weights, gains, pair, carried)
-        if k < len(stage_bits) - 2:
-            received, rest = tie((received, rest))
-        carried = (new_pair, exps)
-        saved.append(rest)
-    a_pair = (parts[0], over_both(parts[0], bits_a[-1]))
-    b_pair = (parts[1], over_both(parts[1], bits_b[-1]))
-    mixed_theirs = jnp.concatenate([s[2] for s in saved[1 : 1 + per]], 0)
+        else:
+            cnt, received = tie((cnt, received))
+            a_parts, b_parts = (
+                [x, y, over_both(x, bit), over_both(y, bit)]
+                for x, y, bit in zip(parts, received, stage_bits[last])
+            )
+        if k == 0:
+            results = attend_forward_call(
+                info, mol, cnt, rows, at, (gathered, far), pair, carried, place, batch_bits, shard
+            )
+            weights, gains = results[6:]
+        else:
+            results = attend_forward_call(
+                info, mol, cnt, rows, at, (weights, gains), pair, carried, place
+            )
+        new_pair, exps, mixed, hid_t, qkv_t, inverse = results[:6]
+        if k < last - 1:
+            received, inverse = tie((received, inverse))
+        carried = (new_pair, exps, mixed) if place[0] + 1 < place[1] else (new_pair, exps)
+        saved.append((mixed, hid_t, (qkv_t, inverse)))
+    mixed_theirs = saved[per][0]
+    mixed_mine = [saved[0][0], *[s[0] for s in saved[1 + per :]]]
     mixed_other = over_head(mixed_theirs)
-    mixed_mine = jnp.concatenate([saved[0][2], *[s[2] for s in saved[1 + per :]]], 0)
-
-    me = (2 * b + h)[None]
-    output, first, gm_mine, gm_other, ga0, ga1, gb0, gb1 = layer_call(
-        me, atoms, mixed_mine, mixed_other, out_cot, gains, a_pair, b_pair, bits_a, bits_b
+
+    output, first, gm_mine, gm_other, *pieces = layer_call(
+        info, atoms, mixed_mine, mixed_other, out_cot, gains, a_parts, b_parts, bits_a, bits_b
     )
     gm_received = over_head(gm_other)
 
-    def scatter_stage(parts, k):
-        if k == nz - 1:
-            parts = (jnp.concatenate(parts, 1),)
-        return tuple(
-            add(keep, over_both(send, bit))
-            for (keep, send), bit in zip(map(halves, parts), stage_bits[k])
-        )
-
-    parts = (add(ga0, over_both(ga1, bits_a[-1])), add(gb0, over_both(gb1, bits_b[-1])))
-    gm_parts = [gm_mine[:length]]
-    gm_parts += [gm_received[k * length : (k + 1) * length] for k in range(per)]
-    gm_parts += [gm_mine[k * length : (k + 1) * length] for k in range(1, per)]
+    def scatter_core(piece, bit):
+        low, high, far_low, far_high = piece
+        return add(low, over_both(far_low, bit)), add(high, over_both(far_high, bit))
+
+    parts = [scatter_core(p, bit) for p, bit in zip((pieces[:4], pieces[4:]), stage_bits[last])]
+    send_halves = lambda parts, k: [over_both(high, bit) for (_, high), bit in zip(parts, stage_bits[k])]
+    add_halves = lambda parts, received: [add(low, r) for (low, _), r in zip(parts, received)]
     carried = ()
     grads = []
-    stage = len(stage_bits) - 2
     cnt = counts
-    for k, ((mols, _), gm, (hid_t, qkv, mixed, inverse)) in enumerate(zip(plan, gm_parts, saved)):
-        if k > 0:
+    stage = last - 1
+    for k, (mol, _, at, place) in enumerate(plan):
+        if k == 1:
             cnt, parts = tie((cnt, parts))
-            parts = scatter_stage(parts, stage)
+            received = send_halves(parts, stage)
+        elif k == len(plan) - 1:
+            cnt, sums = tie((cnt, add_halves(parts, received)))
+            parts = [halves(x) for x in sums]
             stage -= 1
-        pair_grad, *rest = attend_backward_call(
-            mols, cnt, gm, mixed, inverse, qkv, weights, exps, pair_cot, carried
+            received = send_halves(parts, stage)
+        mixed = mixed_theirs if place[1] > 1 else saved[k][0]
+        gm = gm_received if place[1] > 1 else gm_mine
+        pair_grad, gh, gp = attend_backward_call(
+            info, mol, cnt, gm, at, mixed, place[0], saved[k][2], weights, exps, pair_cot, carried, place
         )
-        carried = (pair_grad,)
-        grads.append(rest)
-    hidden_received = over_head(jnp.concatenate([g[1] for g in grads[1 : 1 + per]], 0))
-    near, far = project_grad_call(
-        me_batch, [s[0] for s in saved], [g[0] for g in grads], batch_bits
-    )
+        carried = (pair_grad, gh) if place[0] + 1 < place[1] else (pair_grad,)
+        grads.append((gh, gp))
+    hidden_received = over_head(grads[per][0])
+    gps, received = tie(([g[1] for g in grads], received))
+    near, far = project_grad_call(info, [s[1] for s in saved], gps, batch_bits)
     near = add(near, over_batch(far, batch_bits[-1]))
+    near, received = tie((near, received))
+    bulk = jnp.concatenate(add_halves(parts, received), 1)
     for bit in batch_bits[-2::-1]:
         keep, send = halves(near)
         near = add(keep, over_batch(send, bit))
+        if stage > 0:
+            stage -= 1
+            keep, send = halves(bulk)
+            bulk = add(keep, over_both(send, bits_a[stage]))
     qkv_grad = near[0].reshape(qkv_weight.shape).astype(F32)
     gain_part = jnp.sum(qkv_grad * qkv_weight.astype(F32), (0, 2)).reshape(2, shard)
     gain_mine = lax.dynamic_index_in_dim(gain_part, h, 0, False)
     gain_other = over_head(lax.dynamic_index_in_dim(gain_part, 1 - h, 0, False))
     gain_one_grad = (gain_mine + gain_other) / ln1_gain
-    atoms_grad = last_call(atoms, gains, first, grads[0][1], grads[-1][1], hidden_received)
-    while stage >= 0:
-        parts = scatter_stage(parts, stage)
-        stage -= 1
-    bulk = parts[0][0].astype(F32)
+    atoms_grad = last_call(atoms, gains, first, grads[0][0], grads[-1][0], hidden_received)
+    bulk = bulk[0].astype(F32)
     shard_rows = w_in.shape[0]
     in_grad = jnp.concatenate([bulk[k * shard_rows : (k + 1) * shard_rows] for k in range(blocks)], 1)
     out_grad = jnp.concatenate([bulk[blocks * shard_rows : cut, k * width : (k + 1) * width] for k in range(2)], 0)

time: 207 us -> 183 us (0.88)
  Pallas kernels: 106 us -> 86 us
  other arithmetic: 17.2 us -> 12.4 us
  local copies, waits for them, and re-layouts: 12.5 us -> 9.01 us
  starting transfers between devices: 32.8 us -> 35.4 us
  waiting for transfers between devices: 36.1 us -> 38.6 us
    pallas_call x9 -> x8, Pallas kernels: 85.2 us -> 66.5 us  [the longest x4 34.3 us: attend_backward_call(): pl.pallas_call(partial(attend_backward_kernel, hb=hb, scale=8 ** (-0.5),...]
    concatenate x7 -> x5, other arithmetic: 6.58 us -> 0.18 us  [join(): return jnp.concatenate([values, received], 0)]
    ppermute x30 -> x34, starting transfers between devices: 32.8 us -> 35.4 us  [swap(): return lax.ppermute(values, axes, [(i, i ^ bit) for i in range(count)])]
    ppermute x30 -> x34, waiting for transfers between devices: 36.1 us -> 38.6 us  [swap(): return lax.ppermute(values, axes, [(i, i ^ bit) for i in range(count)])]
    unnamed x81 -> x38, local copies, waits for them, and re-layouts: 8.06 us -> 5.82 us
    convert_element_type x11 -> x13, other arithmetic: 3.45 us -> 5.64 us  [add(): return (kept.astype(F32) + received.astype(F32)).astype(BF16)]
  transfers between devices with their start and end apart: 30 -> 34, of which waited for: 11 -> 15; matrix products, arithmetic and copies ran while one was open for 7% -> 7% of each run, Pallas kernels for 43% -> 37%
where the time goes in v3:
time: 183 us; the launch traced here: 182 us
  Pallas kernels  86 us (47%)
  waiting for transfers between devices  38.6 us (21%)
  starting transfers between devices  35.4 us (19%)
  other arithmetic  12.4 us (7%)
  local copies, waits for them, and re-layouts  9.01 us (5%)
    ppermute x34, waiting for transfers between devices, swap(): return lax.ppermute(values, axes, [(i, i ^ bit) for i in range(count)])  38.6 us
    ppermute x34, starting transfers between devices, swap(): return lax.ppermute(values, axes, [(i, i ^ bit) for i in range(count)])  35.4 us
    pallas_call x4, Pallas kernels, attend_backward_call(): pl.pallas_call(partial(attend_backward_kernel, hb=hb, scale=8 ** (-0.5),...  34.3 us
    pallas_call x4, Pallas kernels, attend_forward_call(): pl.pallas_call(partial(attend_forward_kernel, hb=hb, scale=8 ** (-0.5), c...  32.2 us
    pallas_call x1, Pallas kernels, layer_call(): pl.pallas_call(partial(layer_kernel, bits_a=bits_a, bits_b=bits_b), grid_...  16.3 us
    unnamed x38, local copies, waits for them, and re-layouts  5.82 us
    convert_element_type x13, other arithmetic, add(): return (kept.astype(F32) + received.astype(F32)).astype(BF16)  5.64 us
  transfers between devices with their start and end apart: 34, of which 15 were waited for; matrix products, arithmetic and copies ran while one was open for 7% of the time, Pallas kernels for 37%

profile of v3, /device:TPU:0, one launch (start us, length us, event | category | flops | bytes accessed | tf_op | source)
XLA Modules:
  0.0 182.3 jit_solution(18167286270751554861)
XLA Ops:
  1.5 2.9 %collective-permute-start = (bf16[1,64]{1,0:T(2,128)(2,1)S(1)}, bf16[1,64]{1,0:T(2,128)(2,1)S(1)}, u32[]{:S(2)}, u32[]{:S(2)}) collective-permute-start(bf16[1,64]{1,0:T(2,128)(2,1)S(1)} %maximum_bitcast_fusion.1), channel_id=1, source_target_pairs={{0,1},{1,0},{2,3},{3,2},{4,5},{5,4},{6,7},{7,6},{8,9},{9,8},{10,11... | collective-permute-start | bytes 392 | tf_op jit(solution)/shard_map/ppermute | solution.py:257
  4.4 1.5 collective-permute-done
  6.0 0.8 maximum_bitcast_fusion
  6.8 3.1 %collective-permute-start.1 = (bf16[1,112,256]{2,1,0:T(8,128)(2,1)S(1)}, bf16[1,112,256]{2,1,0:T(8,128)(2,1)S(1)}, u32[]{:S(2)}, u32[]{:S(2)}) collective-permute-start(bf16[1,112,256]{2,1,0:T(8,128)(2,1)S(1)} %maximum_bitcast_fusion), channel_id=1, source_target_pairs={{0,16},{2,18},{4,20},{6,22},{8,24},{10,26},{12,28},{14,30},{16,0},... | collective-permute-start | bytes 172040 | tf_op jit(solution)/shard_map/ppermute | solution.py:257
  13.5 1.6 collective-permute-start.2
  15.2 0.8 constant_dynamic-update-slice_fusion
  16.0 2.4 %collective-permute-done.2 = bf16[2,112,256]{2,1,0:T(8,128)(2,1)S(1)} collective-permute-done((bf16[2,112,256]{2,1,0:T(8,128)(2,1)S(1)}, bf16[2,112,256]{2,1,0:T(8,128)(2,1)S(1)}, u32[]{:S(2)}, u32[]{:S(2)}) %collective-permute-start.2) | collective-permute-done | bytes 114720 | tf_op jit(solution)/shard_map/ppermute | solution.py:257
  18.4 1.6 collective-permute-start.4
  20.0 4.5 %collective-permute-done.4 = bf16[4,112,256]{2,1,0:T(8,128)(2,1)S(1)} collective-permute-done((bf16[4,112,256]{2,1,0:T(8,128)(2,1)S(1)}, bf16[4,112,256]{2,1,0:T(8,128)(2,1)S(1)}, u32[]{:S(2)}, u32[]{:S(2)}) %collective-permute-start.4) | collective-permute-done | bytes 229408 | tf_op jit(solution)/shard_map/ppermute | solution.py:257
  24.6 1.6 collective-permute-start.3
  26.2 1.5 collective-permute-start.9
  27.8 7.2 %collective-permute-done.3 = bf16[1,144,512]{2,1,0:T(8,128)(2,1)S(1)} collective-permute-done((bf16[1,144,512]{2,1,0:T(8,128)(2,1)S(1)}, bf16[1,144,512]{2,1,0:T(8,128)(2,1)S(1)}, u32[]{:S(2)}, u32[]{:S(2)}) %collective-permute-start.3) | collective-permute-done | bytes 147488 | tf_op jit(solution)/shard_map/ppermute | solution.py:257
  35.1 1.0 copy-done
  36.8 8.2 %attend_forward.4 = (bf16[4,32,256,256]{3,2,1,0:T(8,128)(2,1)}, bf16[4,32,256,256]{3,2,1,0:T(8,128)(2,1)}, bf16[256,256]{1,0:T(8,128)(2,1)S(1)}, bf16[512,256]{1...) custom-call(s32[2]{0:T(128)S(1)} %pad_add_fusion.info_ref.me_ref, ...), custom_call_target="tpu_custom_call" | custom-call | flops 2147483648 | bytes 12582912 | tf_op jit(solution)/shard_map/attend_forward/pallas_call | solution.py:412
  45.0 1.6 collective-permute-start.7
  46.6 1.5 collective-permute-start.8
  48.2 8.0 %attend_forward.5 = (bf16[4,32,256,256]{3,2,1,0:T(8,128)(2,1)}, bf16[4,32,256,256]{3,2,1,0:T(8,128)(2,1)}, bf16[512,256]{1,0:T(8,128)(2,1)S(1)}, bf16[512,256]{1...) custom-call(s32[2]{0:T(128)S(1)} %pad_add_fusion.info_ref.me_ref, ...), custom_call_target="tpu_custom_call", output_to_operand_aliasing={{0}: (6, {}), {1}: (7, {})} | custom-call | flops 2147483648 | bytes 12582912 | tf_op jit(solution)/shard_map/attend_forward/pallas_call | solution.py:412
  57.6 7.9 %attend_forward.6 = (bf16[4,32,256,256]{3,2,1,0:T(8,128)(2,1)}, bf16[4,32,256,256]{3,2,1,0:T(8,128)(2,1)}, bf16[512,256]{1,0:T(8,128)(2,1)S(1)}, bf16[512,256]{1...) custom-call(s32[2]{0:T(128)S(1)} %pad_add_fusion.info_ref.me_ref, ...), custom_call_target="tpu_custom_call", output_to_operand_aliasing={{0}: (6, {}), {1}: (7, {}), {2}: (8, {})} | custom-call | flops 2147483648 | bytes 12582912 | tf_op jit(solution)/shard_map/attend_forward/pallas_call | solution.py:412
  65.6 3.9 %collective-permute-done.11.rest_5_ = bf16[8,64,512]{2,1,0:T(8,128)(2,1)S(1)} collective-permute-done((bf16[8,64,512]{2,1,0:T(8,128)(2,1)S(1)}, bf16[8,64,512]{2,1,0:T(8,128)(2,1)S(1)}, u32[]{:S(2)}, u32[]{:S(2)}) %collective-permute-start.11) | collective-permute-done | bytes 524320 | tf_op jit(solution)/shard_map/ppermute | solution.py:257
  69.5 2.7 %collective-permute-done.10.rest_1_ = bf16[8,80,512]{2,1,0:T(8,128)(2,1)S(1)} collective-permute-done((bf16[8,80,512]{2,1,0:T(8,128)(2,1)S(1)}, bf16[8,80,512]{2,1,0:T(8,128)(2,1)S(1)}, u32[]{:S(2)}, u32[]{:S(2)}) %collective-permute-start.10) | collective-permute-done | bytes 655392 | tf_op jit(solution)/shard_map/ppermute | solution.py:257
  73.1 8.0 %attend_forward.7 = (bf16[4,32,256,256]{3,2,1,0:T(8,128)(2,1)}, bf16[4,32,256,256]{3,2,1,0:T(8,128)(2,1)}, bf16[256,256]{1,0:T(8,128)(2,1)S(1)}, bf16[512,256]{1...) custom-call(s32[2]{0:T(128)S(1)} %pad_add_fusion.info_ref.me_ref, ...), custom_call_target="tpu_custom_call", output_to_operand_aliasing={{0}: (6, {}), {1}: (7, {})} | custom-call | flops 2147483648 | bytes 12582912 | tf_op jit(solution)/shard_map/attend_forward/pallas_call | solution.py:412
  81.4 0.8 copy-done.13
  82.6 16.3 %layer.1 = (bf16[512,512]{1,0:T(8,128)(2,1)}, f32[512,512]{1,0:T(8,128)}, bf16[512,256]{1,0:T(8,128)(2,1)S(1)}, bf16[512,256]{1,0:T(8,128)(2,1)S(1)}, bf16[8,80,...) custom-call(s32[2]{0:T(128)S(1)} %pad_add_fusion.info_ref.me_ref, ...), custom_call_target="tpu_custom_call" | custom-call | flops 6442450944 | bytes 8388608 | tf_op jit(solution)/shard_map/layer/pallas_call | solution.py:660
  100.0 1.3 collective-permute-start.23
  101.4 1.0 collective-permute-done.20
  102.8 1.3 add_convert_fusion.2
  104.1 1.3 add_convert_fusion.1
  105.4 1.3 collective-permute-start.21
  107.2 8.6 %attend_backward.4 = (bf16[4,32,256,256]{3,2,1,0:T(8,128)(2,1)}, bf16[256,512]{1,0:T(8,128)(2,1)S(1)}, bf16[3,256,256]{2,1,0:T(8,128)(2,1)S(1)}) custom-call(s32[2]{0:T(128)S(1)} %pad_add_fusion.info_ref.me_ref, s32[4]{0:T(128)S(1)} %copy-done.4, bf16[512,256]{1,0:T(8,128)(2,1)S(1)} %get-tuple-element.148.gm_ref, ...), custom_call_target="tpu_custom_call" | custom-call | flops 3221225472 | bytes 12582912 | tf_op jit(solution)/shard_map/attend_backward/pallas_call | solution.py:516
  115.8 8.6 %attend_backward.5 = (bf16[4,32,256,256]{3,2,1,0:T(8,128)(2,1)}, bf16[512,512]{1,0:T(8,128)(2,1)S(1)}, bf16[3,256,256]{2,1,0:T(8,128)(2,1)S(1)}) custom-call(s32[2]{0:T(128)S(1)} %pad_add_fusion.info_ref.me_ref, s32[4]{0:T(128)S(1)} %copy-done.4, bf16[512,256]{1,0:T(8,128)(2,1)S(1)} %collective-permute-done.23.gm_ref, ...), custom_call_target="tpu_custom_call", output_to_operand_aliasing={{0}: (10, {})} | custom-call | flops 3221225472 | bytes 12582912 | tf_op jit(solution)/shard_map/attend_backward/pallas_call | solution.py:516
  124.8 1.6 collective-permute-start.25
  126.4 8.6 %attend_backward.6 = (bf16[4,32,256,256]{3,2,1,0:T(8,128)(2,1)}, bf16[512,512]{1,0:T(8,128)(2,1)S(1)}, bf16[3,256,256]{2,1,0:T(8,128)(2,1)S(1)}) custom-call(s32[2]{0:T(128)S(1)} %pad_add_fusion.info_ref.me_ref, s32[4]{0:T(128)S(1)} %copy-done.4, ...), custom_call_target="tpu_custom_call", output_to_operand_aliasing={{0}: (10, {}), {1}: (11, {})} | custom-call | flops 3221225472 | bytes 12582912 | tf_op jit(solution)/shard_map/attend_backward/pallas_call | solution.py:516
  135.0 0.8 collective-permute-start.26
  135.8 8.6 %attend_backward.7 = (bf16[4,32,256,256]{3,2,1,0:T(8,128)(2,1)}, bf16[256,512]{1,0:T(8,128)(2,1)S(1)}, bf16[3,256,256]{2,1,0:T(8,128)(2,1)S(1)}) custom-call(s32[2]{0:T(128)S(1)} %pad_add_fusion.info_ref.me_ref, s32[4]{0:T(128)S(1)} %copy-done.4, bf16[512,256]{1,0:T(8,128)(2,1)S(1)} %get-tuple-element.148.gm_ref, ...), custom_call_target="tpu_custom_call", output_to_operand_aliasing={{0}: (10, {})} | custom-call | flops 3221225472 | bytes 12582912 | tf_op jit(solution)/shard_map/attend_backward/pallas_call | solution.py:516
  144.4 1.6 project_grad.1
  146.0 1.3 collective-permute-start.24
  148.6 6.2 %collective-permute-done.28 = bf16[4,96,256]{2,1,0:T(8,128)(2,1)S(1)} collective-permute-done((bf16[4,96,256]{2,1,0:T(8,128)(2,1)S(1)}, bf16[4,96,256]{2,1,0:T(8,128)(2,1)S(1)}, u32[]{:S(2)}, u32[]{:S(2)}) %collective-permute-start.28) | collective-permute-done | bytes 196640 | tf_op jit(solution)/shard_map/ppermute | solution.py:257
  155.7 1.7 collective-permute-start.29
  158.4 1.9 %collective-permute-done.24.recv_ref = bf16[512,512]{1,0:T(8,128)(2,1)S(1)} collective-permute-done((bf16[512,512]{1,0:T(8,128)(2,1)S(1)}, bf16[512,512]{1,0:T(8,128)(2,1)S(1)}, u32[]{:S(2)}, u32[]{:S(2)}) %collective-permute-start.24) | collective-permute-done | bytes 524320 | tf_op jit(solution)/shard_map/ppermute | solution.py:257
  160.4 1.6 last_norm.1
  162.0 1.0 add_convert_fusion.12
  163.0 3.2 %collective-permute-start.30 = (bf16[1,96,256]{2,1,0:T(8,128)(2,1)S(1)}, bf16[1,96,256]{2,1,0:T(8,128)(2,1)S(1)}, u32[]{:S(2)}, u32[]{:S(2)}) collective-permute-start(bf16[1,96,256]{2,1,0:T(8,128)(2,1)S(1)} %slice.141), channel_id=1, source_target_pairs={{0,16},{2,18},{4,20},{6,22},{8,24},{10,26},{12,28},{14,30},{16,0},... | collective-permute-start | bytes 147464 | tf_op jit(solution)/shard_map/ppermute | solution.py:257
  166.1 0.8 collective-permute-done.31
  166.9 1.1 add_convert_fusion.8
  168.7 1.6 multiply_reduce_fusion.1
  170.3 1.3 collective-permute-start.33
  171.6 2.5 %collective-permute-start.32 = (bf16[1,144,512]{2,1,0:T(8,128)(2,1)S(1)}, bf16[1,144,512]{2,1,0:T(8,128)(2,1)S(1)}, u32[]{:S(2)}, u32[]{:S(2)}) collective-permute-start(bf16[1,144,512]{2,1,0:T(8,128)(2,1)S(1)} %slice.145), channel_id=1, source_target_pairs={{0,16},{1,17},{2,18},{3,19},{4,20},{5,21},{6,22},{7,23},{8,24},{9,... | collective-permute-start | bytes 442376 | tf_op jit(solution)/shard_map/ppermute | solution.py:257
  174.6 5.0 %collective-permute-done.32 = bf16[1,144,512]{2,1,0:T(8,128)(2,1)S(1)} collective-permute-done((bf16[1,144,512]{2,1,0:T(8,128)(2,1)S(1)}, bf16[1,144,512]{2,1,0:T(8,128)(2,1)S(1)}, u32[]{:S(2)}, u32[]{:S(2)}) %collective-permute-start.32) | collective-permute-done | bytes 147488 | tf_op jit(solution)/shard_map/ppermute | solution.py:257
  (117 shorter events, 18.1 us)
Async XLA Ops:
  1.5 4.5 %collective-permute-start = (bf16[1,64]{1,0:T(2,128)(2,1)S(1)}, bf16[1,64]{1,0:T(2,128)(2,1)S(1)}, u32[]{:S(2)}, u32[]{:S(2)}) collective-permute-start(bf16[1,64]{1,0:T(2,128)(2,1)S(1)} %maximum_bitcast_fusion.1), channel_id=1, source_target_pairs={{0,1},{1,0},{2,3},{3,2},{4,5},{5,4},{6,7},{7,6},{8,9},{9,8},{10,11... | collective-permute-start | bytes 392 | tf_op jit(solution)/shard_map/ppermute | solution.py:257
  6.8 6.7 %collective-permute-start.1 = (bf16[1,112,256]{2,1,0:T(8,128)(2,1)S(1)}, bf16[1,112,256]{2,1,0:T(8,128)(2,1)S(1)}, u32[]{:S(2)}, u32[]{:S(2)}) collective-permute-start(bf16[1,112,256]{2,1,0:T(8,128)(2,1)S(1)} %maximum_bitcast_fusion), channel_id=1, source_target_pairs={{0,16},{2,18},{4,20},{6,22},{8,24},{10,26},{12,28},{14,30},{16,0},... | collective-permute-start | bytes 172040 | tf_op jit(solution)/shard_map/ppermute | solution.py:257
  13.5 4.9 %collective-permute-start.2 = (bf16[2,112,256]{2,1,0:T(8,128)(2,1)S(1)}, bf16[2,112,256]{2,1,0:T(8,128)(2,1)S(1)}, u32[]{:S(2)}, u32[]{:S(2)}) collective-permute-start(bf16[2,112,256]{2,1,0:T(8,128)(2,1)S(1)} %pad_maximum_fusion.6), channel_id=1, source_target_pairs={{0,8},{2,10},{4,12},{6,14},{8,0},{10,2},{12,4},{14,6},{16,24},{18,... | collective-permute-start | bytes 344072 | tf_op jit(solution)/shard_map/ppermute | solution.py:257
  18.4 6.1 %collective-permute-start.4 = (bf16[4,112,256]{2,1,0:T(8,128)(2,1)S(1)}, bf16[4,112,256]{2,1,0:T(8,128)(2,1)S(1)}, u32[]{:S(2)}, u32[]{:S(2)}) collective-permute-start(bf16[4,112,256]{2,1,0:T(8,128)(2,1)S(1)} %pad_maximum_fusion.4), channel_id=1, source_target_pairs={{0,4},{2,6},{4,0},{6,2},{8,12},{10,14},{12,8},{14,10},{16,20},{18,... | collective-permute-start | bytes 688136 | tf_op jit(solution)/shard_map/ppermute | solution.py:257
  24.5 10.4 %collective-permute-start.5 = (bf16[8,112,256]{2,1,0:T(8,128)(2,1)S(1)}, bf16[8,112,256]{2,1,0:T(8,128)(2,1)S(1)}, u32[]{:S(2)}, u32[]{:S(2)}) collective-permute-start(bf16[8,112,256]{2,1,0:T(8,128)(2,1)S(1)} %constant_dynamic-update-slice_fusion.6.w_ref), channel_id=1, source_target_pairs={{0,2},{2,0},{4,6},{6,4},{8,10},{10,8},{12,14},{14,12},{16,18},{18,... | collective-permute-start | bytes 1376264 | tf_op jit(solution)/shard_map/ppermute | solution.py:257
  24.6 10.3 %collective-permute-start.3 = (bf16[1,144,512]{2,1,0:T(8,128)(2,1)S(1)}, bf16[1,144,512]{2,1,0:T(8,128)(2,1)S(1)}, u32[]{:S(2)}, u32[]{:S(2)}) collective-permute-start(bf16[1,144,512]{2,1,0:T(8,128)(2,1)S(1)} %bitcast.30), channel_id=1, source_target_pairs={{0,16},{1,17},{2,18},{3,19},{4,20},{5,21},{6,22},{7,23},{8,24},{9,... | collective-permute-start | bytes 442376 | tf_op jit(solution)/shard_map/ppermute | solution.py:257
  26.2 21.9 %collective-permute-start.9 = (bf16[512,512]{1,0:T(8,128)(2,1)}, bf16[512,512]{1,0:T(8,128)(2,1)S(1)}, u32[]{:S(2)}, u32[]{:S(2)}) collective-permute-start(bf16[512,512]{1,0:T(8,128)(2,1)} %atoms_ref.7), channel_id=1, source_target_pairs={{0,1},{1,0},{2,3},{3,2},{4,5},{5,4},{6,7},{7,6},{8,9},{9,8},{10,11... | collective-permute-start | bytes 1572872 | tf_op jit(solution)/shard_map/ppermute | solution.py:257
  35.0 10.0 %collective-permute-start.6 = (bf16[2,144,512]{2,1,0:T(8,128)(2,1)S(1)}, bf16[2,144,512]{2,1,0:T(8,128)(2,1)S(1)}, u32[]{:S(2)}, u32[]{:S(2)}) collective-permute-start(bf16[2,144,512]{2,1,0:T(8,128)(2,1)S(1)} %pad_maximum_fusion.3), channel_id=1, source_target_pairs={{0,8},{1,9},{2,10},{3,11},{4,12},{5,13},{6,14},{7,15},{8,0},{9,1},... | collective-permute-start | bytes 884744 | tf_op jit(solution)/shard_map/ppermute | solution.py:257
  35.1 1.0 copy-start
  45.0 11.2 %collective-permute-start.7 = (bf16[4,80,512]{2,1,0:T(8,128)(2,1)S(1)}, bf16[4,80,512]{2,1,0:T(8,128)(2,1)S(1)}, u32[]{:S(2)}, u32[]{:S(2)}) collective-permute-start(bf16[4,80,512]{2,1,0:T(8,128)(2,1)S(1)} %slice.136), channel_id=1, source_target_pairs={{0,4},{1,5},{2,6},{3,7},{4,0},{5,1},{6,2},{7,3},{8,12},{9,13},{10,... | collective-permute-start | bytes 983048 | tf_op jit(solution)/shard_map/ppermute | solution.py:257
  46.6 9.6 %collective-permute-start.8 = (bf16[4,64,512]{2,1,0:T(8,128)(2,1)S(1)}, bf16[4,64,512]{2,1,0:T(8,128)(2,1)S(1)}, u32[]{:S(2)}, u32[]{:S(2)}) collective-permute-start(bf16[4,64,512]{2,1,0:T(8,128)(2,1)S(1)} %slice.137), channel_id=1, source_target_pairs={{0,1},{1,0},{2,3},{3,2},{4,5},{5,4},{6,7},{7,6},{8,9},{9,8},{10,11... | collective-permute-start | bytes 786440 | tf_op jit(solution)/shard_map/ppermute | solution.py:257
  56.3 9.3 %copy-start.8 = (bf16[8,80,512]{2,1,0:T(8,128)(2,1)}, bf16[8,80,512]{2,1,0:T(8,128)(2,1)S(1)}, u32[]{:S(2)}) copy-start(bf16[8,80,512]{2,1,0:T(8,128)(2,1)S(1)} %pad_maximum_fusion.rest_0_) | copy-start | bytes 1966084
  56.3 15.8 %collective-permute-start.10 = (bf16[8,80,512]{2,1,0:T(8,128)(2,1)S(1)}, bf16[8,80,512]{2,1,0:T(8,128)(2,1)S(1)}, u32[]{:S(2)}, u32[]{:S(2)}) collective-permute-start(bf16[8,80,512]{2,1,0:T(8,128)(2,1)S(1)} %pad_maximum_fusion.rest_0_), channel_id=1, source_target_pairs={{0,1},{1,0},{2,3},{3,2},{4,5},{5,4},{6,7},{7,6},{8,9},{9,8},{10,11... | collective-permute-start | bytes 1966088 | tf_op jit(solution)/shard_map/ppermute | solution.py:257
  56.9 12.6 %collective-permute-start.11 = (bf16[8,64,512]{2,1,0:T(8,128)(2,1)S(1)}, bf16[8,64,512]{2,1,0:T(8,128)(2,1)S(1)}, u32[]{:S(2)}, u32[]{:S(2)}) collective-permute-start(bf16[8,64,512]{2,1,0:T(8,128)(2,1)S(1)} %pad_maximum_fusion.1.rest_4_), channel_id=1, source_target_pairs={{0,4},{1,5},{2,6},{3,7},{4,0},{5,1},{6,2},{7,3},{8,12},{9,13},{10,... | collective-permute-start | bytes 1572872 | tf_op jit(solution)/shard_map/ppermute | solution.py:257
  57.6 23.8 %collective-permute-start.13 = (bf16[8,80,512]{2,1,0:T(8,128)(2,1)S(1)}, bf16[8,80,512]{2,1,0:T(8,128)(2,1)S(1)}, u32[]{:S(2)}, u32[]{:S(2)}) collective-permute-start(bf16[8,80,512]{2,1,0:T(8,128)(2,1)S(1)} %pad_maximum_fusion.rest_0_), channel_id=1, source_target_pairs={{0,2},{1,3},{2,0},{3,1},{4,6},{5,7},{6,4},{7,5},{8,10},{9,11},{10,... | collective-permute-start | bytes 1966088 | tf_op jit(solution)/shard_map/ppermute | solution.py:257
  72.2 9.0 %copy-start.12 = (bf16[8,80,512]{2,1,0:T(8,128)(2,1)}, bf16[8,80,512]{2,1,0:T(8,128)(2,1)S(1)}, u32[]{:S(2)}) copy-start(bf16[8,80,512]{2,1,0:T(8,128)(2,1)S(1)} %collective-permute-done.10.rest_1_) | copy-start | bytes 1966084
  72.2 9.3 %collective-permute-start.14 = (bf16[8,80,512]{2,1,0:T(8,128)(2,1)S(1)}, bf16[8,80,512]{2,1,0:T(8,128)(2,1)S(1)}, u32[]{:S(2)}, u32[]{:S(2)}) collective-permute-start(bf16[8,80,512]{2,1,0:T(8,128)(2,1)S(1)} %collective-permute-done.10.rest_1_), channel_id=1, source_target_pairs={{0,2},{1,3},{2,0},{3,1},{4,6},{5,7},{6,4},{7,5},{8,10},{9,11},{10,... | collective-permute-start | bytes 1966088 | tf_op jit(solution)/shard_map/ppermute | solution.py:257
  72.2 9.2 %collective-permute-start.15 = (bf16[8,64,512]{2,1,0:T(8,128)(2,1)S(1)}, bf16[8,64,512]{2,1,0:T(8,128)(2,1)S(1)}, u32[]{:S(2)}, u32[]{:S(2)}) collective-permute-start(bf16[8,64,512]{2,1,0:T(8,128)(2,1)S(1)} %pad_maximum_fusion.1.rest_4_), channel_id=1, source_target_pairs={{0,2},{1,3},{2,0},{3,1},{4,6},{5,7},{6,4},{7,5},{8,10},{9,11},{10,... | collective-permute-start | bytes 1572872 | tf_op jit(solution)/shard_map/ppermute | solution.py:257
  72.7 8.7 %collective-permute-start.16 = (bf16[8,64,512]{2,1,0:T(8,128)(2,1)S(1)}, bf16[8,64,512]{2,1,0:T(8,128)(2,1)S(1)}, u32[]{:S(2)}, u32[]{:S(2)}) collective-permute-start(bf16[8,64,512]{2,1,0:T(8,128)(2,1)S(1)} %collective-permute-done.11.rest_5_), channel_id=1, source_target_pairs={{0,2},{1,3},{2,0},{3,1},{4,6},{5,7},{6,4},{7,5},{8,10},{9,11},{10,... | collective-permute-start | bytes 1572872 | tf_op jit(solution)/shard_map/ppermute | solution.py:257
  72.7 8.7 %collective-permute-start.12 = (bf16[512,256]{1,0:T(8,128)(2,1)S(1)}, bf16[512,256]{1,0:T(8,128)(2,1)S(1)}, u32[]{:S(2)}, u32[]{:S(2)}) collective-permute-start(bf16[512,256]{1,0:T(8,128)(2,1)S(1)} %get-tuple-element.142.mixed_ref), channel_id=1, source_target_pairs={{0,1},{1,0},{2,3},{3,2},{4,5},{5,4},{6,7},{7,6},{8,9},{9,8},{10,11... | collective-permute-start | bytes 786440 | tf_op jit(solution)/shard_map/ppermute | solution.py:257
  73.1 9.5 %copy-start.1 = (bf16[512,512]{1,0:T(8,128)(2,1)S(1)}, bf16[512,512]{1,0:T(8,128)(2,1)}, u32[]{:S(2)}) copy-start(bf16[512,512]{1,0:T(8,128)(2,1)} %atoms_ref.7) | copy-start | bytes 1572868
  73.1 9.5 %copy-start.5 = (bf16[512,512]{1,0:T(8,128)(2,1)S(1)}, bf16[512,512]{1,0:T(8,128)(2,1)}, u32[]{:S(2)}) copy-start(bf16[512,512]{1,0:T(8,128)(2,1)} %cot_ref.5) | copy-start | bytes 1572868
  81.1 26.1 %copy-start.3 = (bf16[16,256]{1,0:T(8,128)(2,1)S(1)}, bf16[16,256]{1,0:T(8,128)(2,1)}, u32[]{:S(2)}) copy-start(bf16[16,256]{1,0:T(8,128)(2,1)} %constant.27.clone.mask_ref) | copy-start | bytes 24580
  81.4 1.0 copy-start.15
  81.4 1.2 copy-start.14
  99.0 2.3 %collective-permute-start.19 = (bf16[8,64,512]{2,1,0:T(8,128)(2,1)S(1)}, bf16[8,64,512]{2,1,0:T(8,128)(2,1)S(1)}, u32[]{:S(2)}, u32[]{:S(2)}) collective-permute-start(bf16[8,64,512]{2,1,0:T(8,128)(2,1)S(1)} %get-tuple-element.158), channel_id=1, source_target_pairs={{0,2},{1,3},{2,0},{3,1},{4,6},{5,7},{6,4},{7,5},{8,10},{9,11},{10,... | collective-permute-start | bytes 1572872 | tf_op jit(solution)/shard_map/ppermute | solution.py:257
  99.0 3.4 %collective-permute-start.20 = (bf16[8,64,512]{2,1,0:T(8,128)(2,1)S(1)}, bf16[8,64,512]{2,1,0:T(8,128)(2,1)S(1)}, u32[]{:S(2)}, u32[]{:S(2)}) collective-permute-start(bf16[8,64,512]{2,1,0:T(8,128)(2,1)S(1)} %get-tuple-element.160), channel_id=1, source_target_pairs={{0,2},{1,3},{2,0},{3,1},{4,6},{5,7},{6,4},{7,5},{8,10},{9,11},{10,... | collective-permute-start | bytes 1572872 | tf_op jit(solution)/shard_map/ppermute | solution.py:257
  99.5 3.3 %collective-permute-start.17 = (bf16[8,80,512]{2,1,0:T(8,128)(2,1)}, bf16[8,80,512]{2,1,0:T(8,128)(2,1)S(1)}, u32[]{:S(2)}, u32[]{:S(2)}) collective-permute-start(bf16[8,80,512]{2,1,0:T(8,128)(2,1)} %get-tuple-element.154), channel_id=1, source_target_pairs={{0,2},{1,3},{2,0},{3,1},{4,6},{5,7},{6,4},{7,5},{8,10},{9,11},{10,... | collective-permute-start | bytes 1966088 | tf_op jit(solution)/shard_map/ppermute | solution.py:257
  99.5 4.6 %collective-permute-start.18 = (bf16[8,80,512]{2,1,0:T(8,128)(2,1)}, bf16[8,80,512]{2,1,0:T(8,128)(2,1)S(1)}, u32[]{:S(2)}, u32[]{:S(2)}) collective-permute-start(bf16[8,80,512]{2,1,0:T(8,128)(2,1)} %get-tuple-element.156), channel_id=1, source_target_pairs={{0,2},{1,3},{2,0},{3,1},{4,6},{5,7},{6,4},{7,5},{8,10},{9,11},{10,... | collective-permute-start | bytes 1966088 | tf_op jit(solution)/shard_map/ppermute | solution.py:257
  100.0 15.8 %collective-permute-start.23 = (bf16[512,256]{1,0:T(8,128)(2,1)S(1)}, bf16[512,256]{1,0:T(8,128)(2,1)S(1)}, u32[]{:S(2)}, u32[]{:S(2)}) collective-permute-start(bf16[512,256]{1,0:T(8,128)(2,1)S(1)} %get-tuple-element.169), channel_id=1, source_target_pairs={{0,1},{1,0},{2,3},{3,2},{4,5},{5,4},{6,7},{7,6},{8,9},{9,8},{10,11... | collective-permute-start | bytes 786440 | tf_op jit(solution)/shard_map/ppermute | solution.py:257
  105.4 19.1 %collective-permute-start.21 = (bf16[8,80,512]{2,1,0:T(8,128)(2,1)S(1)}, bf16[8,80,512]{2,1,0:T(8,128)(2,1)S(1)}, u32[]{:S(2)}, u32[]{:S(2)}) collective-permute-start(bf16[8,80,512]{2,1,0:T(8,128)(2,1)S(1)} %add_convert_fusion.1), channel_id=1, source_target_pairs={{0,1},{1,0},{2,3},{3,2},{4,5},{5,4},{6,7},{7,6},{8,9},{9,8},{10,11... | collective-permute-start | bytes 1966088 | tf_op jit(solution)/shard_map/ppermute | solution.py:257
  106.7 17.7 %collective-permute-start.22 = (bf16[8,64,512]{2,1,0:T(8,128)(2,1)S(1)}, bf16[8,64,512]{2,1,0:T(8,128)(2,1)S(1)}, u32[]{:S(2)}, u32[]{:S(2)}) collective-permute-start(bf16[8,64,512]{2,1,0:T(8,128)(2,1)S(1)} %add_convert_fusion.4), channel_id=1, source_target_pairs={{0,4},{1,5},{2,6},{3,7},{4,0},{5,1},{6,2},{7,3},{8,12},{9,13},{10,... | collective-permute-start | bytes 1572872 | tf_op jit(solution)/shard_map/ppermute | solution.py:257
  124.8 19.6 %collective-permute-start.25 = (bf16[4,80,512]{2,1,0:T(8,128)(2,1)S(1)}, bf16[4,80,512]{2,1,0:T(8,128)(2,1)S(1)}, u32[]{:S(2)}, u32[]{:S(2)}) collective-permute-start(bf16[4,80,512]{2,1,0:T(8,128)(2,1)S(1)} %slice.110), channel_id=1, source_target_pairs={{0,4},{1,5},{2,6},{3,7},{4,0},{5,1},{6,2},{7,3},{8,12},{9,13},{10,... | collective-permute-start | bytes 983048 | tf_op jit(solution)/shard_map/ppermute | solution.py:257
  135.0 9.4 %collective-permute-start.26 = (bf16[4,64,512]{2,1,0:T(8,128)(2,1)S(1)}, bf16[4,64,512]{2,1,0:T(8,128)(2,1)S(1)}, u32[]{:S(2)}, u32[]{:S(2)}) collective-permute-start(bf16[4,64,512]{2,1,0:T(8,128)(2,1)S(1)} %slice.111), channel_id=1, source_target_pairs={{0,1},{1,0},{2,3},{3,2},{4,5},{5,4},{6,7},{7,6},{8,9},{9,8},{10,11... | collective-permute-start | bytes 786440 | tf_op jit(solution)/shard_map/ppermute | solution.py:257
  135.8 24.6 %copy-start.2 = (f32[512,512]{1,0:T(8,128)S(1)}, f32[512,512]{1,0:T(8,128)}, u32[]{:S(2)}) copy-start(f32[512,512]{1,0:T(8,128)} %get-tuple-element.147.first_ref) | copy-start | bytes 3145732
  135.8 38.3 %copy-start.10 = (f32[16]{0:T(128)S(1)}, f32[16]{0:T(128)}, u32[]{:S(2)}) copy-start(f32[16]{0:T(128)} %param.20) | copy-start | bytes 196
  135.8 44.6 %copy-start.9 = (bf16[16,2048]{1,0:T(8,128)(2,1)S(1)}, bf16[16,2048]{1,0:T(8,128)(2,1)}, u32[]{:S(2)}) copy-start(bf16[16,2048]{1,0:T(8,128)(2,1)} %param.22) | copy-start | bytes 196612
  135.8 45.4 %copy-start.11 = (f32[16]{0:T(128)S(1)}, f32[16]{0:T(128)}, u32[]{:S(2)}) copy-start(f32[16]{0:T(128)} %param.21) | copy-start | bytes 196
  146.0 1.8 collective-permute-start.27
  146.0 14.3 %collective-permute-start.24 = (bf16[512,512]{1,0:T(8,128)(2,1)S(1)}, bf16[512,512]{1,0:T(8,128)(2,1)S(1)}, u32[]{:S(2)}, u32[]{:S(2)}) collective-permute-start(bf16[512,512]{1,0:T(8,128)(2,1)S(1)} %get-tuple-element.179), channel_id=1, source_target_pairs={{0,1},{1,0},{2,3},{3,2},{4,5},{5,4},{6,7},{7,6},{8,9},{9,8},{10,11... | collective-permute-start | bytes 1572872 | tf_op jit(solution)/shard_map/ppermute | solution.py:257
  147.9 7.0 %collective-permute-start.28 = (bf16[4,96,256]{2,1,0:T(8,128)(2,1)S(1)}, bf16[4,96,256]{2,1,0:T(8,128)(2,1)S(1)}, u32[]{:S(2)}, u32[]{:S(2)}) collective-permute-start(bf16[4,96,256]{2,1,0:T(8,128)(2,1)S(1)} %slice.113), channel_id=1, source_target_pairs={{0,4},{2,6},{4,0},{6,2},{8,12},{10,14},{12,8},{14,10},{16,20},{18,... | collective-permute-start | bytes 589832 | tf_op jit(solution)/shard_map/ppermute | solution.py:257
  148.6 8.7 %copy-start.6 = (bf16[4,64,512]{2,1,0:T(8,128)(2,1)}, bf16[4,64,512]{2,1,0:T(8,128)(2,1)S(1)}, u32[]{:S(2)}) copy-start(bf16[4,64,512]{2,1,0:T(8,128)(2,1)S(1)} %add_convert_fusion.9) | copy-start | bytes 786436
  154.9 3.2 %copy-start.7 = (bf16[4,96,256]{2,1,0:T(8,128)(2,1)}, bf16[4,96,256]{2,1,0:T(8,128)(2,1)S(1)}, u32[]{:S(2)}) copy-start(bf16[4,96,256]{2,1,0:T(8,128)(2,1)S(1)} %add_convert_fusion.10) | copy-start | bytes 589828
  155.7 6.3 %collective-permute-start.29 = (bf16[2,96,256]{2,1,0:T(8,128)(2,1)}, bf16[2,96,256]{2,1,0:T(8,128)(2,1)}, u32[]{:S(2)}, u32[]{:S(2)}) collective-permute-start(bf16[2,96,256]{2,1,0:T(8,128)(2,1)} %slice.139), channel_id=1, source_target_pairs={{0,8},{2,10},{4,12},{6,14},{8,0},{10,2},{12,4},{14,6},{16,24},{18,... | collective-permute-start | bytes 294920 | tf_op jit(solution)/shard_map/ppermute | solution.py:257
  158.1 8.8 %collective-permute-start.31 = (bf16[2,144,512]{2,1,0:T(8,128)(2,1)}, bf16[2,144,512]{2,1,0:T(8,128)(2,1)}, u32[]{:S(2)}, u32[]{:S(2)}) collective-permute-start(bf16[2,144,512]{2,1,0:T(8,128)(2,1)} %pad_maximum_fusion.2), channel_id=1, source_target_pairs={{0,8},{1,9},{2,10},{3,11},{4,12},{5,13},{6,14},{7,15},{8,0},{9,1},... | collective-permute-start | bytes 884744 | tf_op jit(solution)/shard_map/ppermute | solution.py:257
  163.0 5.7 %collective-permute-start.30 = (bf16[1,96,256]{2,1,0:T(8,128)(2,1)S(1)}, bf16[1,96,256]{2,1,0:T(8,128)(2,1)S(1)}, u32[]{:S(2)}, u32[]{:S(2)}) collective-permute-start(bf16[1,96,256]{2,1,0:T(8,128)(2,1)S(1)} %slice.141), channel_id=1, source_target_pairs={{0,16},{2,18},{4,20},{6,22},{8,24},{10,26},{12,28},{14,30},{16,0},... | collective-permute-start | bytes 147464 | tf_op jit(solution)/shard_map/ppermute | solution.py:257
  170.3 3.8 %collective-permute-start.33 = (f32[16]{0:T(128)S(1)}, f32[16]{0:T(128)S(1)}, u32[]{:S(2)}, u32[]{:S(2)}) collective-permute-start(f32[16]{0:T(128)S(1)} %dynamic-slice_bitcast_fusion), channel_id=1, source_target_pairs={{0,1},{1,0},{2,3},{3,2},{4,5},{5,4},{6,7},{7,6},{8,9},{9,8},{10,11... | collective-permute-start | bytes 200 | tf_op jit(solution)/shard_map/ppermute | solution.py:257
  171.6 8.0 %collective-permute-start.32 = (bf16[1,144,512]{2,1,0:T(8,128)(2,1)S(1)}, bf16[1,144,512]{2,1,0:T(8,128)(2,1)S(1)}, u32[]{:S(2)}, u32[]{:S(2)}) collective-permute-start(bf16[1,144,512]{2,1,0:T(8,128)(2,1)S(1)} %slice.145), channel_id=1, source_target_pairs={{0,16},{1,17},{2,18},{3,19},{4,20},{5,21},{6,22},{7,23},{8,24},{9,... | collective-permute-start | bytes 442376 | tf_op jit(solution)/shard_map/ppermute | solution.py:257
  (2 other events, 1.5 us)

commit v4 on v3

--- a/solution.py
+++ b/solution.py
@@ -265,7 +265,7 @@
     return pl.BlockSpec(shape, lambda *_: (0,) * len(shape))
 
 
-def unpack_shards(info_ref, near_ref, far_ref, w_ref, gains_ref, rows_s, bits, shard):
+def unpack_shards(info_ref, near_ref, far_ref, other_ref, w_ref, gains_ref, rows_s, bits, shard):
     b, h = info_ref[0], info_ref[1]
     half = near_ref.shape[0]
     rows = w_ref.shape[1] // (2 * half)
@@ -275,44 +275,73 @@
         at = pl.multiple_of((b ^ relative(p, bits)) * rows, rows)
         for s in range(3):
             w_ref[s, pl.ds(at, rows), :] = ref[q, s * rows : (s + 1) * rows, :]
-        rows_s[p : p + 1, :] = ref[q, 3 * rows : 3 * rows + 1, :].astype(F32)
-    lanes = rows_s.shape[1]
+        rows_s[0, p : p + 1, :] = ref[q, 3 * rows : 3 * rows + 1, :].astype(F32)
+        rows_s[1, p : p + 1, :] = other_ref[p, 0:1, :].astype(F32)
+    lanes = rows_s.shape[2]
     count = 2 * half
     lane = lax.broadcasted_iota(jnp.int32, (lanes, dim), 0)
     col = lax.broadcasted_iota(jnp.int32, (lanes, dim), 1)
     block = lax.broadcasted_iota(jnp.int32, (count, dim), 1) // rows
+    side = (lax.broadcasted_iota(jnp.int32, (count, dim), 1) // shard) & 1
     place = lax.broadcasted_iota(jnp.int32, (count, dim), 0)
     owner = sum(((place >> k) & 1) * bit for k, bit in enumerate(bits)) ^ b
     values = rows_s[...].astype(BF16)
     for g in range(2):
-        start = (((col // shard) & 1) ^ h) * (4 * shard) + g * 2 * shard + lax.rem(col, shard)
+        start = g * 2 * shard + lax.rem(col, shard)
         pick = jnp.where((lane == start) | (lane == start + shard), 1.0, 0.0).astype(BF16)
-        spread = dot(values, pick)
+        spread = jnp.where(side == h, dot(values[0], pick), dot(values[1], pick))
         gains_ref[g : g + 1, :] = jnp.sum(jnp.where(owner == block, spread, 0.0), 0, keepdims=True)
+
+
+def pack_kernel(in_ref, proj_ref, out_ref, bulk_ref):
+    rows, dim = in_ref.shape[0], bulk_ref.shape[1]
+    blocks = in_ref.shape[1] // dim
+    half, width = proj_ref.shape[0] // 2, proj_ref.shape[1]
+    for k in range(blocks):
+        bulk_ref[k * rows : (k + 1) * rows, :] = in_ref[:, k * dim : (k + 1) * dim]
+    at = blocks * rows
+    for k in range(2):
+        bulk_ref[at : at + half, k * width : (k + 1) * width] = proj_ref[k * half : (k + 1) * half, :]
+    bulk_ref[at + half :, :] = out_ref[...]
+
+
+def pack_call(w_in, out_weight, w_out):
+    args = [w_in, out_weight, w_out]
+    dim = w_out.shape[1]
+    out = jax.ShapeDtypeStruct((sum(x.size for x in args) // dim, dim), BF16)
+    return pl.pallas_call(
+        pack_kernel,
+        grid=(1,),
+        in_specs=[whole(x.shape) for x in args],
+        out_specs=whole(out.shape),
+        out_shape=out,
+        name="pack",
+    )(*args)
 
 
 def attend_forward_kernel(
     info_ref, cnt_ref, atoms_ref, w_ref, gains_ref, pair_ref, *rest, hb, scale, carried, mol, bits, shard
 ):
-    rest = rest[carried:]
+    rest0, rest = rest, rest[carried + bool(bits) :]
     new_ref, exp_ref, mixed_ref, hid_t_ref, qkv_t_ref, inv_ref = rest[:6]
     if bits:
-        near_ref, far_ref, (w_ref, gains_ref) = w_ref, gains_ref, rest[6:8]
+        near_ref, far_ref, other_ref, pair_ref = w_ref, gains_ref, pair_ref, rest0[0]
+        w_ref, gains_ref = rest[6:8]
         rest = (*rest[:6], *rest[8:-1], rest[-1])
         rows_s = rest[-1]
         rest = rest[:-1]
     q_s, kz_s, va_s, valid_s, sum_s = rest[6:]
-    step = pl.program_id(0)
+    mol_at, step = pl.program_id(0), pl.program_id(1)
     length = atoms_ref.shape[0]
     heads = qkv_t_ref.shape[1]
     lanes = 8 * hb
-    count = cnt_ref[mol(info_ref)]
-
-    @pl.when(step == 0)
+    count = cnt_ref[mol(info_ref) + mol_at]
+
+    @pl.when((step == 0) & (mol_at == 0))
     def _():
         kz_s[...] = jnp.zeros_like(kz_s)
         if bits:
-            unpack_shards(info_ref, near_ref, far_ref, w_ref, gains_ref, rows_s, bits, shard)
+            unpack_shards(info_ref, near_ref, far_ref, other_ref, w_ref, gains_ref, rows_s, bits, shard)
 
     @pl.when(step == 0)
     def _():
@@ -364,29 +393,31 @@
 
 
 def pair_spec_of(mol, hb, length):
-    return pl.BlockSpec((1, hb, length, length), lambda j, info, cnt: (mol(info), j, 0, 0))
+    return pl.BlockSpec((1, hb, length, length), lambda i, j, info, cnt: (mol(info) + i, j, 0, 0))
 
 
 def rows_spec(length, cols, at=0):
-    return pl.BlockSpec((length, cols), lambda *_: (at, 0))
-
-
-def attend_forward_call(info, mol, counts, atoms, at, weights, pair, carried, theirs, bits=(), shard=0, hb=16):
+    return pl.BlockSpec((length, cols), lambda i, *_: (at + i, 0))
+
+
+def attend_forward_call(info, mol, n, counts, atoms, at, weights, pair, carried, bits=(), shard=0, hb=16):
     _, heads, length, _ = pair.shape
     dim = atoms.shape[1]
     width = 8 * heads
     lanes = 8 * hb
     pair_spec = pair_spec_of(mol, hb, length)
-    place, blocks = theirs
     args = [atoms, *weights, pair, *carried]
     shape = jax.ShapeDtypeStruct
     outs = [
         (shape(pair.shape, BF16), pair_spec),
         (shape(pair.shape, BF16), pair_spec),
-        (shape((blocks * length, width), BF16), rows_spec(length, width, place)),
-        (shape((dim, length), BF16), whole((dim, length))),
-        (shape((3, heads, 8, length), BF16), whole((3, heads, 8, length))),
-        (shape((length, width), F32), whole((length, width))),
+        (shape((n * length, width), BF16), rows_spec(length, width)),
+        (shape((dim, n * length), BF16), pl.BlockSpec((dim, length), lambda i, *_: (0, i))),
+        (
+            shape((3 * n, heads, 8, length), BF16),
+            pl.BlockSpec((3, heads, 8, length), lambda i, *_: (i, 0, 0, 0)),
+        ),
+        (shape((n * length, width), F32), rows_spec(length, width)),
     ]
     scratch = [
         pltpu.VMEM((heads // hb, length, 2 * lanes), BF16),
@@ -400,10 +431,10 @@
             (shape((3, dim, width), BF16), whole((3, dim, width))),
             (shape((2, dim), F32), whole((2, dim))),
         ]
-        scratch.append(pltpu.VMEM((2 ** len(bits), width), F32))
+        scratch.append(pltpu.VMEM((2, 2 ** len(bits), width), F32))
     spec = pltpu.PrefetchScalarGridSpec(
         num_scalar_prefetch=2,
-        grid=(heads // hb,),
+        grid=(n, heads // hb),
         in_specs=[rows_spec(length, dim, at), *[whole(x.shape) for x in weights], pair_spec]
         + [ANY] * len(carried),
         out_specs=[x[1] for x in outs],
@@ -421,14 +452,14 @@
         ),
         grid_spec=spec,
         out_shape=[x[0] for x in outs],
-        input_output_aliases={6 + k: k for k in range(len(carried))},
+        input_output_aliases={4 + len(weights) + k: k for k in range(len(carried))},
         compiler_params=pltpu.CompilerParams(
-            dimension_semantics=("arbitrary",), vmem_limit_bytes=VMEM_LIMIT
+            dimension_semantics=("arbitrary", "arbitrary"), vmem_limit_bytes=VMEM_LIMIT
         ),
         cost_estimate=pl.CostEstimate(
-            flops=heads * 4 * length**3,
-            transcendentals=heads * length**2,
-            bytes_accessed=6 * heads * length**2,
+            flops=n * heads * 4 * length**3,
+            transcendentals=n * heads * length**2,
+            bytes_accessed=6 * n * heads * length**2,
         ),
         name="attend_forward",
     )(info, counts, *args)
@@ -439,11 +470,12 @@
     hb, scale, carried, mol
 ):
     pg_ref, gh_ref, gp_ref, l_s, r_s, gt_s, valid_s, gq_s, gk_s, gv_s = rest[carried:]
-    step, steps = pl.program_id(0), pl.num_programs(0)
+    mol_at = pl.program_id(0)
+    step, steps = pl.program_id(1), pl.num_programs(1)
     length, width = gm_ref.shape
     heads = qkv_t_ref.shape[1]
     lanes = 8 * hb
-    count = cnt_ref[mol(info_ref)]
+    count = cnt_ref[mol(info_ref) + mol_at]
 
     @pl.when(step == 0)
     def _():
@@ -485,23 +517,27 @@
         ).astype(BF16)
 
 
-def attend_backward_call(info, mol, counts, gm, at, mixed, place, saved, weights, exps, cot, carried, theirs, hb=16):
+def attend_backward_call(info, mol, n, counts, gm, at, saved, weights, exps, cot, carried, hb=16):
     _, heads, length, _ = exps.shape
     dim, width = weights.shape[1], weights.shape[2]
     lanes = 8 * hb
     masks = jnp.asarray(np.tile(np.repeat(np.eye(hb, dtype=np.float32), 8, 1), 2), BF16)
     pair_spec = pair_spec_of(mol, hb, length)
-    qkv_t, inverse = saved
+    mixed, _, qkv_t, inverse = saved
     args = [gm, mixed, inverse, qkv_t, weights, masks, exps, cot, *carried]
-    block, blocks = theirs
     spec = pltpu.PrefetchScalarGridSpec(
         num_scalar_prefetch=2,
-        grid=(heads // hb,),
+        grid=(n, heads // hb),
         in_specs=[
-            rows_spec(length, width, at), rows_spec(length, width, place), whole(inverse.shape),
-            whole(qkv_t.shape), whole(weights.shape), whole(masks.shape), pair_spec, pair_spec,
+            rows_spec(length, width, at), rows_spec(length, width), rows_spec(length, width),
+            pl.BlockSpec((3, heads, 8, length), lambda i, *_: (i, 0, 0, 0)),
+            whole(weights.shape), whole(masks.shape), pair_spec, pair_spec,
         ] + [ANY] * len(carried),
-        out_specs=[pair_spec, rows_spec(length, dim, block), whole((3, length, width))],
+        out_specs=[
+            pair_spec,
+            rows_spec(length, dim),
+            pl.BlockSpec((3, length, width), lambda i, *_: (0, i, 0)),
+        ],
         scratch_shapes=[
             pltpu.VMEM((heads // hb, length, 2 * lanes), BF16),
             pltpu.VMEM((heads // hb, 2 * lanes, length), BF16),
@@ -518,17 +554,17 @@
         grid_spec=spec,
         out_shape=[
             shape(exps.shape, BF16),
-            shape((blocks * length, dim), BF16),
-            shape((3, length, width), BF16),
+            shape((n * length, dim), BF16),
+            shape((3, n * length, width), BF16),
         ],
         input_output_aliases={10 + k: k for k in range(len(carried))},
         compiler_params=pltpu.CompilerParams(
-            dimension_semantics=("arbitrary",), vmem_limit_bytes=VMEM_LIMIT
+            dimension_semantics=("arbitrary", "arbitrary"), vmem_limit_bytes=VMEM_LIMIT
         ),
         cost_estimate=pl.CostEstimate(
-            flops=heads * 6 * length**3,
+            flops=n * heads * 6 * length**3,
             transcendentals=0,
-            bytes_accessed=6 * heads * length**2,
+            bytes_accessed=6 * n * heads * length**2,
         ),
         name="attend_backward",
     )(info, counts, *args)
@@ -777,48 +813,45 @@
         return [high, (gain - high.astype(F32)).astype(BF16)]
 
     gain_row = jnp.concatenate(split_gain(ln1_gain) + split_gain(ln2_gain))[None]
-    gain_row = jnp.concatenate([gain_row, over_head(gain_row)], 1)
-    tail = jnp.pad(gain_row, ((0, 15), (0, width - gain_row.shape[1])))
+    tail = jnp.pad(gain_row, ((0, 7), (0, width - gain_row.shape[1])))
     gathered = jnp.concatenate([qkv_weight.reshape(-1, width), tail], 0)[None]
-    gathered, w_in_late, w_out_late, out_late = tie((gathered, w_in, w_out, out_weight))
-    for bit in far_bits:
+    gathered, late = tie((gathered, (w_in, out_weight, w_out)))
+    bulk = pack_call(*late)[None]
+    cut = bulk.shape[1] - w_out.shape[0]
+    for k, bit in enumerate(batch_bits[:-1]):
         gathered = join(gathered, over_batch(gathered, bit))
-    e_rows = out_weight.shape[0]
-    blocks = w_in.shape[1] // dim
-    in_rows = [w_in_late[:, k * dim : (k + 1) * dim] for k in range(blocks)]
-    out_rows = jnp.concatenate([out_late[: e_rows // 2], out_late[e_rows // 2 :]], 1)
-    bulk = jnp.concatenate([*in_rows, out_rows, w_out_late], 0)[None]
-    cut = bulk.shape[1] - w_out.shape[0]
-    gathered, bulk = tie((gathered, bulk))
-    atoms_other = over_head(atoms)
-    gathered = join(gathered, over_batch(gathered, 2))
+        if k == 0:
+            gathered, bulk = tie((gathered, bulk))
+        elif k == nz - 1:
+            gathered, atoms_late = tie((gathered, atoms))
     far = over_batch(gathered, 1)
+    atoms_other = over_head(atoms_late)
+    gain_at = 3 * qkv_weight.shape[1]
+    gains_other = over_head(jnp.concatenate([gathered[:, gain_at:], far[:, gain_at:]], 0))
 
     per = own // length
     mine = lambda k: lambda info: info[1] * per + k
-    theirs = lambda k: lambda info: (1 - info[1]) * per + k
-    plan = [(mine(0), atoms, 0, (0, 1))]
-    plan += [(theirs(k), atoms_other, k, (k, per)) for k in range(per)]
-    plan += [(mine(k), atoms, k, (0, 1)) for k in range(1, per)]
+    theirs = lambda info: (1 - info[1]) * per
+    plan = [(mine(0), 1, atoms, 0), (theirs, per, atoms_other, 0), (mine(1), per - 1, atoms, 1)]
     stage_bits = [(bit, bit) for bit in bits_a[:nz]] + list(zip(bits_a[nz:], bits_b[nz:]))
     last = len(stage_bits) - 1
-    parts = (bulk,)
+    for bit in bits_a[:nz]:
+        bulk = join(bulk, over_both(bulk, bit))
+    parts = (bulk[:, :cut], bulk[:, cut:])
 
     def send_stage(parts, k):
         return tuple(over_both(x, bit) for x, bit in zip(parts, stage_bits[k]))
 
-    received = send_stage(parts, 0)
-    received, far = tie((received, far))
+    received = ()
     cnt = counts
     carried = ()
     saved = []
-    for k, (mol, rows, at, place) in enumerate(plan):
-        if k < last - 1:
-            parts = tuple(map(join, parts, received))
-            if k + 1 == nz:
-                parts = (parts[0][:, :cut], parts[0][:, cut:])
+    for k, (mol, n, rows, at) in enumerate(plan):
+        stage = nz + k
+        if stage < last:
+            parts = tuple(map(join, parts, received)) if received else parts
             cnt, parts = tie((cnt, parts))
-            received = send_stage(parts, k + 1)
+            received = send_stage(parts, stage)
         else:
             cnt, received = tie((cnt, received))
             a_parts, b_parts = (
@@ -827,75 +860,76 @@
             )
         if k == 0:
             results = attend_forward_call(
-                info, mol, cnt, rows, at, (gathered, far), pair, carried, place, batch_bits, shard
+                info, mol, n, cnt, rows, at, (gathered, far, gains_other), pair, carried, batch_bits, shard
             )
             weights, gains = results[6:]
         else:
             results = attend_forward_call(
-                info, mol, cnt, rows, at, (weights, gains), pair, carried, place
+                info, mol, n, cnt, rows, at, (weights, gains), pair, carried
             )
         new_pair, exps, mixed, hid_t, qkv_t, inverse = results[:6]
-        if k < last - 1:
+        if stage < last:
             received, inverse = tie((received, inverse))
-        carried = (new_pair, exps, mixed) if place[0] + 1 < place[1] else (new_pair, exps)
-        saved.append((mixed, hid_t, (qkv_t, inverse)))
-    mixed_theirs = saved[per][0]
-    mixed_mine = [saved[0][0], *[s[0] for s in saved[1 + per :]]]
-    mixed_other = over_head(mixed_theirs)
+        carried = (new_pair, exps)
+        saved.append((mixed, hid_t, qkv_t, inverse))
+    mixed_other = over_head(saved[1][0])
 
     output, first, gm_mine, gm_other, *pieces = layer_call(
-        info, atoms, mixed_mine, mixed_other, out_cot, gains, a_parts, b_parts, bits_a, bits_b
+        info, atoms, (saved[0][0], saved[2][0]), mixed_other, out_cot, gains, a_parts, b_parts, bits_a, bits_b
     )
     gm_received = over_head(gm_other)
 
-    def scatter_core(piece, bit):
-        low, high, far_low, far_high = piece
-        return add(low, over_both(far_low, bit)), add(high, over_both(far_high, bit))
-
-    parts = [scatter_core(p, bit) for p, bit in zip((pieces[:4], pieces[4:]), stage_bits[last])]
+    parts = [p[:2] for p in (pieces[:4], pieces[4:])]
+    received = [[over_both(x, bit) for x in p[2:]] for p, bit in zip((pieces[:4], pieces[4:]), stage_bits[last])]
     send_halves = lambda parts, k: [over_both(high, bit) for (_, high), bit in zip(parts, stage_bits[k])]
     add_halves = lambda parts, received: [add(low, r) for (low, _), r in zip(parts, received)]
     carried = ()
     grads = []
     cnt = counts
-    stage = last - 1
-    for k, (mol, _, at, place) in enumerate(plan):
+    gms = (gm_mine, gm_received, gm_mine)
+    for k, (mol, n, _, at) in enumerate(plan):
+        if k > 0:
+            if k > 1:
+                parts = [halves(x) for x in add_halves(parts, received)]
+            else:
+                parts = [[add(x, r) for x, r in zip(*pair)] for pair in zip(parts, received)]
+            cnt, parts = tie((cnt, parts))
+            received = send_halves(parts, last - k)
+        pair_grad, gh, gp = attend_backward_call(
+            info, mol, n, cnt, gms[k], at, saved[k], weights, exps, pair_cot, carried
+        )
+        received, gp = tie((received, gp))
         if k == 1:
-            cnt, parts = tie((cnt, parts))
-            received = send_halves(parts, stage)
-        elif k == len(plan) - 1:
-            cnt, sums = tie((cnt, add_halves(parts, received)))
-            parts = [halves(x) for x in sums]
-            stage -= 1
-            received = send_halves(parts, stage)
-        mixed = mixed_theirs if place[1] > 1 else saved[k][0]
-        gm = gm_received if place[1] > 1 else gm_mine
-        pair_grad, gh, gp = attend_backward_call(
-            info, mol, cnt, gm, at, mixed, place[0], saved[k][2], weights, exps, pair_cot, carried, place
-        )
-        carried = (pair_grad, gh) if place[0] + 1 < place[1] else (pair_grad,)
+            hidden_received = over_head(gh)
+        elif k == 2:
+            hidden_received, gp = tie((hidden_received, gp))
+        carried = (pair_grad,)
         grads.append((gh, gp))
-    hidden_received = over_head(grads[per][0])
-    gps, received = tie(([g[1] for g in grads], received))
+    bulk = jnp.concatenate(add_halves(parts, received), 1)
+    gps, bulk = tie(([g[1] for g in grads], bulk))
     near, far = project_grad_call(info, [s[1] for s in saved], gps, batch_bits)
     near = add(near, over_batch(far, batch_bits[-1]))
-    near, received = tie((near, received))
-    bulk = jnp.concatenate(add_halves(parts, received), 1)
-    for bit in batch_bits[-2::-1]:
+    bulk_keep, bulk_send = halves(bulk)
+    bulk_received = over_both(bulk_send, bits_a[nz - 1])
+    for k, bit in enumerate(batch_bits[-2::-1]):
         keep, send = halves(near)
-        near = add(keep, over_batch(send, bit))
-        if stage > 0:
-            stage -= 1
-            keep, send = halves(bulk)
-            bulk = add(keep, over_both(send, bits_a[stage]))
+        received = over_batch(send, bit)
+        near = add(keep, received)
+        if k == 0:
+            _, bulk_received = tie((received, bulk_received))
+    bulk = add(bulk_keep, bulk_received)
+    for bit in bits_a[: nz - 1][::-1]:
+        keep, send = halves(bulk)
+        bulk = add(keep, over_both(send, bit))
     qkv_grad = near[0].reshape(qkv_weight.shape).astype(F32)
     gain_part = jnp.sum(qkv_grad * qkv_weight.astype(F32), (0, 2)).reshape(2, shard)
     gain_mine = lax.dynamic_index_in_dim(gain_part, h, 0, False)
     gain_other = over_head(lax.dynamic_index_in_dim(gain_part, 1 - h, 0, False))
     gain_one_grad = (gain_mine + gain_other) / ln1_gain
-    atoms_grad = last_call(atoms, gains, first, grads[0][0], grads[-1][0], hidden_received)
+    atoms_grad = last_call(atoms, gains, first, grads[0][0], grads[2][0], hidden_received)
     bulk = bulk[0].astype(F32)
     shard_rows = w_in.shape[0]
+    blocks = w_in.shape[1] // dim
     in_grad = jnp.concatenate([bulk[k * shard_rows : (k + 1) * shard_rows] for k in range(blocks)], 1)
     out_grad = jnp.concatenate([bulk[blocks * shard_rows : cut, k * width : (k + 1) * width] for k in range(2)], 0)
     outer_grad = bulk[cut:]

time: 183 us -> 173 us (0.945)
  Pallas kernels: 86 us -> 80.9 us
  other arithmetic: 12.4 us -> 7.49 us
  local copies, waits for them, and re-layouts: 9.01 us -> 5.26 us
  waiting for transfers between devices: 38.6 us -> 41.5 us
    pallas_call x4 -> x3, Pallas kernels: 34.3 us -> 30.9 us  [attend_backward_call(): pl.pallas_call(partial(attend_backward_kernel, hb=hb, scale=8 ** (-0.5),...]
    convert_element_type x13, other arithmetic: 5.64 us -> 2.32 us  [add(): return (kept.astype(F32) + received.astype(F32)).astype(BF16)]
    unnamed x38 -> x41, local copies, waits for them, and re-layouts: 5.82 us -> 2.88 us
    ppermute x34, waiting for transfers between devices: 38.6 us -> 41.5 us  [swap(): return lax.ppermute(values, axes, [(i, i ^ bit) for i in range(count)])]
    pallas_call x4 -> x3, Pallas kernels: 32.2 us -> 29.6 us  [attend_forward_call(): pl.pallas_call(partial(attend_forward_kernel, hb=hb, scale=8 ** (-0.5), c...]
  transfers between devices with their start and end apart: 34 -> 34, of which waited for: 15 -> 12; matrix products, arithmetic and copies ran while one was open for 7% -> 3% of each run, Pallas kernels for 37% -> 37%
where the time goes in v4:
time: 173 us
  Pallas kernels  80.9 us (47%)
  waiting for transfers between devices  41.5 us (24%)
  starting transfers between devices  36.4 us (21%)
  other arithmetic  7.49 us (4%)
  local copies, waits for them, and re-layouts  5.26 us (3%)
    ppermute x34, waiting for transfers between devices, swap(): return lax.ppermute(values, axes, [(i, i ^ bit) for i in range(count)])  41.5 us
    ppermute x34, starting transfers between devices, swap(): return lax.ppermute(values, axes, [(i, i ^ bit) for i in range(count)])  36.4 us
    pallas_call x3, Pallas kernels, attend_backward_call(): pl.pallas_call(partial(attend_backward_kernel, hb=hb, scale=8 ** (-0.5),...  30.9 us
    pallas_call x3, Pallas kernels, attend_forward_call(): pl.pallas_call(partial(attend_forward_kernel, hb=hb, scale=8 ** (-0.5), c...  29.6 us
    pallas_call x1, Pallas kernels, layer_call(): pl.pallas_call(partial(layer_kernel, bits_a=bits_a, bits_b=bits_b), grid_...  15.8 us
  transfers between devices with their start and end apart: 34, of which 12 were waited for; matrix products, arithmetic and copies ran while one was open for 3% of the time, Pallas kernels for 37%

profile of v4, /device:TPU:0, one launch (start us, length us, event | category | flops | bytes accessed | tf_op | source)
XLA Modules:
  0.0 172.7 jit_solution(16650321353458749872)
XLA Ops:
  0.6 0.7 fusion.9
  1.5 0.8 fusion.3
  2.3 4.0 %collective-permute-start = (bf16[1,104,256]{2,1,0:T(8,128)(2,1)S(1)}, bf16[1,104,256]{2,1,0:T(8,128)(2,1)S(1)}, u32[]{:S(2)}, u32[]{:S(2)}) collective-permute-start(bf16[1,104,256]{2,1,0:T(8,128)(2,1)S(1)} %fusion.3), channel_id=1, source_target_pairs={{0,16},{2,18},{4,20},{6,22},{8,24},{10,26},{12,28},{14,30},{16,0},... | collective-permute-start | bytes 159752 | tf_op jit(solution)/shard_map/ppermute | solution.py:257
  6.3 1.6 pack.1
  7.9 1.1 collective-permute-done
  9.0 1.4 collective-permute-start.3
  10.4 3.4 %collective-permute-done.3 = bf16[2,104,256]{2,1,0:T(8,128)(2,1)S(1)} collective-permute-done((bf16[2,104,256]{2,1,0:T(8,128)(2,1)S(1)}, bf16[2,104,256]{2,1,0:T(8,128)(2,1)S(1)}, u32[]{:S(2)}, u32[]{:S(2)}) %collective-permute-start.3) | collective-permute-done | bytes 106528 | tf_op jit(solution)/shard_map/ppermute | solution.py:257
  13.8 1.8 %collective-permute-start.4 = (bf16[4,104,256]{2,1,0:T(8,128)(2,1)S(1)}, bf16[4,104,256]{2,1,0:T(8,128)(2,1)S(1)}, u32[]{:S(2)}, u32[]{:S(2)}) collective-permute-start(bf16[4,104,256]{2,1,0:T(8,128)(2,1)S(1)} %pad_maximum_fusion.4), channel_id=1, source_target_pairs={{0,4},{2,6},{4,0},{6,2},{8,12},{10,14},{12,8},{14,10},{16,20},{18,... | collective-permute-start | bytes 638984 | tf_op jit(solution)/shard_map/ppermute | solution.py:257
  15.6 2.2 %collective-permute-start.1 = (bf16[1,144,512]{2,1,0:T(8,128)(2,1)}, bf16[1,144,512]{2,1,0:T(8,128)(2,1)S(1)}, u32[]{:S(2)}, u32[]{:S(2)}) collective-permute-start(bf16[1,144,512]{2,1,0:T(8,128)(2,1)} %bitcast.28), channel_id=1, source_target_pairs={{0,16},{1,17},{2,18},{3,19},{4,20},{5,21},{6,22},{7,23},{8,24},{9,... | collective-permute-start | bytes 442376 | tf_op jit(solution)/shard_map/ppermute | solution.py:257
  17.8 1.9 %collective-permute-done.4 = bf16[4,104,256]{2,1,0:T(8,128)(2,1)S(1)} collective-permute-done((bf16[4,104,256]{2,1,0:T(8,128)(2,1)S(1)}, bf16[4,104,256]{2,1,0:T(8,128)(2,1)S(1)}, u32[]{:S(2)}, u32[]{:S(2)}) %collective-permute-start.4) | collective-permute-done | bytes 213024 | tf_op jit(solution)/shard_map/ppermute | solution.py:257
  19.8 3.7 %collective-permute-done.1 = bf16[1,144,512]{2,1,0:T(8,128)(2,1)S(1)} collective-permute-done((bf16[1,144,512]{2,1,0:T(8,128)(2,1)}, bf16[1,144,512]{2,1,0:T(8,128)(2,1)S(1)}, u32[]{:S(2)}, u32[]{:S(2)}) %collective-permute-start.1) | collective-permute-done | bytes 147488 | tf_op jit(solution)/shard_map/ppermute | solution.py:257
  24.0 6.3 %collective-permute-done.2 = bf16[2,144,512]{2,1,0:T(8,128)(2,1)S(1)} collective-permute-done((bf16[2,144,512]{2,1,0:T(8,128)(2,1)S(1)}, bf16[2,144,512]{2,1,0:T(8,128)(2,1)S(1)}, u32[]{:S(2)}, u32[]{:S(2)}) %collective-permute-start.2) | collective-permute-done | bytes 294944 | tf_op jit(solution)/shard_map/ppermute | solution.py:257
  30.4 0.8 collective-permute-start.7
  31.2 1.5 collective-permute-start.8
  33.4 1.5 collective-permute-start.11
  34.9 7.0 %collective-permute-done.6.pair_ref = bf16[16,8,256]{2,1,0:T(8,128)(2,1)S(1)} collective-permute-done((bf16[16,8,256]{2,1,0:T(8,128)(2,1)S(1)}, bf16[16,8,256]{2,1,0:T(8,128)(2,1)S(1)}, u32[]{:S(2)}, u32[]{:S(2)}) %collective-permute-start.6) | collective-permute-done | bytes 65568 | tf_op jit(solution)/shard_map/ppermute | solution.py:257
  41.9 8.2 %attend_forward.3 = (bf16[4,32,256,256]{3,2,1,0:T(8,128)(2,1)}, bf16[4,32,256,256]{3,2,1,0:T(8,128)(2,1)}, bf16[256,256]{1,0:T(8,128)(2,1)S(1)}, bf16[512,256]{1...) custom-call(s32[2]{0:T(128)S(1)} %pad_add_fusion.info_ref.me_ref, ...), custom_call_target="tpu_custom_call" | custom-call | flops 2147483648 | bytes 12582912 | tf_op jit(solution)/shard_map/attend_forward/pallas_call | solution.py:443
  50.2 1.6 collective-permute-start.9
  51.8 1.2 collective-permute-start.10
  53.1 13.4 %attend_forward.4 = (bf16[4,32,256,256]{3,2,1,0:T(8,128)(2,1)}, bf16[4,32,256,256]{3,2,1,0:T(8,128)(2,1)}, bf16[512,256]{1,0:T(8,128)(2,1)S(1)}, bf16[512,512]{1...) custom-call(s32[2]{0:T(128)S(1)} %pad_add_fusion.info_ref.me_ref, ...), custom_call_target="tpu_custom_call", output_to_operand_aliasing={{0}: (6, {}), {1}: (7, {})} | custom-call | flops 4294967296 | bytes 25165824 | tf_op jit(solution)/shard_map/attend_forward/pallas_call | solution.py:443
  68.2 8.0 %attend_forward.5 = (bf16[4,32,256,256]{3,2,1,0:T(8,128)(2,1)}, bf16[4,32,256,256]{3,2,1,0:T(8,128)(2,1)}, bf16[256,256]{1,0:T(8,128)(2,1)S(1)}, bf16[512,256]{1...) custom-call(s32[2]{0:T(128)S(1)} %pad_add_fusion.info_ref.me_ref, ...), custom_call_target="tpu_custom_call", output_to_operand_aliasing={{0}: (6, {}), {1}: (7, {})} | custom-call | flops 2147483648 | bytes 12582912 | tf_op jit(solution)/shard_map/attend_forward/pallas_call | solution.py:443
  76.3 0.8 copy-done.16
  77.5 15.8 %layer.1 = (bf16[512,512]{1,0:T(8,128)(2,1)}, f32[512,512]{1,0:T(8,128)}, bf16[512,256]{1,0:T(8,128)(2,1)S(1)}, bf16[512,256]{1,0:T(8,128)(2,1)S(1)}, bf16[8,80,...) custom-call(s32[2]{0:T(128)S(1)} %pad_add_fusion.info_ref.me_ref, ...), custom_call_target="tpu_custom_call" | custom-call | flops 6442450944 | bytes 8388608 | tf_op jit(solution)/shard_map/layer/pallas_call | solution.py:696
  94.3 1.4 collective-permute-start.23
  95.6 8.5 %attend_backward.3 = (bf16[4,32,256,256]{3,2,1,0:T(8,128)(2,1)}, bf16[256,512]{1,0:T(8,128)(2,1)S(1)}, bf16[3,256,256]{2,1,0:T(8,128)(2,1)S(1)}) custom-call(s32[2]{0:T(128)S(1)} %pad_add_fusion.info_ref.me_ref, s32[4]{0:T(128)S(1)} %copy-done.3, bf16[512,256]{1,0:T(8,128)(2,1)S(1)} %get-tuple-element.139.gm_ref, ...), custom_call_target="tpu_custom_call" | custom-call | flops 3221225472 | bytes 12582912 | tf_op jit(solution)/shard_map/attend_backward/pallas_call | solution.py:552
  104.3 0.9 copy-done.9
  106.4 0.8 collective-permute-start.22
  107.1 13.9 %attend_backward.4 = (bf16[4,32,256,256]{3,2,1,0:T(8,128)(2,1)}, bf16[512,512]{1,0:T(8,128)(2,1)S(1)}, bf16[3,512,256]{2,1,0:T(8,128)(2,1)S(1)}) custom-call(s32[2]{0:T(128)S(1)} %pad_add_fusion.info_ref.me_ref, s32[4]{0:T(128)S(1)} %copy-done.3, bf16[512,256]{1,0:T(8,128)(2,1)S(1)} %collective-permute-done.23.gm_ref, ...), custom_call_target="tpu_custom_call", output_to_operand_aliasing={{0}: (10, {})} | custom-call | flops 6442450944 | bytes 25165824 | tf_op jit(solution)/shard_map/attend_backward/pallas_call | solution.py:552
  121.1 1.4 collective-permute-start.24
  122.9 1.3 collective-permute-start.25
  124.9 8.5 %attend_backward.5 = (bf16[4,32,256,256]{3,2,1,0:T(8,128)(2,1)}, bf16[256,512]{1,0:T(8,128)(2,1)S(1)}, bf16[3,256,256]{2,1,0:T(8,128)(2,1)S(1)}) custom-call(s32[2]{0:T(128)S(1)} %pad_add_fusion.info_ref.me_ref, s32[4]{0:T(128)S(1)} %copy-done.3, bf16[512,256]{1,0:T(8,128)(2,1)S(1)} %get-tuple-element.139.gm_ref, ...), custom_call_target="tpu_custom_call", output_to_operand_aliasing={{0}: (10, {})} | custom-call | flops 3221225472 | bytes 12582912 | tf_op jit(solution)/shard_map/attend_backward/pallas_call | solution.py:552
  133.4 6.3 %collective-permute-done.26 = bf16[4,64,512]{2,1,0:T(8,128)(2,1)S(1)} collective-permute-done((bf16[4,64,512]{2,1,0:T(8,128)(2,1)S(1)}, bf16[4,64,512]{2,1,0:T(8,128)(2,1)S(1)}, u32[]{:S(2)}, u32[]{:S(2)}) %collective-permute-start.26) | collective-permute-done | bytes 262176 | tf_op jit(solution)/shard_map/ppermute | solution.py:257
  139.9 1.6 project_grad.1
  141.6 1.7 collective-permute-done.27
  144.8 1.3 collective-permute-start.28
  146.9 1.8 %collective-permute-start.31 = (bf16[2,144,512]{2,1,0:T(8,128)(2,1)}, bf16[2,144,512]{2,1,0:T(8,128)(2,1)S(1)}, u32[]{:S(2)}, u32[]{:S(2)}) collective-permute-start(bf16[2,144,512]{2,1,0:T(8,128)(2,1)} %slice.105), channel_id=1, source_target_pairs={{0,8},{1,9},{2,10},{3,11},{4,12},{5,13},{6,14},{7,15},{8,0},{9,1},... | collective-permute-start | bytes 884744 | tf_op jit(solution)/shard_map/ppermute | solution.py:257
  148.7 1.5 last_norm.1
  150.2 1.9 %collective-permute-done.28 = bf16[4,96,256]{2,1,0:T(8,128)(2,1)} collective-permute-done((bf16[4,96,256]{2,1,0:T(8,128)(2,1)}, bf16[4,96,256]{2,1,0:T(8,128)(2,1)}, u32[]{:S(2)}, u32[]{:S(2)}) %collective-permute-start.28) | collective-permute-done | bytes 196640 | tf_op jit(solution)/shard_map/ppermute | solution.py:257
  152.1 1.0 add_convert_fusion.10
  153.1 1.7 collective-permute-start.29
  154.8 2.0 %collective-permute-done.31 = bf16[2,144,512]{2,1,0:T(8,128)(2,1)S(1)} collective-permute-done((bf16[2,144,512]{2,1,0:T(8,128)(2,1)}, bf16[2,144,512]{2,1,0:T(8,128)(2,1)S(1)}, u32[]{:S(2)}, u32[]{:S(2)}) %collective-permute-start.31) | collective-permute-done | bytes 294944 | tf_op jit(solution)/shard_map/ppermute | solution.py:257
  156.9 3.3 %collective-permute-start.32 = (bf16[1,144,512]{2,1,0:T(8,128)(2,1)S(1)}, bf16[1,144,512]{2,1,0:T(8,128)(2,1)S(1)}, u32[]{:S(2)}, u32[]{:S(2)}) collective-permute-start(bf16[1,144,512]{2,1,0:T(8,128)(2,1)S(1)} %slice.135), channel_id=1, source_target_pairs={{0,16},{1,17},{2,18},{3,19},{4,20},{5,21},{6,22},{7,23},{8,24},{9,... | collective-permute-start | bytes 442376 | tf_op jit(solution)/shard_map/ppermute | solution.py:257
  160.2 1.4 collective-permute-start.30
  161.6 5.4 %collective-permute-done.32 = bf16[1,144,512]{2,1,0:T(8,128)(2,1)S(1)} collective-permute-done((bf16[1,144,512]{2,1,0:T(8,128)(2,1)S(1)}, bf16[1,144,512]{2,1,0:T(8,128)(2,1)S(1)}, u32[]{:S(2)}, u32[]{:S(2)}) %collective-permute-start.32) | collective-permute-done | bytes 147488 | tf_op jit(solution)/shard_map/ppermute | solution.py:257
  167.7 0.8 multiply_reduce_fusion.1
  168.6 0.8 collective-permute-start.33
  170.0 0.8 multiply_reduce_fusion
  171.3 0.8 collective-permute-done.33
  (119 shorter events, 12.3 us)
Async XLA Ops:
  2.3 6.7 %collective-permute-start = (bf16[1,104,256]{2,1,0:T(8,128)(2,1)S(1)}, bf16[1,104,256]{2,1,0:T(8,128)(2,1)S(1)}, u32[]{:S(2)}, u32[]{:S(2)}) collective-permute-start(bf16[1,104,256]{2,1,0:T(8,128)(2,1)S(1)} %fusion.3), channel_id=1, source_target_pairs={{0,16},{2,18},{4,20},{6,22},{8,24},{10,26},{12,28},{14,30},{16,0},... | collective-permute-start | bytes 159752 | tf_op jit(solution)/shard_map/ppermute | solution.py:257
  7.9 15.6 %copy-start.7 = (bf16[144,512]{1,0:T(8,128)(2,1)S(1)}, bf16[144,512]{1,0:T(8,128)(2,1)}, u32[]{:S(2)}) copy-start(bf16[144,512]{1,0:T(8,128)(2,1)} %pack.1) | copy-start | bytes 442372
  9.0 4.8 %collective-permute-start.3 = (bf16[2,104,256]{2,1,0:T(8,128)(2,1)S(1)}, bf16[2,104,256]{2,1,0:T(8,128)(2,1)S(1)}, u32[]{:S(2)}, u32[]{:S(2)}) collective-permute-start(bf16[2,104,256]{2,1,0:T(8,128)(2,1)S(1)} %pad_maximum_fusion.6), channel_id=1, source_target_pairs={{0,8},{2,10},{4,12},{6,14},{8,0},{10,2},{12,4},{14,6},{16,24},{18,... | collective-permute-start | bytes 319496 | tf_op jit(solution)/shard_map/ppermute | solution.py:257
  13.8 5.9 %collective-permute-start.4 = (bf16[4,104,256]{2,1,0:T(8,128)(2,1)S(1)}, bf16[4,104,256]{2,1,0:T(8,128)(2,1)S(1)}, u32[]{:S(2)}, u32[]{:S(2)}) collective-permute-start(bf16[4,104,256]{2,1,0:T(8,128)(2,1)S(1)} %pad_maximum_fusion.4), channel_id=1, source_target_pairs={{0,4},{2,6},{4,0},{6,2},{8,12},{10,14},{12,8},{14,10},{16,20},{18,... | collective-permute-start | bytes 638984 | tf_op jit(solution)/shard_map/ppermute | solution.py:257
  15.6 7.9 %collective-permute-start.1 = (bf16[1,144,512]{2,1,0:T(8,128)(2,1)}, bf16[1,144,512]{2,1,0:T(8,128)(2,1)S(1)}, u32[]{:S(2)}, u32[]{:S(2)}) collective-permute-start(bf16[1,144,512]{2,1,0:T(8,128)(2,1)} %bitcast.28), channel_id=1, source_target_pairs={{0,16},{1,17},{2,18},{3,19},{4,20},{5,21},{6,22},{7,23},{8,24},{9,... | collective-permute-start | bytes 442376 | tf_op jit(solution)/shard_map/ppermute | solution.py:257
  19.7 13.0 %collective-permute-start.5 = (bf16[8,104,256]{2,1,0:T(8,128)(2,1)S(1)}, bf16[8,104,256]{2,1,0:T(8,128)(2,1)S(1)}, u32[]{:S(2)}, u32[]{:S(2)}) collective-permute-start(bf16[8,104,256]{2,1,0:T(8,128)(2,1)S(1)} %constant_dynamic-update-slice_fusion.3.w_ref), channel_id=1, source_target_pairs={{0,2},{2,0},{4,6},{6,4},{8,10},{10,8},{12,14},{14,12},{16,18},{18,... | collective-permute-start | bytes 1277960 | tf_op jit(solution)/shard_map/ppermute | solution.py:257
  23.5 6.8 %collective-permute-start.2 = (bf16[2,144,512]{2,1,0:T(8,128)(2,1)S(1)}, bf16[2,144,512]{2,1,0:T(8,128)(2,1)S(1)}, u32[]{:S(2)}, u32[]{:S(2)}) collective-permute-start(bf16[2,144,512]{2,1,0:T(8,128)(2,1)S(1)} %pad_maximum_fusion.3), channel_id=1, source_target_pairs={{0,8},{1,9},{2,10},{3,11},{4,12},{5,13},{6,14},{7,15},{8,0},{9,1},... | collective-permute-start | bytes 884744 | tf_op jit(solution)/shard_map/ppermute | solution.py:257
  23.9 9.5 %copy-start = (bf16[512,512]{1,0:T(8,128)(2,1)S(1)}, bf16[512,512]{1,0:T(8,128)(2,1)}, u32[]{:S(2)}) copy-start(bf16[512,512]{1,0:T(8,128)(2,1)} %atoms_ref.7) | copy-start | bytes 1572868
  23.9 17.9 %copy-start.3 = (s32[4]{0:T(128)S(1)}, s32[4]{0:T(128)}, u32[]{:S(2)}) copy-start(s32[4]{0:T(128)} %cnt_ref.6) | copy-start | bytes 52
  30.4 19.7 %collective-permute-start.7 = (bf16[4,80,512]{2,1,0:T(8,128)(2,1)S(1)}, bf16[4,80,512]{2,1,0:T(8,128)(2,1)S(1)}, u32[]{:S(2)}, u32[]{:S(2)}) collective-permute-start(bf16[4,80,512]{2,1,0:T(8,128)(2,1)S(1)} %slice.120), channel_id=1, source_target_pairs={{0,4},{1,5},{2,6},{3,7},{4,0},{5,1},{6,2},{7,3},{8,12},{9,13},{10,... | collective-permute-start | bytes 983048 | tf_op jit(solution)/shard_map/ppermute | solution.py:257
  31.2 18.9 %collective-permute-start.8 = (bf16[4,64,512]{2,1,0:T(8,128)(2,1)S(1)}, bf16[4,64,512]{2,1,0:T(8,128)(2,1)S(1)}, u32[]{:S(2)}, u32[]{:S(2)}) collective-permute-start(bf16[4,64,512]{2,1,0:T(8,128)(2,1)S(1)} %slice.121), channel_id=1, source_target_pairs={{0,1},{1,0},{2,3},{3,2},{4,5},{5,4},{6,7},{7,6},{8,9},{9,8},{10,11... | collective-permute-start | bytes 786440 | tf_op jit(solution)/shard_map/ppermute | solution.py:257
  32.7 9.1 %collective-permute-start.6 = (bf16[16,8,256]{2,1,0:T(8,128)(2,1)S(1)}, bf16[16,8,256]{2,1,0:T(8,128)(2,1)S(1)}, u32[]{:S(2)}, u32[]{:S(2)}) collective-permute-start(bf16[16,8,256]{2,1,0:T(8,128)(2,1)S(1)} %pad_maximum_fusion.7), channel_id=1, source_target_pairs={{0,1},{1,0},{2,3},{3,2},{4,5},{5,4},{6,7},{7,6},{8,9},{9,8},{10,11... | collective-permute-start | bytes 196616 | tf_op jit(solution)/shard_map/ppermute | solution.py:257
  33.4 19.7 %collective-permute-start.11 = (bf16[512,512]{1,0:T(8,128)(2,1)S(1)}, bf16[512,512]{1,0:T(8,128)(2,1)S(1)}, u32[]{:S(2)}, u32[]{:S(2)}) collective-permute-start(bf16[512,512]{1,0:T(8,128)(2,1)S(1)} %copy-done), channel_id=1, source_target_pairs={{0,1},{1,0},{2,3},{3,2},{4,5},{5,4},{6,7},{7,6},{8,9},{9,8},{10,11... | collective-permute-start | bytes 1572872 | tf_op jit(solution)/shard_map/ppermute | solution.py:257
  50.2 16.2 %copy-start.8 = (bf16[8,80,512]{2,1,0:T(8,128)(2,1)}, bf16[8,80,512]{2,1,0:T(8,128)(2,1)S(1)}, u32[]{:S(2)}) copy-start(bf16[8,80,512]{2,1,0:T(8,128)(2,1)S(1)} %pad_maximum_fusion.rest_0_) | copy-start | bytes 1966084
  50.2 16.2 %collective-permute-start.9 = (bf16[8,80,512]{2,1,0:T(8,128)(2,1)S(1)}, bf16[8,80,512]{2,1,0:T(8,128)(2,1)S(1)}, u32[]{:S(2)}, u32[]{:S(2)}) collective-permute-start(bf16[8,80,512]{2,1,0:T(8,128)(2,1)S(1)} %pad_maximum_fusion.rest_0_), channel_id=1, source_target_pairs={{0,1},{1,0},{2,3},{3,2},{4,5},{5,4},{6,7},{7,6},{8,9},{9,8},{10,11... | collective-permute-start | bytes 1966088 | tf_op jit(solution)/shard_map/ppermute | solution.py:257
  51.8 14.6 %collective-permute-start.10 = (bf16[8,64,512]{2,1,0:T(8,128)(2,1)S(1)}, bf16[8,64,512]{2,1,0:T(8,128)(2,1)S(1)}, u32[]{:S(2)}, u32[]{:S(2)}) collective-permute-start(bf16[8,64,512]{2,1,0:T(8,128)(2,1)S(1)} %pad_maximum_fusion.2.rest_4_), channel_id=1, source_target_pairs={{0,4},{1,5},{2,6},{3,7},{4,0},{5,1},{6,2},{7,3},{8,12},{9,13},{10,... | collective-permute-start | bytes 1572872 | tf_op jit(solution)/shard_map/ppermute | solution.py:257
  53.1 23.1 %collective-permute-start.13 = (bf16[8,80,512]{2,1,0:T(8,128)(2,1)S(1)}, bf16[8,80,512]{2,1,0:T(8,128)(2,1)S(1)}, u32[]{:S(2)}, u32[]{:S(2)}) collective-permute-start(bf16[8,80,512]{2,1,0:T(8,128)(2,1)S(1)} %pad_maximum_fusion.rest_0_), channel_id=1, source_target_pairs={{0,2},{1,3},{2,0},{3,1},{4,6},{5,7},{6,4},{7,5},{8,10},{9,11},{10,... | collective-permute-start | bytes 1966088 | tf_op jit(solution)/shard_map/ppermute | solution.py:257
  66.5 9.7 %copy-start.15 = (bf16[8,80,512]{2,1,0:T(8,128)(2,1)}, bf16[8,80,512]{2,1,0:T(8,128)(2,1)S(1)}, u32[]{:S(2)}) copy-start(bf16[8,80,512]{2,1,0:T(8,128)(2,1)S(1)} %collective-permute-done.9.rest_1_) | copy-start | bytes 1966084
  66.5 9.8 %collective-permute-start.14 = (bf16[8,80,512]{2,1,0:T(8,128)(2,1)S(1)}, bf16[8,80,512]{2,1,0:T(8,128)(2,1)S(1)}, u32[]{:S(2)}, u32[]{:S(2)}) collective-permute-start(bf16[8,80,512]{2,1,0:T(8,128)(2,1)S(1)} %collective-permute-done.9.rest_1_), channel_id=1, source_target_pairs={{0,2},{1,3},{2,0},{3,1},{4,6},{5,7},{6,4},{7,5},{8,10},{9,11},{10,... | collective-permute-start | bytes 1966088 | tf_op jit(solution)/shard_map/ppermute | solution.py:257
  67.0 9.1 %collective-permute-start.15 = (bf16[8,64,512]{2,1,0:T(8,128)(2,1)S(1)}, bf16[8,64,512]{2,1,0:T(8,128)(2,1)S(1)}, u32[]{:S(2)}, u32[]{:S(2)}) collective-permute-start(bf16[8,64,512]{2,1,0:T(8,128)(2,1)S(1)} %pad_maximum_fusion.2.rest_4_), channel_id=1, source_target_pairs={{0,2},{1,3},{2,0},{3,1},{4,6},{5,7},{6,4},{7,5},{8,10},{9,11},{10,... | collective-permute-start | bytes 1572872 | tf_op jit(solution)/shard_map/ppermute | solution.py:257
  67.1 9.1 %collective-permute-start.16 = (bf16[8,64,512]{2,1,0:T(8,128)(2,1)S(1)}, bf16[8,64,512]{2,1,0:T(8,128)(2,1)S(1)}, u32[]{:S(2)}, u32[]{:S(2)}) collective-permute-start(bf16[8,64,512]{2,1,0:T(8,128)(2,1)S(1)} %collective-permute-done.10.rest_5_), channel_id=1, source_target_pairs={{0,2},{1,3},{2,0},{3,1},{4,6},{5,7},{6,4},{7,5},{8,10},{9,11},{10,... | collective-permute-start | bytes 1572872 | tf_op jit(solution)/shard_map/ppermute | solution.py:257
  67.6 8.6 %collective-permute-start.12 = (bf16[512,256]{1,0:T(8,128)(2,1)S(1)}, bf16[512,256]{1,0:T(8,128)(2,1)S(1)}, u32[]{:S(2)}, u32[]{:S(2)}) collective-permute-start(bf16[512,256]{1,0:T(8,128)(2,1)S(1)} %get-tuple-element.133.mixed_ref), channel_id=1, source_target_pairs={{0,1},{1,0},{2,3},{3,2},{4,5},{5,4},{6,7},{7,6},{8,9},{9,8},{10,11... | collective-permute-start | bytes 786440 | tf_op jit(solution)/shard_map/ppermute | solution.py:257
  68.2 9.3 %copy-start.4 = (bf16[512,512]{1,0:T(8,128)(2,1)S(1)}, bf16[512,512]{1,0:T(8,128)(2,1)}, u32[]{:S(2)}) copy-start(bf16[512,512]{1,0:T(8,128)(2,1)} %cot_ref.4) | copy-start | bytes 1572868
  77.4 18.2 %copy-start.2 = (bf16[16,256]{1,0:T(8,128)(2,1)S(1)}, bf16[16,256]{1,0:T(8,128)(2,1)}, u32[]{:S(2)}) copy-start(bf16[16,256]{1,0:T(8,128)(2,1)} %constant.27.clone.mask_ref) | copy-start | bytes 24580
  93.2 10.9 %collective-permute-start.17 = (bf16[8,80,512]{2,1,0:T(8,128)(2,1)}, bf16[8,80,512]{2,1,0:T(8,128)(2,1)S(1)}, u32[]{:S(2)}, u32[]{:S(2)}) collective-permute-start(bf16[8,80,512]{2,1,0:T(8,128)(2,1)} %get-tuple-element.145), channel_id=1, source_target_pairs={{0,2},{1,3},{2,0},{3,1},{4,6},{5,7},{6,4},{7,5},{8,10},{9,11},{10,... | collective-permute-start | bytes 1966088 | tf_op jit(solution)/shard_map/ppermute | solution.py:257
  93.3 10.8 %collective-permute-start.18 = (bf16[8,80,512]{2,1,0:T(8,128)(2,1)}, bf16[8,80,512]{2,1,0:T(8,128)(2,1)S(1)}, u32[]{:S(2)}, u32[]{:S(2)}) collective-permute-start(bf16[8,80,512]{2,1,0:T(8,128)(2,1)} %get-tuple-element.146), channel_id=1, source_target_pairs={{0,2},{1,3},{2,0},{3,1},{4,6},{5,7},{6,4},{7,5},{8,10},{9,11},{10,... | collective-permute-start | bytes 1966088 | tf_op jit(solution)/shard_map/ppermute | solution.py:257
  93.7 10.3 %collective-permute-start.19 = (bf16[8,64,512]{2,1,0:T(8,128)(2,1)S(1)}, bf16[8,64,512]{2,1,0:T(8,128)(2,1)S(1)}, u32[]{:S(2)}, u32[]{:S(2)}) collective-permute-start(bf16[8,64,512]{2,1,0:T(8,128)(2,1)S(1)} %get-tuple-element.147), channel_id=1, source_target_pairs={{0,2},{1,3},{2,0},{3,1},{4,6},{5,7},{6,4},{7,5},{8,10},{9,11},{10,... | collective-permute-start | bytes 1572872 | tf_op jit(solution)/shard_map/ppermute | solution.py:257
  93.8 10.3 %collective-permute-start.20 = (bf16[8,64,512]{2,1,0:T(8,128)(2,1)S(1)}, bf16[8,64,512]{2,1,0:T(8,128)(2,1)S(1)}, u32[]{:S(2)}, u32[]{:S(2)}) collective-permute-start(bf16[8,64,512]{2,1,0:T(8,128)(2,1)S(1)} %get-tuple-element.148), channel_id=1, source_target_pairs={{0,2},{1,3},{2,0},{3,1},{4,6},{5,7},{6,4},{7,5},{8,10},{9,11},{10,... | collective-permute-start | bytes 1572872 | tf_op jit(solution)/shard_map/ppermute | solution.py:257
  94.3 12.9 %collective-permute-start.23 = (bf16[512,256]{1,0:T(8,128)(2,1)S(1)}, bf16[512,256]{1,0:T(8,128)(2,1)S(1)}, u32[]{:S(2)}, u32[]{:S(2)}) collective-permute-start(bf16[512,256]{1,0:T(8,128)(2,1)S(1)} %get-tuple-element.161), channel_id=1, source_target_pairs={{0,1},{1,0},{2,3},{3,2},{4,5},{5,4},{6,7},{7,6},{8,9},{9,8},{10,11... | collective-permute-start | bytes 786440 | tf_op jit(solution)/shard_map/ppermute | solution.py:257
  95.6 8.5 %copy-start.10 = (bf16[8,80,512]{2,1,0:T(8,128)(2,1)S(1)}, bf16[8,80,512]{2,1,0:T(8,128)(2,1)}, u32[]{:S(2)}) copy-start(bf16[8,80,512]{2,1,0:T(8,128)(2,1)} %get-tuple-element.144) | copy-start | bytes 1966084
  105.7 16.8 %collective-permute-start.21 = (bf16[8,80,512]{2,1,0:T(8,128)(2,1)S(1)}, bf16[8,80,512]{2,1,0:T(8,128)(2,1)S(1)}, u32[]{:S(2)}, u32[]{:S(2)}) collective-permute-start(bf16[8,80,512]{2,1,0:T(8,128)(2,1)S(1)} %add_convert_fusion.1), channel_id=1, source_target_pairs={{0,1},{1,0},{2,3},{3,2},{4,5},{5,4},{6,7},{7,6},{8,9},{9,8},{10,11... | collective-permute-start | bytes 1966088 | tf_op jit(solution)/shard_map/ppermute | solution.py:257
  106.4 16.1 %collective-permute-start.22 = (bf16[8,64,512]{2,1,0:T(8,128)(2,1)S(1)}, bf16[8,64,512]{2,1,0:T(8,128)(2,1)S(1)}, u32[]{:S(2)}, u32[]{:S(2)}) collective-permute-start(bf16[8,64,512]{2,1,0:T(8,128)(2,1)S(1)} %add_convert_fusion.4), channel_id=1, source_target_pairs={{0,4},{1,5},{2,6},{3,7},{4,0},{5,1},{6,2},{7,3},{8,12},{9,13},{10,... | collective-permute-start | bytes 1572872 | tf_op jit(solution)/shard_map/ppermute | solution.py:257
  121.1 18.6 %collective-permute-start.24 = (bf16[512,512]{1,0:T(8,128)(2,1)S(1)}, bf16[512,512]{1,0:T(8,128)(2,1)S(1)}, u32[]{:S(2)}, u32[]{:S(2)}) collective-permute-start(bf16[512,512]{1,0:T(8,128)(2,1)S(1)} %get-tuple-element.174), channel_id=1, source_target_pairs={{0,1},{1,0},{2,3},{3,2},{4,5},{5,4},{6,7},{7,6},{8,9},{9,8},{10,11... | collective-permute-start | bytes 1572872 | tf_op jit(solution)/shard_map/ppermute | solution.py:257
  122.9 16.8 %collective-permute-start.25 = (bf16[4,80,512]{2,1,0:T(8,128)(2,1)S(1)}, bf16[4,80,512]{2,1,0:T(8,128)(2,1)S(1)}, u32[]{:S(2)}, u32[]{:S(2)}) collective-permute-start(bf16[4,80,512]{2,1,0:T(8,128)(2,1)S(1)} %get-tuple-element.175), channel_id=1, source_target_pairs={{0,4},{1,5},{2,6},{3,7},{4,0},{5,1},{6,2},{7,3},{8,12},{9,13},{10,... | collective-permute-start | bytes 983048 | tf_op jit(solution)/shard_map/ppermute | solution.py:257
  124.2 15.5 %collective-permute-start.26 = (bf16[4,64,512]{2,1,0:T(8,128)(2,1)S(1)}, bf16[4,64,512]{2,1,0:T(8,128)(2,1)S(1)}, u32[]{:S(2)}, u32[]{:S(2)}) collective-permute-start(bf16[4,64,512]{2,1,0:T(8,128)(2,1)S(1)} %get-tuple-element.176), channel_id=1, source_target_pairs={{0,1},{1,0},{2,3},{3,2},{4,5},{5,4},{6,7},{7,6},{8,9},{9,8},{10,11... | collective-permute-start | bytes 786440 | tf_op jit(solution)/shard_map/ppermute | solution.py:257
  141.5 7.2 %copy-start.1 = (f32[512,512]{1,0:T(8,128)S(1)}, f32[512,512]{1,0:T(8,128)}, u32[]{:S(2)}) copy-start(f32[512,512]{1,0:T(8,128)} %get-tuple-element.138.first_ref) | copy-start | bytes 3145732
  141.5 1.8 %collective-permute-start.27 = (bf16[8,96,256]{2,1,0:T(8,128)(2,1)S(1)}, bf16[8,96,256]{2,1,0:T(8,128)(2,1)S(1)}, u32[]{:S(2)}, u32[]{:S(2)}) collective-permute-start(bf16[8,96,256]{2,1,0:T(8,128)(2,1)S(1)} %get-tuple-element.195), channel_id=1, source_target_pairs={{0,2},{2,0},{4,6},{6,4},{8,10},{10,8},{12,14},{14,12},{16,18},{18,... | collective-permute-start | bytes 1179656 | tf_op jit(solution)/shard_map/ppermute | solution.py:257
  144.8 7.3 %collective-permute-start.28 = (bf16[4,96,256]{2,1,0:T(8,128)(2,1)}, bf16[4,96,256]{2,1,0:T(8,128)(2,1)}, u32[]{:S(2)}, u32[]{:S(2)}) collective-permute-start(bf16[4,96,256]{2,1,0:T(8,128)(2,1)} %slice.129), channel_id=1, source_target_pairs={{0,4},{2,6},{4,0},{6,2},{8,12},{10,14},{12,8},{14,10},{16,20},{18,... | collective-permute-start | bytes 589832 | tf_op jit(solution)/shard_map/ppermute | solution.py:257
  146.9 9.8 %collective-permute-start.31 = (bf16[2,144,512]{2,1,0:T(8,128)(2,1)}, bf16[2,144,512]{2,1,0:T(8,128)(2,1)S(1)}, u32[]{:S(2)}, u32[]{:S(2)}) collective-permute-start(bf16[2,144,512]{2,1,0:T(8,128)(2,1)} %slice.105), channel_id=1, source_target_pairs={{0,8},{1,9},{2,10},{3,11},{4,12},{5,13},{6,14},{7,15},{8,0},{9,1},... | collective-permute-start | bytes 884744 | tf_op jit(solution)/shard_map/ppermute | solution.py:257
  148.7 3.4 %copy-start.6 = (bf16[8,96,256]{2,1,0:T(8,128)(2,1)S(1)}, bf16[8,96,256]{2,1,0:T(8,128)(2,1)}, u32[]{:S(2)}) copy-start(bf16[8,96,256]{2,1,0:T(8,128)(2,1)} %copy-done.5) | copy-start | bytes 1179652
  153.1 7.0 %collective-permute-start.29 = (bf16[2,96,256]{2,1,0:T(8,128)(2,1)S(1)}, bf16[2,96,256]{2,1,0:T(8,128)(2,1)S(1)}, u32[]{:S(2)}, u32[]{:S(2)}) collective-permute-start(bf16[2,96,256]{2,1,0:T(8,128)(2,1)S(1)} %slice.131), channel_id=1, source_target_pairs={{0,8},{2,10},{4,12},{6,14},{8,0},{10,2},{12,4},{14,6},{16,24},{18,... | collective-permute-start | bytes 294920 | tf_op jit(solution)/shard_map/ppermute | solution.py:257
  156.8 10.9 %copy-start.12 = (bf16[3,32,256]{2,1,0:T(8,128)(2,1)S(1)}, bf16[3,32,256]{2,1,0:T(8,128)(2,1)}, u32[]{:S(2)}) copy-start(bf16[3,32,256]{2,1,0:T(8,128)(2,1)} %param.17) | copy-start | bytes 147460
  156.8 13.2 %copy-start.11 = (bf16[16,2048]{1,0:T(8,128)(2,1)S(1)}, bf16[16,2048]{1,0:T(8,128)(2,1)}, u32[]{:S(2)}) copy-start(bf16[16,2048]{1,0:T(8,128)(2,1)} %in_ref) | copy-start | bytes 196612
  156.9 14.0 %copy-start.14 = (f32[16]{0:T(128)S(1)}, f32[16]{0:T(128)}, u32[]{:S(2)}) copy-start(f32[16]{0:T(128)} %param.20) | copy-start | bytes 196
  156.9 15.3 %copy-start.13 = (f32[16]{0:T(128)S(1)}, f32[16]{0:T(128)}, u32[]{:S(2)}) copy-start(f32[16]{0:T(128)} %param.19) | copy-start | bytes 196
  156.9 10.1 %collective-permute-start.32 = (bf16[1,144,512]{2,1,0:T(8,128)(2,1)S(1)}, bf16[1,144,512]{2,1,0:T(8,128)(2,1)S(1)}, u32[]{:S(2)}, u32[]{:S(2)}) collective-permute-start(bf16[1,144,512]{2,1,0:T(8,128)(2,1)S(1)} %slice.135), channel_id=1, source_target_pairs={{0,16},{1,17},{2,18},{3,19},{4,20},{5,21},{6,22},{7,23},{8,24},{9,... | collective-permute-start | bytes 442376 | tf_op jit(solution)/shard_map/ppermute | solution.py:257
  160.2 7.5 %collective-permute-start.30 = (bf16[1,96,256]{2,1,0:T(8,128)(2,1)S(1)}, bf16[1,96,256]{2,1,0:T(8,128)(2,1)S(1)}, u32[]{:S(2)}, u32[]{:S(2)}) collective-permute-start(bf16[1,96,256]{2,1,0:T(8,128)(2,1)S(1)} %slice.133), channel_id=1, source_target_pairs={{0,16},{2,18},{4,20},{6,22},{8,24},{10,26},{12,28},{14,30},{16,0},... | collective-permute-start | bytes 147464 | tf_op jit(solution)/shard_map/ppermute | solution.py:257
  168.6 3.5 %collective-permute-start.33 = (f32[16]{0:T(128)S(1)}, f32[16]{0:T(128)S(1)}, u32[]{:S(2)}, u32[]{:S(2)}) collective-permute-start(f32[16]{0:T(128)S(1)} %dynamic-slice_bitcast_fusion), channel_id=1, source_target_pairs={{0,1},{1,0},{2,3},{3,2},{4,5},{5,4},{6,7},{7,6},{8,9},{9,8},{10,11... | collective-permute-start | bytes 200 | tf_op jit(solution)/shard_map/ppermute | solution.py:257
  (5 other events, 4.9 us)

commit v5 on v4

--- a/solution.py
+++ b/solution.py
@@ -738,6 +738,7 @@
         ),
         out_shape=outs,
         compiler_params=pltpu.CompilerParams(vmem_limit_bytes=32 << 20),
+        cost_estimate=pl.CostEstimate(flops=1000, transcendentals=0, bytes_accessed=1000),
         name="project_grad",
     )(me, *args)
 
@@ -770,6 +771,7 @@
         out_specs=whole(atoms.shape),
         out_shape=jax.ShapeDtypeStruct(atoms.shape, BF16),
         compiler_params=pltpu.CompilerParams(vmem_limit_bytes=32 << 20),
+        cost_estimate=pl.CostEstimate(flops=1000, transcendentals=0, bytes_accessed=1000),
         name="last_norm",
     )(*args)
 
@@ -815,15 +817,13 @@
     gain_row = jnp.concatenate(split_gain(ln1_gain) + split_gain(ln2_gain))[None]
     tail = jnp.pad(gain_row, ((0, 7), (0, width - gain_row.shape[1])))
     gathered = jnp.concatenate([qkv_weight.reshape(-1, width), tail], 0)[None]
-    gathered, late = tie((gathered, (w_in, out_weight, w_out)))
+    gathered, late, atoms_late = tie((gathered, (w_in, out_weight, w_out), atoms))
     bulk = pack_call(*late)[None]
     cut = bulk.shape[1] - w_out.shape[0]
     for k, bit in enumerate(batch_bits[:-1]):
         gathered = join(gathered, over_batch(gathered, bit))
         if k == 0:
             gathered, bulk = tie((gathered, bulk))
-        elif k == nz - 1:
-            gathered, atoms_late = tie((gathered, atoms))
     far = over_batch(gathered, 1)
     atoms_other = over_head(atoms_late)
     gain_at = 3 * qkv_weight.shape[1]
@@ -832,16 +832,17 @@
     per = own // length
     mine = lambda k: lambda info: info[1] * per + k
     theirs = lambda info: (1 - info[1]) * per
-    plan = [(mine(0), 1, atoms, 0), (theirs, per, atoms_other, 0), (mine(1), per - 1, atoms, 1)]
     stage_bits = [(bit, bit) for bit in bits_a[:nz]] + list(zip(bits_a[nz:], bits_b[nz:]))
     last = len(stage_bits) - 1
     for bit in bits_a[:nz]:
         bulk = join(bulk, over_both(bulk, bit))
+    bulk, gains_other, atoms_other = tie((bulk, gains_other, atoms_other))
     parts = (bulk[:, :cut], bulk[:, cut:])
 
     def send_stage(parts, k):
         return tuple(over_both(x, bit) for x, bit in zip(parts, stage_bits[k]))
 
+    plan = [(mine(0), 1, atoms, 0), (theirs, per, atoms_other, 0), (mine(1), per - 1, atoms, 1)]
     received = ()
     cnt = counts
     carried = ()
@@ -899,17 +900,13 @@
             info, mol, n, cnt, gms[k], at, saved[k], weights, exps, pair_cot, carried
         )
         received, gp = tie((received, gp))
-        if k == 1:
-            hidden_received = over_head(gh)
-        elif k == 2:
-            hidden_received, gp = tie((hidden_received, gp))
         carried = (pair_grad,)
         grads.append((gh, gp))
-    bulk = jnp.concatenate(add_halves(parts, received), 1)
-    gps, bulk = tie(([g[1] for g in grads], bulk))
+    bulk_keep, bulk_send = halves(jnp.concatenate(add_halves(parts, received), 1))
+    gps, bulk_keep, bulk_send, gh = tie(([g[1] for g in grads], bulk_keep, bulk_send, grads[1][0]))
+    hidden_received = over_head(gh)
     near, far = project_grad_call(info, [s[1] for s in saved], gps, batch_bits)
     near = add(near, over_batch(far, batch_bits[-1]))
-    bulk_keep, bulk_send = halves(bulk)
     bulk_received = over_both(bulk_send, bits_a[nz - 1])
     for k, bit in enumerate(batch_bits[-2::-1]):
         keep, send = halves(near)
@@ -917,6 +914,8 @@
         near = add(keep, received)
         if k == 0:
             _, bulk_received = tie((received, bulk_received))
+        elif k == 1:
+            _, hidden_received = tie((received, hidden_received))
     bulk = add(bulk_keep, bulk_received)
     for bit in bits_a[: nz - 1][::-1]:
         keep, send = halves(bulk)

time: 173 us -> 166 us (0.960)
  waiting for transfers between devices: 41.5 us -> 28.3 us
  other arithmetic: 7.49 us -> 13 us
    ppermute x34, waiting for transfers between devices: 41.5 us -> 28.3 us  [swap(): return lax.ppermute(values, axes, [(i, i ^ bit) for i in range(count)])]
    concatenate x5 -> x6, other arithmetic: 0.17 us -> 2.05 us  [join(): return jnp.concatenate([values, received], 0)]
  transfers between devices with their start and end apart: 34 -> 34, of which waited for: 12 -> 13; matrix products, arithmetic and copies ran while one was open for 3% -> 5% of each run, Pallas kernels for 37% -> 39%
where the time goes in v5:
time: 166 us
  Pallas kernels  81.8 us (49%)
  starting transfers between devices  36.9 us (22%)
  waiting for transfers between devices  28.3 us (17%)
  other arithmetic  13 us (8%)
  local copies, waits for them, and re-layouts  4.57 us (3%)
    ppermute x34, starting transfers between devices, swap(): return lax.ppermute(values, axes, [(i, i ^ bit) for i in range(count)])  36.9 us
    pallas_call x3, Pallas kernels, attend_backward_call(): pl.pallas_call(partial(attend_backward_kernel, hb=hb, scale=8 ** (-0.5),...  31.2 us
    pallas_call x3, Pallas kernels, attend_forward_call(): pl.pallas_call(partial(attend_forward_kernel, hb=hb, scale=8 ** (-0.5), c...  29.7 us
    ppermute x34, waiting for transfers between devices, swap(): return lax.ppermute(values, axes, [(i, i ^ bit) for i in range(count)])  28.3 us
    pallas_call x1, Pallas kernels, layer_call(): pl.pallas_call(partial(layer_kernel, bits_a=bits_a, bits_b=bits_b), grid_...  16.1 us
    convert_element_type x13, other arithmetic, add(): return (kept.astype(F32) + received.astype(F32)).astype(BF16)  3.44 us
  transfers between devices with their start and end apart: 34, of which 13 were waited for; matrix products, arithmetic and copies ran while one was open for 5% of the time, Pallas kernels for 39%

profile of v5, /device:TPU:0, one launch (start us, length us, event | category | flops | bytes accessed | tf_op | source)
XLA Modules:
  0.0 165.6 jit_solution(14076651782751740480)
XLA Ops:
  2.3 4.0 %collective-permute-start = (bf16[1,104,256]{2,1,0:T(8,128)(2,1)S(1)}, bf16[1,104,256]{2,1,0:T(8,128)(2,1)S(1)}, u32[]{:S(2)}, u32[]{:S(2)}) collective-permute-start(bf16[1,104,256]{2,1,0:T(8,128)(2,1)S(1)} %fusion.4), channel_id=1, source_target_pairs={{0,16},{2,18},{4,20},{6,22},{8,24},{10,26},{12,28},{14,30},{16,0},... | collective-permute-start | bytes 159752 | tf_op jit(solution)/shard_map/ppermute | solution.py:257
  6.3 1.6 pack.1
  7.9 1.1 collective-permute-done
  9.0 1.4 collective-permute-start.3
  10.4 3.1 %collective-permute-start.1 = (bf16[1,144,512]{2,1,0:T(8,128)(2,1)}, bf16[1,144,512]{2,1,0:T(8,128)(2,1)S(1)}, u32[]{:S(2)}, u32[]{:S(2)}) collective-permute-start(bf16[1,144,512]{2,1,0:T(8,128)(2,1)} %bitcast.28), channel_id=1, source_target_pairs={{0,16},{1,17},{2,18},{3,19},{4,20},{5,21},{6,22},{7,23},{8,24},{9,... | collective-permute-start | bytes 442376 | tf_op jit(solution)/shard_map/ppermute | solution.py:257
  13.5 1.1 collective-permute-done.3
  14.5 1.8 %collective-permute-start.4 = (bf16[4,104,256]{2,1,0:T(8,128)(2,1)S(1)}, bf16[4,104,256]{2,1,0:T(8,128)(2,1)S(1)}, u32[]{:S(2)}, u32[]{:S(2)}) collective-permute-start(bf16[4,104,256]{2,1,0:T(8,128)(2,1)S(1)} %pad_maximum_fusion.5), channel_id=1, source_target_pairs={{0,4},{2,6},{4,0},{6,2},{8,12},{10,14},{12,8},{14,10},{16,20},{18,... | collective-permute-start | bytes 638984 | tf_op jit(solution)/shard_map/ppermute | solution.py:257
  16.4 4.0 %collective-permute-done.4 = bf16[4,104,256]{2,1,0:T(8,128)(2,1)S(1)} collective-permute-done((bf16[4,104,256]{2,1,0:T(8,128)(2,1)S(1)}, bf16[4,104,256]{2,1,0:T(8,128)(2,1)S(1)}, u32[]{:S(2)}, u32[]{:S(2)}) %collective-permute-start.4) | collective-permute-done | bytes 213024 | tf_op jit(solution)/shard_map/ppermute | solution.py:257
  20.6 1.8 %collective-permute-start.7 = (bf16[512,512]{1,0:T(8,128)(2,1)}, bf16[512,512]{1,0:T(8,128)(2,1)S(1)}, u32[]{:S(2)}, u32[]{:S(2)}) collective-permute-start(bf16[512,512]{1,0:T(8,128)(2,1)} %atoms_ref.7), channel_id=1, source_target_pairs={{0,1},{1,0},{2,3},{3,2},{4,5},{5,4},{6,7},{7,6},{8,9},{9,8},{10,11... | collective-permute-start | bytes 1572872 | tf_op jit(solution)/shard_map/ppermute | solution.py:257
  22.4 0.9 pad_maximum_fusion.4
  23.3 0.9 collective-permute-start.2
  24.8 7.6 %collective-permute-done.2 = bf16[2,144,512]{2,1,0:T(8,128)(2,1)S(1)} collective-permute-done((bf16[2,144,512]{2,1,0:T(8,128)(2,1)S(1)}, bf16[2,144,512]{2,1,0:T(8,128)(2,1)S(1)}, u32[]{:S(2)}, u32[]{:S(2)}) %collective-permute-start.2) | collective-permute-done | bytes 294944 | tf_op jit(solution)/shard_map/ppermute | solution.py:257
  32.5 1.0 pad_maximum_fusion.1
  33.4 2.1 %collective-permute-done.7.atoms_ref = bf16[512,512]{1,0:T(8,128)(2,1)S(1)} collective-permute-done((bf16[512,512]{1,0:T(8,128)(2,1)}, bf16[512,512]{1,0:T(8,128)(2,1)S(1)}, u32[]{:S(2)}, u32[]{:S(2)}) %collective-permute-start.7) | collective-permute-done | bytes 524320 | tf_op jit(solution)/shard_map/ppermute | solution.py:257
  35.6 1.0 collective-permute-done.6.pair_ref
  36.6 1.8 %collective-permute-start.8 = (bf16[4,80,512]{2,1,0:T(8,128)(2,1)S(1)}, bf16[4,80,512]{2,1,0:T(8,128)(2,1)S(1)}, u32[]{:S(2)}, u32[]{:S(2)}) collective-permute-start(bf16[4,80,512]{2,1,0:T(8,128)(2,1)S(1)} %slice.92), channel_id=1, source_target_pairs={{0,4},{1,5},{2,6},{3,7},{4,0},{5,1},{6,2},{7,3},{8,12},{9,13},{10,... | collective-permute-start | bytes 983048 | tf_op jit(solution)/shard_map/ppermute | solution.py:257
  38.4 1.5 collective-permute-start.9
  40.0 1.0 copy-done
  41.7 8.3 %attend_forward.3 = (bf16[4,32,256,256]{3,2,1,0:T(8,128)(2,1)}, bf16[4,32,256,256]{3,2,1,0:T(8,128)(2,1)}, bf16[256,256]{1,0:T(8,128)(2,1)S(1)}, bf16[512,256]{1...) custom-call(s32[2]{0:T(128)S(1)} %pad_add_fusion.info_ref.me_ref, ...), custom_call_target="tpu_custom_call" | custom-call | flops 2147483648 | bytes 12582912 | tf_op jit(solution)/shard_map/attend_forward/pallas_call | solution.py:443
  51.0 13.4 %attend_forward.4 = (bf16[4,32,256,256]{3,2,1,0:T(8,128)(2,1)}, bf16[4,32,256,256]{3,2,1,0:T(8,128)(2,1)}, bf16[512,256]{1,0:T(8,128)(2,1)S(1)}, bf16[512,512]{1...) custom-call(s32[2]{0:T(128)S(1)} %pad_add_fusion.info_ref.me_ref, ...), custom_call_target="tpu_custom_call", output_to_operand_aliasing={{0}: (6, {}), {1}: (7, {})} | custom-call | flops 4294967296 | bytes 25165824 | tf_op jit(solution)/shard_map/attend_forward/pallas_call | solution.py:443
  64.4 1.5 collective-permute-done.10.rest_1_
  66.4 0.9 collective-permute-start.12
  67.3 8.0 %attend_forward.5 = (bf16[4,32,256,256]{3,2,1,0:T(8,128)(2,1)}, bf16[4,32,256,256]{3,2,1,0:T(8,128)(2,1)}, bf16[256,256]{1,0:T(8,128)(2,1)S(1)}, bf16[512,256]{1...) custom-call(s32[2]{0:T(128)S(1)} %pad_add_fusion.info_ref.me_ref, ...), custom_call_target="tpu_custom_call", output_to_operand_aliasing={{0}: (6, {}), {1}: (7, {})} | custom-call | flops 2147483648 | bytes 12582912 | tf_op jit(solution)/shard_map/attend_forward/pallas_call | solution.py:443
  76.6 16.1 %layer.1 = (bf16[512,512]{1,0:T(8,128)(2,1)}, f32[512,512]{1,0:T(8,128)}, bf16[512,256]{1,0:T(8,128)(2,1)S(1)}, bf16[512,256]{1,0:T(8,128)(2,1)S(1)}, bf16[8,80,...) custom-call(s32[2]{0:T(128)S(1)} %pad_add_fusion.info_ref.me_ref, ...), custom_call_target="tpu_custom_call" | custom-call | flops 6442450944 | bytes 8388608 | tf_op jit(solution)/shard_map/layer/pallas_call | solution.py:696
  93.7 1.1 collective-permute-start.23
  94.8 8.6 %attend_backward.3 = (bf16[4,32,256,256]{3,2,1,0:T(8,128)(2,1)}, bf16[256,512]{1,0:T(8,128)(2,1)S(1)}, bf16[3,256,256]{2,1,0:T(8,128)(2,1)S(1)}) custom-call(s32[2]{0:T(128)S(1)} %pad_add_fusion.info_ref.me_ref, s32[4]{0:T(128)S(1)} %copy-done.4, bf16[512,256]{1,0:T(8,128)(2,1)S(1)} %get-tuple-element.144.gm_ref, ...), custom_call_target="tpu_custom_call" | custom-call | flops 3221225472 | bytes 12582912 | tf_op jit(solution)/shard_map/attend_backward/pallas_call | solution.py:552
  104.1 1.0 collective-permute-start.21
  105.2 1.5 collective-permute-start.22
  106.7 14.1 %attend_backward.4 = (bf16[4,32,256,256]{3,2,1,0:T(8,128)(2,1)}, bf16[512,512]{1,0:T(8,128)(2,1)S(1)}, bf16[3,512,256]{2,1,0:T(8,128)(2,1)S(1)}) custom-call(s32[2]{0:T(128)S(1)} %pad_add_fusion.info_ref.me_ref, s32[4]{0:T(128)S(1)} %copy-done.4, bf16[512,256]{1,0:T(8,128)(2,1)S(1)} %collective-permute-done.23.gm_ref, ...), custom_call_target="tpu_custom_call", output_to_operand_aliasing={{0}: (10, {})} | custom-call | flops 6442450944 | bytes 25165824 | tf_op jit(solution)/shard_map/attend_backward/pallas_call | solution.py:552
  122.0 1.6 collective-permute-start.25
  123.6 8.6 %attend_backward.5 = (bf16[4,32,256,256]{3,2,1,0:T(8,128)(2,1)}, bf16[256,512]{1,0:T(8,128)(2,1)S(1)}, bf16[3,256,256]{2,1,0:T(8,128)(2,1)S(1)}) custom-call(s32[2]{0:T(128)S(1)} %pad_add_fusion.info_ref.me_ref, s32[4]{0:T(128)S(1)} %copy-done.4, bf16[512,256]{1,0:T(8,128)(2,1)S(1)} %get-tuple-element.144.gm_ref, ...), custom_call_target="tpu_custom_call", output_to_operand_aliasing={{0}: (10, {})} | custom-call | flops 3221225472 | bytes 12582912 | tf_op jit(solution)/shard_map/attend_backward/pallas_call | solution.py:552
  132.3 0.9 pad_maximum_fusion.3
  133.2 1.6 project_grad.1
  134.8 1.7 %collective-permute-done.26 = bf16[8,96,256]{2,1,0:T(8,128)(2,1)S(1)} collective-permute-done((bf16[8,96,256]{2,1,0:T(8,128)(2,1)S(1)}, bf16[8,96,256]{2,1,0:T(8,128)(2,1)S(1)}, u32[]{:S(2)}, u32[]{:S(2)}) %collective-permute-start.26) | collective-permute-done | bytes 393248 | tf_op jit(solution)/shard_map/ppermute | solution.py:257
  137.9 0.8 collective-permute-start.31
  138.7 1.3 collective-permute-start.29
  140.0 4.6 %collective-permute-done.27 = bf16[4,96,256]{2,1,0:T(8,128)(2,1)} collective-permute-done((bf16[4,96,256]{2,1,0:T(8,128)(2,1)}, bf16[4,96,256]{2,1,0:T(8,128)(2,1)}, u32[]{:S(2)}, u32[]{:S(2)}) %collective-permute-start.27) | collective-permute-done | bytes 196640 | tf_op jit(solution)/shard_map/ppermute | solution.py:257
  144.6 1.0 add_convert_fusion.10
  145.6 0.9 collective-permute-start.28
  146.9 1.1 add_convert_fusion.8
  148.1 2.7 %collective-permute-start.32 = (bf16[1,144,512]{2,1,0:T(8,128)(2,1)S(1)}, bf16[1,144,512]{2,1,0:T(8,128)(2,1)S(1)}, u32[]{:S(2)}, u32[]{:S(2)}) collective-permute-start(bf16[1,144,512]{2,1,0:T(8,128)(2,1)S(1)} %slice.135), channel_id=1, source_target_pairs={{0,16},{1,17},{2,18},{3,19},{4,20},{5,21},{6,22},{7,23},{8,24},{9,... | collective-permute-start | bytes 442376 | tf_op jit(solution)/shard_map/ppermute | solution.py:257
  150.8 1.3 collective-permute-done.29.recv_ref
  152.1 3.1 %collective-permute-start.30 = (bf16[1,96,256]{2,1,0:T(8,128)(2,1)S(1)}, bf16[1,96,256]{2,1,0:T(8,128)(2,1)S(1)}, u32[]{:S(2)}, u32[]{:S(2)}) collective-permute-start(bf16[1,96,256]{2,1,0:T(8,128)(2,1)S(1)} %slice.133), channel_id=1, source_target_pairs={{0,16},{2,18},{4,20},{6,22},{8,24},{10,26},{12,28},{14,30},{16,0},... | collective-permute-start | bytes 147464 | tf_op jit(solution)/shard_map/ppermute | solution.py:257
  155.2 1.6 last_norm.1
  156.8 1.7 %collective-permute-done.32 = bf16[1,144,512]{2,1,0:T(8,128)(2,1)S(1)} collective-permute-done((bf16[1,144,512]{2,1,0:T(8,128)(2,1)S(1)}, bf16[1,144,512]{2,1,0:T(8,128)(2,1)S(1)}, u32[]{:S(2)}, u32[]{:S(2)}) %collective-permute-start.32) | collective-permute-done | bytes 147488 | tf_op jit(solution)/shard_map/ppermute | solution.py:257
  159.3 1.6 multiply_reduce_fusion.1
  161.0 1.3 collective-permute-start.33
  162.9 1.6 multiply_reduce_fusion
  (109 shorter events, 13.4 us)
Async XLA Ops:
  2.3 6.7 %collective-permute-start = (bf16[1,104,256]{2,1,0:T(8,128)(2,1)S(1)}, bf16[1,104,256]{2,1,0:T(8,128)(2,1)S(1)}, u32[]{:S(2)}, u32[]{:S(2)}) collective-permute-start(bf16[1,104,256]{2,1,0:T(8,128)(2,1)S(1)} %fusion.4), channel_id=1, source_target_pairs={{0,16},{2,18},{4,20},{6,22},{8,24},{10,26},{12,28},{14,30},{16,0},... | collective-permute-start | bytes 159752 | tf_op jit(solution)/shard_map/ppermute | solution.py:257
  9.0 5.5 %collective-permute-start.3 = (bf16[2,104,256]{2,1,0:T(8,128)(2,1)S(1)}, bf16[2,104,256]{2,1,0:T(8,128)(2,1)S(1)}, u32[]{:S(2)}, u32[]{:S(2)}) collective-permute-start(bf16[2,104,256]{2,1,0:T(8,128)(2,1)S(1)} %pad_maximum_fusion.7), channel_id=1, source_target_pairs={{0,8},{2,10},{4,12},{6,14},{8,0},{10,2},{12,4},{14,6},{16,24},{18,... | collective-permute-start | bytes 319496 | tf_op jit(solution)/shard_map/ppermute | solution.py:257
  10.4 12.0 %collective-permute-start.1 = (bf16[1,144,512]{2,1,0:T(8,128)(2,1)}, bf16[1,144,512]{2,1,0:T(8,128)(2,1)S(1)}, u32[]{:S(2)}, u32[]{:S(2)}) collective-permute-start(bf16[1,144,512]{2,1,0:T(8,128)(2,1)} %bitcast.28), channel_id=1, source_target_pairs={{0,16},{1,17},{2,18},{3,19},{4,20},{5,21},{6,22},{7,23},{8,24},{9,... | collective-permute-start | bytes 442376 | tf_op jit(solution)/shard_map/ppermute | solution.py:257
  14.5 5.9 %collective-permute-start.4 = (bf16[4,104,256]{2,1,0:T(8,128)(2,1)S(1)}, bf16[4,104,256]{2,1,0:T(8,128)(2,1)S(1)}, u32[]{:S(2)}, u32[]{:S(2)}) collective-permute-start(bf16[4,104,256]{2,1,0:T(8,128)(2,1)S(1)} %pad_maximum_fusion.5), channel_id=1, source_target_pairs={{0,4},{2,6},{4,0},{6,2},{8,12},{10,14},{12,8},{14,10},{16,20},{18,... | collective-permute-start | bytes 638984 | tf_op jit(solution)/shard_map/ppermute | solution.py:257
  20.5 3.7 %collective-permute-start.5 = (bf16[8,104,256]{2,1,0:T(8,128)(2,1)S(1)}, bf16[8,104,256]{2,1,0:T(8,128)(2,1)S(1)}, u32[]{:S(2)}, u32[]{:S(2)}) collective-permute-start(bf16[8,104,256]{2,1,0:T(8,128)(2,1)S(1)} %constant_dynamic-update-slice_fusion.w_ref), channel_id=1, source_target_pairs={{0,2},{2,0},{4,6},{6,4},{8,10},{10,8},{12,14},{14,12},{16,18},{18,... | collective-permute-start | bytes 1277960 | tf_op jit(solution)/shard_map/ppermute | solution.py:257
  20.6 15.0 %collective-permute-start.7 = (bf16[512,512]{1,0:T(8,128)(2,1)}, bf16[512,512]{1,0:T(8,128)(2,1)S(1)}, u32[]{:S(2)}, u32[]{:S(2)}) collective-permute-start(bf16[512,512]{1,0:T(8,128)(2,1)} %atoms_ref.7), channel_id=1, source_target_pairs={{0,1},{1,0},{2,3},{3,2},{4,5},{5,4},{6,7},{7,6},{8,9},{9,8},{10,11... | collective-permute-start | bytes 1572872 | tf_op jit(solution)/shard_map/ppermute | solution.py:257
  23.3 9.1 %collective-permute-start.2 = (bf16[2,144,512]{2,1,0:T(8,128)(2,1)S(1)}, bf16[2,144,512]{2,1,0:T(8,128)(2,1)S(1)}, u32[]{:S(2)}, u32[]{:S(2)}) collective-permute-start(bf16[2,144,512]{2,1,0:T(8,128)(2,1)S(1)} %pad_maximum_fusion.4), channel_id=1, source_target_pairs={{0,8},{1,9},{2,10},{3,11},{4,12},{5,13},{6,14},{7,15},{8,0},{9,1},... | collective-permute-start | bytes 884744 | tf_op jit(solution)/shard_map/ppermute | solution.py:257
  24.2 12.3 %collective-permute-start.6 = (bf16[16,8,256]{2,1,0:T(8,128)(2,1)S(1)}, bf16[16,8,256]{2,1,0:T(8,128)(2,1)S(1)}, u32[]{:S(2)}, u32[]{:S(2)}) collective-permute-start(bf16[16,8,256]{2,1,0:T(8,128)(2,1)S(1)} %pad_maximum_fusion.8), channel_id=1, source_target_pairs={{0,1},{1,0},{2,3},{3,2},{4,5},{5,4},{6,7},{7,6},{8,9},{9,8},{10,11... | collective-permute-start | bytes 196616 | tf_op jit(solution)/shard_map/ppermute | solution.py:257
  36.6 13.4 %collective-permute-start.8 = (bf16[4,80,512]{2,1,0:T(8,128)(2,1)S(1)}, bf16[4,80,512]{2,1,0:T(8,128)(2,1)S(1)}, u32[]{:S(2)}, u32[]{:S(2)}) collective-permute-start(bf16[4,80,512]{2,1,0:T(8,128)(2,1)S(1)} %slice.92), channel_id=1, source_target_pairs={{0,4},{1,5},{2,6},{3,7},{4,0},{5,1},{6,2},{7,3},{8,12},{9,13},{10,... | collective-permute-start | bytes 983048 | tf_op jit(solution)/shard_map/ppermute | solution.py:257
  38.4 11.5 %collective-permute-start.9 = (bf16[4,64,512]{2,1,0:T(8,128)(2,1)S(1)}, bf16[4,64,512]{2,1,0:T(8,128)(2,1)S(1)}, u32[]{:S(2)}, u32[]{:S(2)}) collective-permute-start(bf16[4,64,512]{2,1,0:T(8,128)(2,1)S(1)} %slice.93), channel_id=1, source_target_pairs={{0,1},{1,0},{2,3},{3,2},{4,5},{5,4},{6,7},{7,6},{8,9},{9,8},{10,11... | collective-permute-start | bytes 786440 | tf_op jit(solution)/shard_map/ppermute | solution.py:257
  40.0 1.0 copy-start
  50.0 14.4 %copy-start.6 = (bf16[8,80,512]{2,1,0:T(8,128)(2,1)}, bf16[8,80,512]{2,1,0:T(8,128)(2,1)S(1)}, u32[]{:S(2)}) copy-start(bf16[8,80,512]{2,1,0:T(8,128)(2,1)S(1)} %pad_maximum_fusion.rest_0_) | copy-start | bytes 1966084
  50.1 15.8 %collective-permute-start.10 = (bf16[8,80,512]{2,1,0:T(8,128)(2,1)S(1)}, bf16[8,80,512]{2,1,0:T(8,128)(2,1)S(1)}, u32[]{:S(2)}, u32[]{:S(2)}) collective-permute-start(bf16[8,80,512]{2,1,0:T(8,128)(2,1)S(1)} %pad_maximum_fusion.rest_0_), channel_id=1, source_target_pairs={{0,1},{1,0},{2,3},{3,2},{4,5},{5,4},{6,7},{7,6},{8,9},{9,8},{10,11... | collective-permute-start | bytes 1966088 | tf_op jit(solution)/shard_map/ppermute | solution.py:257
  50.7 13.7 %collective-permute-start.11 = (bf16[8,64,512]{2,1,0:T(8,128)(2,1)S(1)}, bf16[8,64,512]{2,1,0:T(8,128)(2,1)S(1)}, u32[]{:S(2)}, u32[]{:S(2)}) collective-permute-start(bf16[8,64,512]{2,1,0:T(8,128)(2,1)S(1)} %pad_maximum_fusion.2.rest_4_), channel_id=1, source_target_pairs={{0,4},{1,5},{2,6},{3,7},{4,0},{5,1},{6,2},{7,3},{8,12},{9,13},{10,... | collective-permute-start | bytes 1572872 | tf_op jit(solution)/shard_map/ppermute | solution.py:257
  51.0 24.4 %collective-permute-start.13 = (bf16[8,80,512]{2,1,0:T(8,128)(2,1)S(1)}, bf16[8,80,512]{2,1,0:T(8,128)(2,1)S(1)}, u32[]{:S(2)}, u32[]{:S(2)}) collective-permute-start(bf16[8,80,512]{2,1,0:T(8,128)(2,1)S(1)} %pad_maximum_fusion.rest_0_), channel_id=1, source_target_pairs={{0,2},{1,3},{2,0},{3,1},{4,6},{5,7},{6,4},{7,5},{8,10},{9,11},{10,... | collective-permute-start | bytes 1966088 | tf_op jit(solution)/shard_map/ppermute | solution.py:257
  65.9 9.5 %copy-start.11 = (bf16[8,80,512]{2,1,0:T(8,128)(2,1)}, bf16[8,80,512]{2,1,0:T(8,128)(2,1)S(1)}, u32[]{:S(2)}) copy-start(bf16[8,80,512]{2,1,0:T(8,128)(2,1)S(1)} %collective-permute-done.10.rest_1_) | copy-start | bytes 1966084
  65.9 9.5 %collective-permute-start.14 = (bf16[8,80,512]{2,1,0:T(8,128)(2,1)S(1)}, bf16[8,80,512]{2,1,0:T(8,128)(2,1)S(1)}, u32[]{:S(2)}, u32[]{:S(2)}) collective-permute-start(bf16[8,80,512]{2,1,0:T(8,128)(2,1)S(1)} %collective-permute-done.10.rest_1_), channel_id=1, source_target_pairs={{0,2},{1,3},{2,0},{3,1},{4,6},{5,7},{6,4},{7,5},{8,10},{9,11},{10,... | collective-permute-start | bytes 1966088 | tf_op jit(solution)/shard_map/ppermute | solution.py:257
  65.9 9.5 %collective-permute-start.15 = (bf16[8,64,512]{2,1,0:T(8,128)(2,1)S(1)}, bf16[8,64,512]{2,1,0:T(8,128)(2,1)S(1)}, u32[]{:S(2)}, u32[]{:S(2)}) collective-permute-start(bf16[8,64,512]{2,1,0:T(8,128)(2,1)S(1)} %pad_maximum_fusion.2.rest_4_), channel_id=1, source_target_pairs={{0,2},{1,3},{2,0},{3,1},{4,6},{5,7},{6,4},{7,5},{8,10},{9,11},{10,... | collective-permute-start | bytes 1572872 | tf_op jit(solution)/shard_map/ppermute | solution.py:257
  66.4 9.0 %collective-permute-start.16 = (bf16[8,64,512]{2,1,0:T(8,128)(2,1)S(1)}, bf16[8,64,512]{2,1,0:T(8,128)(2,1)S(1)}, u32[]{:S(2)}, u32[]{:S(2)}) collective-permute-start(bf16[8,64,512]{2,1,0:T(8,128)(2,1)S(1)} %collective-permute-done.11.rest_5_), channel_id=1, source_target_pairs={{0,2},{1,3},{2,0},{3,1},{4,6},{5,7},{6,4},{7,5},{8,10},{9,11},{10,... | collective-permute-start | bytes 1572872 | tf_op jit(solution)/shard_map/ppermute | solution.py:257
  66.4 8.9 %collective-permute-start.12 = (bf16[512,256]{1,0:T(8,128)(2,1)S(1)}, bf16[512,256]{1,0:T(8,128)(2,1)S(1)}, u32[]{:S(2)}, u32[]{:S(2)}) collective-permute-start(bf16[512,256]{1,0:T(8,128)(2,1)S(1)} %get-tuple-element.138.mixed_ref), channel_id=1, source_target_pairs={{0,1},{1,0},{2,3},{3,2},{4,5},{5,4},{6,7},{7,6},{8,9},{9,8},{10,11... | collective-permute-start | bytes 786440 | tf_op jit(solution)/shard_map/ppermute | solution.py:257
  67.3 9.3 %copy-start.1 = (bf16[512,512]{1,0:T(8,128)(2,1)S(1)}, bf16[512,512]{1,0:T(8,128)(2,1)}, u32[]{:S(2)}) copy-start(bf16[512,512]{1,0:T(8,128)(2,1)} %atoms_ref.7) | copy-start | bytes 1572868
  67.3 9.3 %copy-start.5 = (bf16[512,512]{1,0:T(8,128)(2,1)S(1)}, bf16[512,512]{1,0:T(8,128)(2,1)}, u32[]{:S(2)}) copy-start(bf16[512,512]{1,0:T(8,128)(2,1)} %cot_ref.4) | copy-start | bytes 1572868
  75.3 19.5 %copy-start.3 = (bf16[16,256]{1,0:T(8,128)(2,1)S(1)}, bf16[16,256]{1,0:T(8,128)(2,1)}, u32[]{:S(2)}) copy-start(bf16[16,256]{1,0:T(8,128)(2,1)} %constant.27.clone.mask_ref) | copy-start | bytes 24580
  75.4 0.9 copy-start.12
  75.4 1.0 copy-start.14
  75.4 1.2 copy-start.13
  92.7 10.7 %collective-permute-start.17 = (bf16[8,80,512]{2,1,0:T(8,128)(2,1)}, bf16[8,80,512]{2,1,0:T(8,128)(2,1)S(1)}, u32[]{:S(2)}, u32[]{:S(2)}) collective-permute-start(bf16[8,80,512]{2,1,0:T(8,128)(2,1)} %get-tuple-element.150), channel_id=1, source_target_pairs={{0,2},{1,3},{2,0},{3,1},{4,6},{5,7},{6,4},{7,5},{8,10},{9,11},{10,... | collective-permute-start | bytes 1966088 | tf_op jit(solution)/shard_map/ppermute | solution.py:257
  92.7 10.7 %collective-permute-start.18 = (bf16[8,80,512]{2,1,0:T(8,128)(2,1)}, bf16[8,80,512]{2,1,0:T(8,128)(2,1)S(1)}, u32[]{:S(2)}, u32[]{:S(2)}) collective-permute-start(bf16[8,80,512]{2,1,0:T(8,128)(2,1)} %get-tuple-element.151), channel_id=1, source_target_pairs={{0,2},{1,3},{2,0},{3,1},{4,6},{5,7},{6,4},{7,5},{8,10},{9,11},{10,... | collective-permute-start | bytes 1966088 | tf_op jit(solution)/shard_map/ppermute | solution.py:257
  93.2 10.1 %collective-permute-start.19 = (bf16[8,64,512]{2,1,0:T(8,128)(2,1)S(1)}, bf16[8,64,512]{2,1,0:T(8,128)(2,1)S(1)}, u32[]{:S(2)}, u32[]{:S(2)}) collective-permute-start(bf16[8,64,512]{2,1,0:T(8,128)(2,1)S(1)} %get-tuple-element.152), channel_id=1, source_target_pairs={{0,2},{1,3},{2,0},{3,1},{4,6},{5,7},{6,4},{7,5},{8,10},{9,11},{10,... | collective-permute-start | bytes 1572872 | tf_op jit(solution)/shard_map/ppermute | solution.py:257
  93.2 10.1 %collective-permute-start.20 = (bf16[8,64,512]{2,1,0:T(8,128)(2,1)S(1)}, bf16[8,64,512]{2,1,0:T(8,128)(2,1)S(1)}, u32[]{:S(2)}, u32[]{:S(2)}) collective-permute-start(bf16[8,64,512]{2,1,0:T(8,128)(2,1)S(1)} %get-tuple-element.153), channel_id=1, source_target_pairs={{0,2},{1,3},{2,0},{3,1},{4,6},{5,7},{6,4},{7,5},{8,10},{9,11},{10,... | collective-permute-start | bytes 1572872 | tf_op jit(solution)/shard_map/ppermute | solution.py:257
  93.7 12.9 %collective-permute-start.23 = (bf16[512,256]{1,0:T(8,128)(2,1)S(1)}, bf16[512,256]{1,0:T(8,128)(2,1)S(1)}, u32[]{:S(2)}, u32[]{:S(2)}) collective-permute-start(bf16[512,256]{1,0:T(8,128)(2,1)S(1)} %get-tuple-element.166), channel_id=1, source_target_pairs={{0,1},{1,0},{2,3},{3,2},{4,5},{5,4},{6,7},{7,6},{8,9},{9,8},{10,11... | collective-permute-start | bytes 786440 | tf_op jit(solution)/shard_map/ppermute | solution.py:257
  94.8 8.6 %copy-start.8 = (bf16[8,80,512]{2,1,0:T(8,128)(2,1)S(1)}, bf16[8,80,512]{2,1,0:T(8,128)(2,1)}, u32[]{:S(2)}) copy-start(bf16[8,80,512]{2,1,0:T(8,128)(2,1)} %get-tuple-element.149) | copy-start | bytes 1966084
  94.8 8.8 %copy-start.7 = (bf16[8,80,512]{2,1,0:T(8,128)(2,1)S(1)}, bf16[8,80,512]{2,1,0:T(8,128)(2,1)}, u32[]{:S(2)}) copy-start(bf16[8,80,512]{2,1,0:T(8,128)(2,1)} %get-tuple-element.156) | copy-start | bytes 1966084
  104.1 16.7 %collective-permute-start.21 = (bf16[8,80,512]{2,1,0:T(8,128)(2,1)S(1)}, bf16[8,80,512]{2,1,0:T(8,128)(2,1)S(1)}, u32[]{:S(2)}, u32[]{:S(2)}) collective-permute-start(bf16[8,80,512]{2,1,0:T(8,128)(2,1)S(1)} %add_convert_fusion.1), channel_id=1, source_target_pairs={{0,1},{1,0},{2,3},{3,2},{4,5},{5,4},{6,7},{7,6},{8,9},{9,8},{10,11... | collective-permute-start | bytes 1966088 | tf_op jit(solution)/shard_map/ppermute | solution.py:257
  105.2 15.6 %collective-permute-start.22 = (bf16[8,64,512]{2,1,0:T(8,128)(2,1)S(1)}, bf16[8,64,512]{2,1,0:T(8,128)(2,1)S(1)}, u32[]{:S(2)}, u32[]{:S(2)}) collective-permute-start(bf16[8,64,512]{2,1,0:T(8,128)(2,1)S(1)} %add_convert_fusion.4), channel_id=1, source_target_pairs={{0,4},{1,5},{2,6},{3,7},{4,0},{5,1},{6,2},{7,3},{8,12},{9,13},{10,... | collective-permute-start | bytes 1572872 | tf_op jit(solution)/shard_map/ppermute | solution.py:257
  121.2 10.9 %collective-permute-start.24 = (bf16[4,80,512]{2,1,0:T(8,128)(2,1)S(1)}, bf16[4,80,512]{2,1,0:T(8,128)(2,1)S(1)}, u32[]{:S(2)}, u32[]{:S(2)}) collective-permute-start(bf16[4,80,512]{2,1,0:T(8,128)(2,1)S(1)} %get-tuple-element.184), channel_id=1, source_target_pairs={{0,4},{1,5},{2,6},{3,7},{4,0},{5,1},{6,2},{7,3},{8,12},{9,13},{10,... | collective-permute-start | bytes 983048 | tf_op jit(solution)/shard_map/ppermute | solution.py:257
  122.0 10.2 %collective-permute-start.25 = (bf16[4,64,512]{2,1,0:T(8,128)(2,1)S(1)}, bf16[4,64,512]{2,1,0:T(8,128)(2,1)S(1)}, u32[]{:S(2)}, u32[]{:S(2)}) collective-permute-start(bf16[4,64,512]{2,1,0:T(8,128)(2,1)S(1)} %get-tuple-element.185), channel_id=1, source_target_pairs={{0,1},{1,0},{2,3},{3,2},{4,5},{5,4},{6,7},{7,6},{8,9},{9,8},{10,11... | collective-permute-start | bytes 786440 | tf_op jit(solution)/shard_map/ppermute | solution.py:257
  123.6 31.7 %copy-start.2 = (f32[512,512]{1,0:T(8,128)S(1)}, f32[512,512]{1,0:T(8,128)}, u32[]{:S(2)}) copy-start(f32[512,512]{1,0:T(8,128)} %get-tuple-element.143.first_ref) | copy-start | bytes 3145732
  123.6 41.0 %copy-start.10 = (f32[16]{0:T(128)S(1)}, f32[16]{0:T(128)}, u32[]{:S(2)}) copy-start(f32[16]{0:T(128)} %param.20) | copy-start | bytes 196
  123.6 41.5 %copy-start.9 = (f32[16]{0:T(128)S(1)}, f32[16]{0:T(128)}, u32[]{:S(2)}) copy-start(f32[16]{0:T(128)} %param.19) | copy-start | bytes 196
  134.8 1.8 %collective-permute-start.26 = (bf16[8,96,256]{2,1,0:T(8,128)(2,1)S(1)}, bf16[8,96,256]{2,1,0:T(8,128)(2,1)S(1)}, u32[]{:S(2)}, u32[]{:S(2)}) collective-permute-start(bf16[8,96,256]{2,1,0:T(8,128)(2,1)S(1)} %get-tuple-element.197), channel_id=1, source_target_pairs={{0,2},{2,0},{4,6},{6,4},{8,10},{10,8},{12,14},{14,12},{16,18},{18,... | collective-permute-start | bytes 1179656 | tf_op jit(solution)/shard_map/ppermute | solution.py:257
  137.4 7.3 %collective-permute-start.27 = (bf16[4,96,256]{2,1,0:T(8,128)(2,1)}, bf16[4,96,256]{2,1,0:T(8,128)(2,1)}, u32[]{:S(2)}, u32[]{:S(2)}) collective-permute-start(bf16[4,96,256]{2,1,0:T(8,128)(2,1)} %slice.129), channel_id=1, source_target_pairs={{0,4},{2,6},{4,0},{6,2},{8,12},{10,14},{12,8},{14,10},{16,20},{18,... | collective-permute-start | bytes 589832 | tf_op jit(solution)/shard_map/ppermute | solution.py:257
  137.9 9.1 %collective-permute-start.31 = (bf16[2,144,512]{2,1,0:T(8,128)(2,1)}, bf16[2,144,512]{2,1,0:T(8,128)(2,1)}, u32[]{:S(2)}, u32[]{:S(2)}) collective-permute-start(bf16[2,144,512]{2,1,0:T(8,128)(2,1)} %get-tuple-element.202), channel_id=1, source_target_pairs={{0,8},{1,9},{2,10},{3,11},{4,12},{5,13},{6,14},{7,15},{8,0},{9,1},... | collective-permute-start | bytes 884744 | tf_op jit(solution)/shard_map/ppermute | solution.py:257
  138.7 13.4 %collective-permute-start.29 = (bf16[512,512]{1,0:T(8,128)(2,1)S(1)}, bf16[512,512]{1,0:T(8,128)(2,1)S(1)}, u32[]{:S(2)}, u32[]{:S(2)}) collective-permute-start(bf16[512,512]{1,0:T(8,128)(2,1)S(1)} %get-tuple-element.198), channel_id=1, source_target_pairs={{0,1},{1,0},{2,3},{3,2},{4,5},{5,4},{6,7},{7,6},{8,9},{9,8},{10,11... | collective-permute-start | bytes 1572872 | tf_op jit(solution)/shard_map/ppermute | solution.py:257
  145.6 6.5 %collective-permute-start.28 = (bf16[2,96,256]{2,1,0:T(8,128)(2,1)S(1)}, bf16[2,96,256]{2,1,0:T(8,128)(2,1)S(1)}, u32[]{:S(2)}, u32[]{:S(2)}) collective-permute-start(bf16[2,96,256]{2,1,0:T(8,128)(2,1)S(1)} %slice.130), channel_id=1, source_target_pairs={{0,8},{2,10},{4,12},{6,14},{8,0},{10,2},{12,4},{14,6},{16,24},{18,... | collective-permute-start | bytes 294920 | tf_op jit(solution)/shard_map/ppermute | solution.py:257
  148.1 10.4 %collective-permute-start.32 = (bf16[1,144,512]{2,1,0:T(8,128)(2,1)S(1)}, bf16[1,144,512]{2,1,0:T(8,128)(2,1)S(1)}, u32[]{:S(2)}, u32[]{:S(2)}) collective-permute-start(bf16[1,144,512]{2,1,0:T(8,128)(2,1)S(1)} %slice.135), channel_id=1, source_target_pairs={{0,16},{1,17},{2,18},{3,19},{4,20},{5,21},{6,22},{7,23},{8,24},{9,... | collective-permute-start | bytes 442376 | tf_op jit(solution)/shard_map/ppermute | solution.py:257
  152.1 7.2 %collective-permute-start.30 = (bf16[1,96,256]{2,1,0:T(8,128)(2,1)S(1)}, bf16[1,96,256]{2,1,0:T(8,128)(2,1)S(1)}, u32[]{:S(2)}, u32[]{:S(2)}) collective-permute-start(bf16[1,96,256]{2,1,0:T(8,128)(2,1)S(1)} %slice.133), channel_id=1, source_target_pairs={{0,16},{2,18},{4,20},{6,22},{8,24},{10,26},{12,28},{14,30},{16,0},... | collective-permute-start | bytes 147464 | tf_op jit(solution)/shard_map/ppermute | solution.py:257
  161.0 4.1 %collective-permute-start.33 = (f32[16]{0:T(128)S(1)}, f32[16]{0:T(128)S(1)}, u32[]{:S(2)}, u32[]{:S(2)}) collective-permute-start(f32[16]{0:T(128)S(1)} %dynamic-slice_bitcast_fusion), channel_id=1, source_target_pairs={{0,1},{1,0},{2,3},{3,2},{4,5},{5,4},{6,7},{7,6},{8,9},{9,8},{10,11... | collective-permute-start | bytes 200 | tf_op jit(solution)/shard_map/ppermute | solution.py:257
  (1 other events, 0.7 us)
